TPU v7x, 512 devices: a whole 4x8x8 slice. The times are simulated.
512 devices in a mesh: section: 8 (over y_lo, core), dp: 64 (over z, x, y_hi).
Axes of the slice: x: 4, y: 8 (y_hi: 2, y_lo: 4; y = y_hi * 4 + y_lo), z: 8, core: 2. Of those that a mesh axis runs over, the one named last changes fastest.
Arguments:
- acts: float32 [8, 8192, 1024], P('section', 'dp'), may hold values from -6 to 6
- grads: float32 [8, 8192, 1024], P('section', 'dp'), may hold values from -0.6 to 0.6
- in_proj: bfloat16 [8, 2048, 512], P('section', 'dp'), may hold values from -0.25 to 0.25
- out_proj: bfloat16 [8, 2048, 512], P('section', 'dp'), may hold values from -0.125 to 0.125
- gain: float32 [8, 512], P('section'), may hold values from 0.1 to 1.9
Outputs:
- acts_out: float32 [8, 8192, 1024], P('section', 'dp')
- grads_out: float32 [8, 8192, 1024], P('section', 'dp')
- out_proj_grad: float32 [8, 2048, 512], P('section', 'dp')
All inputs are finite; a program needn't handle non-finite values.
Results may differ from a plain program's by a relative error of at most 0.012.
Values may be sent and summed in bfloat16 or wider, within the bound.
No kernel may reach another device: no remote copies, remote signals or barrier semaphores. Data moves between devices by JAX's collectives and lax.ppermute only.
A program may use at most 64 MiB of HBM per device.

v0:
```python
import functools

import jax
import jax.numpy as jnp
from jax import lax
from jax.experimental import pallas as pl
from jax.experimental.pallas import tpu as pltpu
from jax.sharding import PartitionSpec as P


coupling_scale = 32.0**0.25
rms_epsilon = 1e-06
root_half = 0.7071067811865476
inv_root_two_pi = 0.3989422804014327

x_size = 4
pair_size = 2


def dp_index(z, x, y):
    return (z * x_size + x) * pair_size + y


def z_size():
    return lax.axis_size("dp") // (x_size * pair_size)


def alike_groups():
    return [
        [
            dp_index(z, x, y)
            for z in range(parity, z_size(), 2)
            for y in range(pair_size)
        ]
        for parity in range(2)
        for x in range(x_size)
    ]


def swapped_along_x(block, peer):
    route = [
        (dp_index(z, peer(x), y), dp_index(z, x, y))
        for z in range(z_size())
        for x in range(x_size)
        for y in range(pair_size)
    ]
    return lax.ppermute(block, "dp", route)


def partner(index):
    return index ^ (x_size * pair_size)


def swapped_with_partner(block):
    return lax.ppermute(block, "dp", [(partner(i), i) for i in range(lax.axis_size("dp"))])


def near_x(x):
    return x ^ 1


def next_x(x):
    return (x + 1 if x % 2 else x - 1) % x_size


def far_x(x):
    return (x + 2) % x_size


def exchanged(blocks):
    return lax.all_to_all(
        blocks, "dp", 0, 0, axis_index_groups=alike_groups(), tiled=True
    )


def passed_back(block):
    devices = range(lax.axis_size("section"))
    return lax.ppermute(block, "section", [(i, i - 1) for i in devices if i])


def passed_back_to_partner(block):
    size = lax.axis_size("dp")
    route = [
        (section * size + i, (section - 1) * size + partner(i))
        for section in range(1, lax.axis_size("section"))
        for i in range(size)
    ]
    return lax.ppermute(block, ("section", "dp"), route)


def gathered_along_x(block):
    rows = block.shape[0] // 2
    near, following = swapped_along_x(block, near_x), swapped_along_x(block, next_x)
    far_head = swapped_along_x(following[:rows], near_x)
    far_tail = swapped_along_x(near[rows:], next_x)
    return block, near, following, far_head, far_tail


def inverse_rms(first):
    return lax.rsqrt(jnp.mean(first * first, axis=-1, keepdims=True) + rms_epsilon)


def pair_sums(straight, crossed):
    tokens = crossed.shape[0] // 2
    straight, crossed = straight.astype(jnp.float32), crossed.astype(jnp.float32)
    return jnp.concatenate(
        [straight[:tokens] + crossed[tokens:], straight[tokens:] + crossed[:tokens]], axis=0
    )


def pair_state(fresh, own_ref, other_ref, current):
    if fresh:
        half = other_ref.shape[1]
        waiting = half - current
        both = jnp.concatenate(
            [
                own_ref[:, current : current + half].astype(jnp.float32),
                other_ref[...].astype(jnp.float32),
            ],
            axis=0,
        )
        return both, own_ref[:, waiting : waiting + half]
    rows = other_ref.shape[0]
    return pair_sums(own_ref[:rows], other_ref[...]), own_ref[rows:].astype(jnp.float32)


def put_addends(last, straight_ref, crossed_ref, own, other, kept):
    tokens = own.shape[0]
    dtype = straight_ref.dtype
    straight_ref[:tokens] = own.astype(dtype)
    if last:
        crossed_ref[...] = other.astype(dtype)
        straight_ref[tokens:] = kept.astype(dtype)
    else:
        straight_ref[tokens : 2 * tokens] = other.astype(dtype)
        straight_ref[2 * tokens :] = kept.astype(dtype)
        crossed_ref[:tokens] = own.astype(dtype)
        crossed_ref[tokens:] = other.astype(dtype)


def forward_kernel(fresh, last, own_ref, other_ref, gain_ref, *refs):
    weight_refs, (hidden_ref, slopes_ref, straight_ref, crossed_ref) = refs[:-4], refs[-4:]
    first, second = pair_state(fresh, own_ref, other_ref, 0)
    tokens, half = second.shape
    normed = (first * inverse_rms(first) * gain_ref[...]).astype(jnp.bfloat16)
    for span, weight_ref in spans(weight_refs):
        preact = lax.dot_general(
            normed,
            weight_ref[:, :half],
            (((1,), (1,)), ((), ())),
            preferred_element_type=jnp.float32,
        )
        normal_cdf = 0.5 * (1.0 + lax.erf(preact * root_half))
        density = jnp.exp(-0.5 * preact * preact) * inv_root_two_pi
        hidden_ref[:, span] = (preact * normal_cdf).astype(jnp.bfloat16)
        slopes_ref[:, span] = (normal_cdf + preact * density).astype(slopes_ref.dtype)
    branch = sum(
        jnp.dot(hidden_ref[:, span], weight_ref[:, half:], preferred_element_type=jnp.float32)
        for span, weight_ref in spans(weight_refs)
    )
    own = (second - branch[:tokens]) / coupling_scale
    other = (0.0 - branch[tokens:]) / coupling_scale
    put_addends(last, straight_ref, crossed_ref, own, other, first[:tokens])


def backward_kernel(
    fresh, last, acts_ref, acts_other_ref, own_ref, other_ref, gain_ref, slopes_ref, *refs
):
    weight_refs, (cotangent_ref, straight_ref, crossed_ref, pre_grad) = refs[:-4], refs[-4:]
    half = gain_ref.shape[1]
    second_grad, first_grad = pair_state(fresh, own_ref, other_ref, half)
    tokens = first_grad.shape[0]
    if not fresh:
        first_grad = coupling_scale * first_grad
    cotangent = second_grad.astype(jnp.bfloat16)
    cotangent_ref[...] = cotangent
    for span, weight_ref in spans(weight_refs):
        hidden_grad = lax.dot_general(
            cotangent,
            weight_ref[:, half:],
            (((1,), (1,)), ((), ())),
            preferred_element_type=jnp.float32,
        )
        slopes = slopes_ref[:, span].astype(jnp.float32)
        pre_grad[:, span] = (hidden_grad * slopes).astype(jnp.bfloat16)
    norm_grad = sum(
        jnp.dot(pre_grad[:, span], weight_ref[:, :half], preferred_element_type=jnp.float32)
        for span, weight_ref in spans(weight_refs)
    )
    first, _ = pair_state(fresh, acts_ref, acts_other_ref, 0)
    inv_rms = inverse_rms(first)
    scaled = norm_grad * gain_ref[...]
    inner = jnp.mean(first * scaled, axis=-1, keepdims=True)
    input_grad = inv_rms * scaled - first * (inv_rms * inv_rms * inv_rms) * inner
    own = first_grad + input_grad[:tokens]
    put_addends(last, straight_ref, crossed_ref, own, input_grad[tokens:], cotangent[:tokens])


def cotangent_kernel(own_ref, other_ref, out_ref):
    rows = other_ref.shape[0]
    out_ref[...] = pair_sums(own_ref[:rows], other_ref[...]).astype(out_ref.dtype)


def output_kernel(kept_scale, kept_first, straight_ref, crossed_ref, out_ref):
    tokens, half = crossed_ref.shape
    fresh = straight_ref[:tokens].astype(jnp.float32) + crossed_ref[...].astype(jnp.float32)
    kept = straight_ref[tokens:].astype(jnp.float32)
    if kept_scale != 1.0:
        kept = kept * kept_scale
    first, second = (kept, fresh) if kept_first else (fresh, kept)
    out_ref[:, :half] = first
    out_ref[:, half:] = second


def outer_kernel(start, *refs):
    ticks = len(refs) // 2
    hidden_refs, cotangent_refs, out_ref = refs[:ticks], refs[ticks:-1], refs[-1]
    count = out_ref.shape[0]
    rows = jnp.concatenate([ref[:, start : start + count] for ref in hidden_refs], axis=0)
    cotangents = jnp.concatenate([ref[...] for ref in cotangent_refs], axis=0)
    total = lax.dot_general(
        rows, cotangents, (((0,), (0,)), ((), ())), preferred_element_type=jnp.float32
    )
    out_ref[...] = total.astype(out_ref.dtype)


def spans(weight_refs):
    offset = 0
    for ref in weight_refs:
        yield pl.ds(offset, ref.shape[0]), ref
        offset += ref.shape[0]


def in_vmem(count):
    return [pl.BlockSpec(memory_space=pltpu.VMEM)] * count


def cost(tokens, units, half):
    return pl.CostEstimate(
        flops=4 * tokens * units * half,
        bytes_accessed=4 * units * half + 4 * tokens * units,
        transcendentals=2 * tokens * units,
    )


def kernel_params():
    return pltpu.CompilerParams(vmem_limit_bytes=16 * 2**20)


def call(kernel, cost_estimate, outs, operands, scratch=()):
    return pl.pallas_call(
        kernel,
        out_shape=tuple(jax.ShapeDtypeStruct(shape, dtype) for shape, dtype in outs),
        in_specs=in_vmem(len(operands)),
        out_specs=tuple(in_vmem(len(outs))),
        scratch_shapes=list(scratch),
        cost_estimate=cost_estimate,
        compiler_params=kernel_params(),
    )(*operands)


def addend_shapes(last, tokens, half):
    straight, crossed = (2, 1) if last else (3, 2)
    return (
        ((straight * tokens, half), jnp.bfloat16),
        ((crossed * tokens, half), jnp.bfloat16),
    )


def forward(fresh, last, tokens, acts, gain, weights):
    half = gain.shape[1]
    units = sum(w.shape[0] for w in weights)
    return call(
        functools.partial(forward_kernel, fresh, last),
        cost(2 * tokens, units, half),
        (
            ((2 * tokens, units), jnp.bfloat16),
            ((2 * tokens, units), jnp.bfloat16),
            *addend_shapes(last, tokens, half),
        ),
        (*acts, gain, *weights),
    )


def backward(fresh, last, tokens, acts, grads, gain, slopes, weights):
    half = gain.shape[1]
    units = slopes.shape[1]
    return call(
        functools.partial(backward_kernel, fresh, last),
        cost(2 * tokens, units, half),
        (((2 * tokens, half), jnp.bfloat16), *addend_shapes(last, tokens, half)),
        (*acts, *grads, gain, slopes, *weights),
        (pltpu.VMEM((2 * tokens, units), jnp.bfloat16),),
    )


def small_cost(tokens, half):
    return pl.CostEstimate(
        flops=16 * tokens * half, bytes_accessed=16 * tokens * half, transcendentals=0
    )


def cotangent_of(grads):
    _, crossed = grads
    return call(
        cotangent_kernel, small_cost(*crossed.shape), ((crossed.shape, jnp.bfloat16),), grads
    )[0]


def output_of(kept_scale, kept_first, straight, crossed):
    tokens, half = crossed.shape
    return call(
        functools.partial(output_kernel, kept_scale, kept_first),
        small_cost(tokens, half),
        (((tokens, 2 * half), jnp.float32),),
        (straight, crossed),
    )[0]


def outer_rows(hiddens, cotangents, start, count):
    half = cotangents[0].shape[1]
    tokens = hiddens[0].shape[0] * len(hiddens)
    return call(
        functools.partial(outer_kernel, start),
        pl.CostEstimate(
            flops=2 * tokens * count * half,
            bytes_accessed=2 * (tokens * count + tokens * half + count * half),
            transcendentals=0,
        ),
        (((count, half), jnp.bfloat16),),
        (*hiddens, *cotangents),
    )[0]


def sent_back(straight, crossed):
    crossed = passed_back_to_partner(crossed)
    straight = passed_back(straight)
    return straight, crossed


def local(acts, grads, in_proj, out_proj, gain):
    tokens, half = acts.shape[1], acts.shape[2] // 2
    units = in_proj.shape[1]
    tick_count = min(4, lax.axis_size("section") // 2)
    shard = jnp.concatenate([in_proj[0], out_proj[0]], axis=1)
    group_size = len(alike_groups()[0])
    weights = gathered_along_x(exchanged(jnp.tile(shard, (group_size, 1))))
    quarter = group_size * units

    acts_pair = (acts[0], swapped_with_partner(acts[0, :, :half]))
    grads_pair = (grads[0], swapped_with_partner(grads[0, :, half:].astype(jnp.bfloat16)))
    hiddens, cotangents = [], []
    for tick_index in range(tick_count):
        fresh, last = tick_index == 0, tick_index == tick_count - 1
        hidden, slopes, *addends = forward(fresh, last, tokens, acts_pair, gain, weights)
        hiddens.append(hidden)
        next_acts = sent_back(*addends)
        if last:
            grads_pair, hidden, addends = lax.optimization_barrier((grads_pair, hidden, addends))
            cotangents.append(cotangent_of(grads_pair))
            outer = functools.partial(outer_rows, hiddens, cotangents, count=quarter)
            parts = [outer(i * quarter) for i in (3, 1, 2)]
            from_far = swapped_along_x(parts[0], far_x)
            from_near = swapped_along_x(parts[1], near_x)
            from_next = swapped_along_x(parts[2], next_x)
            slopes, _ = lax.optimization_barrier((slopes, parts))
        cotangent, *addends = backward(
            fresh, last, tokens, acts_pair, grads_pair, gain, slopes, weights
        )
        if last:
            own = outer(0)
            blocks = sum(
                x.astype(jnp.float32) for x in (own, from_near, from_next, from_far)
            ).astype(jnp.bfloat16)
            parts = exchanged(blocks).reshape(-1, units, half)
        else:
            cotangents.append(cotangent)
        next_grads = sent_back(*addends)
        acts_pair, grads_pair = next_acts, next_grads

    share = jnp.sum(parts.astype(jnp.float32), axis=0)
    acts_out = output_of(1.0, False, *acts_pair)
    grads_out = output_of(coupling_scale, True, *grads_pair)
    return (acts_out[None], grads_out[None], share[None])


def solution(mesh):
    pair = P("section", "dp", None)
    return jax.shard_map(
        local,
        mesh=mesh,
        in_specs=(pair, pair, pair, pair, P("section", None)),
        out_specs=(pair, pair, pair),
        check_vma=False,
    )
```

profile of v0, /device:TPU:48, one launch (start us, length us, event | category | flops | bytes accessed | tf_op | source)
XLA Modules:
  0.0 176.0 jit_solution(15941661744872028258)
XLA Ops:
  1.5 32.8 %all_to_all.17 = bf16[8,32,1024]{2,1,0:T(8,128)(2,1)S(1)} all-to-all(bf16[8,32,1024]{2,1,0:T(8,128)(2,1)S(1)} %tile.2), channel_id=1, replica_groups={{0,1,16,17,32,33,48,49},{2,3,18,19,34,35,50,51},{4,5,20,21,36,37,52,53}..., dimensions={0} | all-to-all | bytes 1048576 | tf_op jit(solution)/shard_map/all_to_all | solution.py:71
  34.3 4.7 %collective-permute-start.2 = (bf16[256,1024]{1,0:T(8,128)(2,1)S(1)}, bf16[256,1024]{1,0:T(8,128)(2,1)S(1)}, u32[]{:S(2)}, u32[]{:S(2)}) collective-permute-start(bf16[256,1024]{1,0:T(8,128)(2,1)S(1)} %bitcast.13), channel_id=1, source_target_pairs={{6,0},{7,1},{4,2},{5,3},{2,4},{3,5},{0,6},{1,7},{14,8},{15,9},{12,... | collective-permute-start | bytes 1572872 | tf_op jit(solution)/shard_map/ppermute | solution.py:47
  41.1 3.2 %collective-permute-start = (f32[128,512]{1,0:T(8,128)S(1)}, f32[128,512]{1,0:T(8,128)S(1)}, u32[]{:S(2)}, u32[]{:S(2)}) collective-permute-start(f32[128,512]{1,0:T(8,128)S(1)} %slice_bitcast_fusion), channel_id=1, source_target_pairs={{8,0},{9,1},{10,2},{11,3},{12,4},{13,5},{14,6},{15,7},{0,8},{1,9},... | collective-permute-start | bytes 786440 | tf_op jit(solution)/shard_map/ppermute | solution.py:55
  44.3 5.1 %collective-permute-done.2.refs_2_ = bf16[256,1024]{1,0:T(8,128)(2,1)S(1)} collective-permute-done((bf16[256,1024]{1,0:T(8,128)(2,1)S(1)}, bf16[256,1024]{1,0:T(8,128)(2,1)S(1)}, u32[]{:S(2)}, u32[]{:S(2)}) %collective-permute-start.2) | collective-permute-done | bytes 524320 | tf_op jit(solution)/shard_map/ppermute | solution.py:47
  51.6 2.3 %collective-permute-done.1.refs_1_ = bf16[256,1024]{1,0:T(8,128)(2,1)S(1)} collective-permute-done((bf16[256,1024]{1,0:T(8,128)(2,1)S(1)}, bf16[256,1024]{1,0:T(8,128)(2,1)S(1)}, u32[]{:S(2)}, u32[]{:S(2)}) %collective-permute-start.1) | collective-permute-done | bytes 524320 | tf_op jit(solution)/shard_map/ppermute | solution.py:47
  56.1 3.0 %collective-permute-start.13 = (bf16[128,512]{1,0:T(8,128)(2,1)S(1)}, bf16[128,512]{1,0:T(8,128)(2,1)S(1)}, u32[]{:S(2)}, u32[]{:S(2)}) collective-permute-start(bf16[128,512]{1,0:T(8,128)(2,1)S(1)} %fusion), channel_id=1, source_target_pairs={{8,0},{9,1},{10,2},{11,3},{12,4},{13,5},{14,6},{15,7},{0,8},{1,9},... | collective-permute-start | bytes 393224 | tf_op jit(solution)/shard_map/ppermute | solution.py:55
  59.1 4.3 %collective-permute-done.4.refs_4_ = bf16[128,1024]{1,0:T(8,128)(2,1)S(1)} collective-permute-done((bf16[128,1024]{1,0:T(8,128)(2,1)S(1)}, bf16[128,1024]{1,0:T(8,128)(2,1)S(1)}, u32[]{:S(2)}, u32[]{:S(2)}) %collective-permute-start.4) | collective-permute-done | bytes 262176 | tf_op jit(solution)/shard_map/ppermute | solution.py:47
  68.0 3.3 %collective-permute-start.14 = (bf16[384,512]{1,0:T(8,128)(2,1)S(1)}, bf16[384,512]{1,0:T(8,128)(2,1)S(1)}, u32[]{:S(2)}, u32[]{:S(2)}) collective-permute-start(bf16[384,512]{1,0:T(8,128)(2,1)S(1)} %get-tuple-element.42), channel_id=1, source_target_pairs={{64,0},{128,64},{192,128},{256,192},{320,256},{384,320},{448,384},... | collective-permute-start | bytes 1179656 | tf_op jit(solution)/shard_map/ppermute | solution.py:78
  73.6 3.8 %collective-permute-start.15 = (bf16[256,512]{1,0:T(8,128)(2,1)S(1)}, bf16[256,512]{1,0:T(8,128)(2,1)S(1)}, u32[]{:S(2)}, u32[]{:S(2)}) collective-permute-start(bf16[256,512]{1,0:T(8,128)(2,1)S(1)} %get-tuple-element.43), channel_id=1, source_target_pairs={{64,8},{65,9},{66,10},{67,11},{68,12},{69,13},{70,14},{71,15},{72,... | collective-permute-start | bytes 786440 | tf_op jit(solution)/shard_map/ppermute | solution.py:88
  77.4 7.2 %collective-permute-done.6.other_ref.acts_other_ref = bf16[256,512]{1,0:T(8,128)(2,1)S(1)} collective-permute-done((bf16[256,512]{1,0:T(8,128)(2,1)S(1)}, bf16[256,512]{1,0:T(8,128)(2,1)S(1)}, u32[]{:S(2)}, u32[]{:S(2)}) %collective-permute-start.6) | collective-permute-done | bytes 262176 | tf_op jit(solution)/shard_map/ppermute | solution.py:88
  89.2 3.1 %collective-permute-start.16 = (bf16[384,512]{1,0:T(8,128)(2,1)S(1)}, bf16[384,512]{1,0:T(8,128)(2,1)S(1)}, u32[]{:S(2)}, u32[]{:S(2)}) collective-permute-start(bf16[384,512]{1,0:T(8,128)(2,1)S(1)} %get-tuple-element.45), channel_id=1, source_target_pairs={{64,0},{128,64},{192,128},{256,192},{320,256},{384,320},{448,384},... | collective-permute-start | bytes 1179656 | tf_op jit(solution)/shard_map/ppermute | solution.py:78
  92.3 2.5 %collective-permute-start.8 = (bf16[256,512]{1,0:T(8,128)(2,1)S(1)}, bf16[256,512]{1,0:T(8,128)(2,1)S(1)}, u32[]{:S(2)}, u32[]{:S(2)}) collective-permute-start(bf16[256,512]{1,0:T(8,128)(2,1)S(1)} %get-tuple-element.36), channel_id=1, source_target_pairs={{64,8},{65,9},{66,10},{67,11},{68,12},{69,13},{70,14},{71,15},{72,... | collective-permute-start | bytes 786440 | tf_op jit(solution)/shard_map/ppermute | solution.py:88
  94.8 2.4 %collective-permute-start.17 = (bf16[256,512]{1,0:T(8,128)(2,1)S(1)}, bf16[256,512]{1,0:T(8,128)(2,1)S(1)}, u32[]{:S(2)}, u32[]{:S(2)}) collective-permute-start(bf16[256,512]{1,0:T(8,128)(2,1)S(1)} %get-tuple-element.46), channel_id=1, source_target_pairs={{64,8},{65,9},{66,10},{67,11},{68,12},{69,13},{70,14},{71,15},{72,... | collective-permute-start | bytes 786440 | tf_op jit(solution)/shard_map/ppermute | solution.py:88
  97.2 8.4 %collective-permute-done.8.other_ref.acts_other_ref = bf16[256,512]{1,0:T(8,128)(2,1)S(1)} collective-permute-done((bf16[256,512]{1,0:T(8,128)(2,1)S(1)}, bf16[256,512]{1,0:T(8,128)(2,1)S(1)}, u32[]{:S(2)}, u32[]{:S(2)}) %collective-permute-start.8) | collective-permute-done | bytes 262176 | tf_op jit(solution)/shard_map/ppermute | solution.py:88
  114.1 2.5 %collective-permute-start.19 = (bf16[256,512]{1,0:T(8,128)(2,1)S(1)}, bf16[256,512]{1,0:T(8,128)(2,1)S(1)}, u32[]{:S(2)}, u32[]{:S(2)}) collective-permute-start(bf16[256,512]{1,0:T(8,128)(2,1)S(1)} %get-tuple-element.49), channel_id=1, source_target_pairs={{64,8},{65,9},{66,10},{67,11},{68,12},{69,13},{70,14},{71,15},{72,... | collective-permute-start | bytes 786440 | tf_op jit(solution)/shard_map/ppermute | solution.py:88
  116.5 4.7 %collective-permute-done.10.other_ref.acts_other_ref = bf16[256,512]{1,0:T(8,128)(2,1)S(1)} collective-permute-done((bf16[256,512]{1,0:T(8,128)(2,1)S(1)}, bf16[256,512]{1,0:T(8,128)(2,1)S(1)}, u32[]{:S(2)}, u32[]{:S(2)}) %collective-permute-start.10) | collective-permute-done | bytes 262176 | tf_op jit(solution)/shard_map/ppermute | solution.py:88
  122.6 5.6 %collective-permute-done.19.other_ref = bf16[256,512]{1,0:T(8,128)(2,1)S(1)} collective-permute-done((bf16[256,512]{1,0:T(8,128)(2,1)S(1)}, bf16[256,512]{1,0:T(8,128)(2,1)S(1)}, u32[]{:S(2)}, u32[]{:S(2)}) %collective-permute-start.19) | collective-permute-done | bytes 262176 | tf_op jit(solution)/shard_map/ppermute | solution.py:88
  129.8 3.7 %collective-permute-start.24 = (bf16[256,512]{1,0:T(8,128)(2,1)S(1)}, bf16[256,512]{1,0:T(8,128)(2,1)S(1)}, u32[]{:S(2)}, u32[]{:S(2)}) collective-permute-start(bf16[256,512]{1,0:T(8,128)(2,1)S(1)} %shard_map.85), channel_id=1, source_target_pairs={{4,0},{5,1},{6,2},{7,3},{0,4},{1,5},{2,6},{3,7},{12,8},{13,9},{14,... | collective-permute-start | bytes 786440 | tf_op jit(solution)/shard_map/ppermute | solution.py:47
  133.5 2.8 %collective-permute-start.22 = (bf16[256,512]{1,0:T(8,128)(2,1)S(1)}, bf16[256,512]{1,0:T(8,128)(2,1)S(1)}, u32[]{:S(2)}, u32[]{:S(2)}) collective-permute-start(bf16[256,512]{1,0:T(8,128)(2,1)S(1)} %shard_map.86), channel_id=1, source_target_pairs={{2,0},{3,1},{0,2},{1,3},{6,4},{7,5},{4,6},{5,7},{10,8},{11,9},{8,1... | collective-permute-start | bytes 786440 | tf_op jit(solution)/shard_map/ppermute | solution.py:47
  136.3 3.3 %collective-permute-start.23 = (bf16[256,512]{1,0:T(8,128)(2,1)S(1)}, bf16[256,512]{1,0:T(8,128)(2,1)S(1)}, u32[]{:S(2)}, u32[]{:S(2)}) collective-permute-start(bf16[256,512]{1,0:T(8,128)(2,1)S(1)} %shard_map.87), channel_id=1, source_target_pairs={{6,0},{7,1},{4,2},{5,3},{2,4},{3,5},{0,6},{1,7},{14,8},{15,9},{12,... | collective-permute-start | bytes 786440 | tf_op jit(solution)/shard_map/ppermute | solution.py:47
  142.4 2.5 %collective-permute-done.22 = bf16[256,512]{1,0:T(8,128)(2,1)S(1)} collective-permute-done((bf16[256,512]{1,0:T(8,128)(2,1)S(1)}, bf16[256,512]{1,0:T(8,128)(2,1)S(1)}, u32[]{:S(2)}, u32[]{:S(2)}) %collective-permute-start.22) | collective-permute-done | bytes 262176 | tf_op jit(solution)/shard_map/ppermute | solution.py:47
  147.7 7.9 %all-to-all-start.1 = ((bf16[8,32,512]{2,1,0:T(8,128)(2,1)}), bf16[8,32,512]{2,1,0:T(8,128)(2,1)}, u32[]{:S(2)}, u32[]{:S(2)}) async-start(bf16[8,32,512]{2,1,0:T(8,128)(2,1)} %bitcast.26), calls=%async_computation.1 | async-start | bytes 524288 | tf_op jit(solution)/shard_map/all_to_all | solution.py:71
  164.7 2.5 %collective-permute-start.12 = (bf16[128,512]{1,0:T(8,128)(2,1)S(1)}, bf16[128,512]{1,0:T(8,128)(2,1)S(1)}, u32[]{:S(2)}, u32[]{:S(2)}) collective-permute-start(bf16[128,512]{1,0:T(8,128)(2,1)S(1)} %get-tuple-element.40), channel_id=1, source_target_pairs={{64,8},{65,9},{66,10},{67,11},{68,12},{69,13},{70,14},{71,15},{72,... | collective-permute-start | bytes 393224 | tf_op jit(solution)/shard_map/ppermute | solution.py:88
  169.5 4.0 %collective-permute-done.12.crossed_ref = bf16[128,512]{1,0:T(8,128)(2,1)S(1)} collective-permute-done((bf16[128,512]{1,0:T(8,128)(2,1)S(1)}, bf16[128,512]{1,0:T(8,128)(2,1)S(1)}, u32[]{:S(2)}, u32[]{:S(2)}) %collective-permute-start.12) | collective-permute-done | bytes 131104 | tf_op jit(solution)/shard_map/ppermute | solution.py:88
  (66 shorter events, 49.4 us)
Async XLA Ops:
  34.3 15.1 %collective-permute-start.2 = (bf16[256,1024]{1,0:T(8,128)(2,1)S(1)}, bf16[256,1024]{1,0:T(8,128)(2,1)S(1)}, u32[]{:S(2)}, u32[]{:S(2)}) collective-permute-start(bf16[256,1024]{1,0:T(8,128)(2,1)S(1)} %bitcast.13), channel_id=1, source_target_pairs={{6,0},{7,1},{4,2},{5,3},{2,4},{3,5},{0,6},{1,7},{14,8},{15,9},{12,... | collective-permute-start | bytes 1572872 | tf_op jit(solution)/shard_map/ppermute | solution.py:47
  39.0 15.0 %collective-permute-start.1 = (bf16[256,1024]{1,0:T(8,128)(2,1)S(1)}, bf16[256,1024]{1,0:T(8,128)(2,1)S(1)}, u32[]{:S(2)}, u32[]{:S(2)}) collective-permute-start(bf16[256,1024]{1,0:T(8,128)(2,1)S(1)} %bitcast.14), channel_id=1, source_target_pairs={{2,0},{3,1},{0,2},{1,3},{6,4},{7,5},{4,6},{5,7},{10,8},{11,9},{8,1... | collective-permute-start | bytes 1572872 | tf_op jit(solution)/shard_map/ppermute | solution.py:47
  41.1 17.9 %collective-permute-start = (f32[128,512]{1,0:T(8,128)S(1)}, f32[128,512]{1,0:T(8,128)S(1)}, u32[]{:S(2)}, u32[]{:S(2)}) collective-permute-start(f32[128,512]{1,0:T(8,128)S(1)} %slice_bitcast_fusion), channel_id=1, source_target_pairs={{8,0},{9,1},{10,2},{11,3},{12,4},{13,5},{14,6},{15,7},{0,8},{1,9},... | collective-permute-start | bytes 786440 | tf_op jit(solution)/shard_map/ppermute | solution.py:55
  49.4 9.7 %collective-permute-start.3 = (bf16[128,1024]{1,0:T(8,128)(2,1)S(1)}, bf16[128,1024]{1,0:T(8,128)(2,1)S(1)}, u32[]{:S(2)}, u32[]{:S(2)}) collective-permute-start(bf16[128,1024]{1,0:T(8,128)(2,1)S(1)} %slice.17), channel_id=1, source_target_pairs={{2,0},{3,1},{0,2},{1,3},{6,4},{7,5},{4,6},{5,7},{10,8},{11,9},{8,1... | collective-permute-start | bytes 786440 | tf_op jit(solution)/shard_map/ppermute | solution.py:47
  53.9 9.5 %collective-permute-start.4 = (bf16[128,1024]{1,0:T(8,128)(2,1)S(1)}, bf16[128,1024]{1,0:T(8,128)(2,1)S(1)}, u32[]{:S(2)}, u32[]{:S(2)}) collective-permute-start(bf16[128,1024]{1,0:T(8,128)(2,1)S(1)} %slice.18), channel_id=1, source_target_pairs={{6,0},{7,1},{4,2},{5,3},{2,4},{3,5},{0,6},{1,7},{14,8},{15,9},{12,... | collective-permute-start | bytes 786440 | tf_op jit(solution)/shard_map/ppermute | solution.py:47
  56.1 10.6 %collective-permute-start.13 = (bf16[128,512]{1,0:T(8,128)(2,1)S(1)}, bf16[128,512]{1,0:T(8,128)(2,1)S(1)}, u32[]{:S(2)}, u32[]{:S(2)}) collective-permute-start(bf16[128,512]{1,0:T(8,128)(2,1)S(1)} %fusion), channel_id=1, source_target_pairs={{8,0},{9,1},{10,2},{11,3},{12,4},{13,5},{14,6},{15,7},{0,8},{1,9},... | collective-permute-start | bytes 393224 | tf_op jit(solution)/shard_map/ppermute | solution.py:55
  64.8 19.8 %collective-permute-start.5 = (bf16[384,512]{1,0:T(8,128)(2,1)S(1)}, bf16[384,512]{1,0:T(8,128)(2,1)S(1)}, u32[]{:S(2)}, u32[]{:S(2)}) collective-permute-start(bf16[384,512]{1,0:T(8,128)(2,1)S(1)} %get-tuple-element.33), channel_id=1, source_target_pairs={{64,0},{128,64},{192,128},{256,192},{320,256},{384,320},{448,384},... | collective-permute-start | bytes 1179656 | tf_op jit(solution)/shard_map/ppermute | solution.py:78
  68.0 19.9 %collective-permute-start.14 = (bf16[384,512]{1,0:T(8,128)(2,1)S(1)}, bf16[384,512]{1,0:T(8,128)(2,1)S(1)}, u32[]{:S(2)}, u32[]{:S(2)}) collective-permute-start(bf16[384,512]{1,0:T(8,128)(2,1)S(1)} %get-tuple-element.42), channel_id=1, source_target_pairs={{64,0},{128,64},{192,128},{256,192},{320,256},{384,320},{448,384},... | collective-permute-start | bytes 1179656 | tf_op jit(solution)/shard_map/ppermute | solution.py:78
  71.3 13.3 %collective-permute-start.6 = (bf16[256,512]{1,0:T(8,128)(2,1)S(1)}, bf16[256,512]{1,0:T(8,128)(2,1)S(1)}, u32[]{:S(2)}, u32[]{:S(2)}) collective-permute-start(bf16[256,512]{1,0:T(8,128)(2,1)S(1)} %get-tuple-element.34), channel_id=1, source_target_pairs={{64,8},{65,9},{66,10},{67,11},{68,12},{69,13},{70,14},{71,15},{72,... | collective-permute-start | bytes 786440 | tf_op jit(solution)/shard_map/ppermute | solution.py:88
  73.6 14.3 %collective-permute-start.15 = (bf16[256,512]{1,0:T(8,128)(2,1)S(1)}, bf16[256,512]{1,0:T(8,128)(2,1)S(1)}, u32[]{:S(2)}, u32[]{:S(2)}) collective-permute-start(bf16[256,512]{1,0:T(8,128)(2,1)S(1)} %get-tuple-element.43), channel_id=1, source_target_pairs={{64,8},{65,9},{66,10},{67,11},{68,12},{69,13},{70,14},{71,15},{72,... | collective-permute-start | bytes 786440 | tf_op jit(solution)/shard_map/ppermute | solution.py:88
  86.0 19.6 %collective-permute-start.7 = (bf16[384,512]{1,0:T(8,128)(2,1)S(1)}, bf16[384,512]{1,0:T(8,128)(2,1)S(1)}, u32[]{:S(2)}, u32[]{:S(2)}) collective-permute-start(bf16[384,512]{1,0:T(8,128)(2,1)S(1)} %get-tuple-element.35), channel_id=1, source_target_pairs={{64,0},{128,64},{192,128},{256,192},{320,256},{384,320},{448,384},... | collective-permute-start | bytes 1179656 | tf_op jit(solution)/shard_map/ppermute | solution.py:78
  89.2 19.7 %collective-permute-start.16 = (bf16[384,512]{1,0:T(8,128)(2,1)S(1)}, bf16[384,512]{1,0:T(8,128)(2,1)S(1)}, u32[]{:S(2)}, u32[]{:S(2)}) collective-permute-start(bf16[384,512]{1,0:T(8,128)(2,1)S(1)} %get-tuple-element.45), channel_id=1, source_target_pairs={{64,0},{128,64},{192,128},{256,192},{320,256},{384,320},{448,384},... | collective-permute-start | bytes 1179656 | tf_op jit(solution)/shard_map/ppermute | solution.py:78
  92.3 13.3 %collective-permute-start.8 = (bf16[256,512]{1,0:T(8,128)(2,1)S(1)}, bf16[256,512]{1,0:T(8,128)(2,1)S(1)}, u32[]{:S(2)}, u32[]{:S(2)}) collective-permute-start(bf16[256,512]{1,0:T(8,128)(2,1)S(1)} %get-tuple-element.36), channel_id=1, source_target_pairs={{64,8},{65,9},{66,10},{67,11},{68,12},{69,13},{70,14},{71,15},{72,... | collective-permute-start | bytes 786440 | tf_op jit(solution)/shard_map/ppermute | solution.py:88
  94.8 14.1 %collective-permute-start.17 = (bf16[256,512]{1,0:T(8,128)(2,1)S(1)}, bf16[256,512]{1,0:T(8,128)(2,1)S(1)}, u32[]{:S(2)}, u32[]{:S(2)}) collective-permute-start(bf16[256,512]{1,0:T(8,128)(2,1)S(1)} %get-tuple-element.46), channel_id=1, source_target_pairs={{64,8},{65,9},{66,10},{67,11},{68,12},{69,13},{70,14},{71,15},{72,... | collective-permute-start | bytes 786440 | tf_op jit(solution)/shard_map/ppermute | solution.py:88
  107.0 14.3 %collective-permute-start.9 = (bf16[384,512]{1,0:T(8,128)(2,1)S(1)}, bf16[384,512]{1,0:T(8,128)(2,1)S(1)}, u32[]{:S(2)}, u32[]{:S(2)}) collective-permute-start(bf16[384,512]{1,0:T(8,128)(2,1)S(1)} %get-tuple-element.37), channel_id=1, source_target_pairs={{64,0},{128,64},{192,128},{256,192},{320,256},{384,320},{448,384},... | collective-permute-start | bytes 1179656 | tf_op jit(solution)/shard_map/ppermute | solution.py:78
  110.2 18.0 %collective-permute-start.18 = (bf16[384,512]{1,0:T(8,128)(2,1)S(1)}, bf16[384,512]{1,0:T(8,128)(2,1)S(1)}, u32[]{:S(2)}, u32[]{:S(2)}) collective-permute-start(bf16[384,512]{1,0:T(8,128)(2,1)S(1)} %get-tuple-element.48), channel_id=1, source_target_pairs={{64,0},{128,64},{192,128},{256,192},{320,256},{384,320},{448,384},... | collective-permute-start | bytes 1179656 | tf_op jit(solution)/shard_map/ppermute | solution.py:78
  112.1 9.1 %collective-permute-start.10 = (bf16[256,512]{1,0:T(8,128)(2,1)S(1)}, bf16[256,512]{1,0:T(8,128)(2,1)S(1)}, u32[]{:S(2)}, u32[]{:S(2)}) collective-permute-start(bf16[256,512]{1,0:T(8,128)(2,1)S(1)} %get-tuple-element.38), channel_id=1, source_target_pairs={{64,8},{65,9},{66,10},{67,11},{68,12},{69,13},{70,14},{71,15},{72,... | collective-permute-start | bytes 786440 | tf_op jit(solution)/shard_map/ppermute | solution.py:88
  114.1 14.2 %collective-permute-start.19 = (bf16[256,512]{1,0:T(8,128)(2,1)S(1)}, bf16[256,512]{1,0:T(8,128)(2,1)S(1)}, u32[]{:S(2)}, u32[]{:S(2)}) collective-permute-start(bf16[256,512]{1,0:T(8,128)(2,1)S(1)} %get-tuple-element.49), channel_id=1, source_target_pairs={{64,8},{65,9},{66,10},{67,11},{68,12},{69,13},{70,14},{71,15},{72,... | collective-permute-start | bytes 786440 | tf_op jit(solution)/shard_map/ppermute | solution.py:88
  129.8 12.6 %collective-permute-start.24 = (bf16[256,512]{1,0:T(8,128)(2,1)S(1)}, bf16[256,512]{1,0:T(8,128)(2,1)S(1)}, u32[]{:S(2)}, u32[]{:S(2)}) collective-permute-start(bf16[256,512]{1,0:T(8,128)(2,1)S(1)} %shard_map.85), channel_id=1, source_target_pairs={{4,0},{5,1},{6,2},{7,3},{0,4},{1,5},{2,6},{3,7},{12,8},{13,9},{14,... | collective-permute-start | bytes 786440 | tf_op jit(solution)/shard_map/ppermute | solution.py:47
  133.5 11.4 %collective-permute-start.22 = (bf16[256,512]{1,0:T(8,128)(2,1)S(1)}, bf16[256,512]{1,0:T(8,128)(2,1)S(1)}, u32[]{:S(2)}, u32[]{:S(2)}) collective-permute-start(bf16[256,512]{1,0:T(8,128)(2,1)S(1)} %shard_map.86), channel_id=1, source_target_pairs={{2,0},{3,1},{0,2},{1,3},{6,4},{7,5},{4,6},{5,7},{10,8},{11,9},{8,1... | collective-permute-start | bytes 786440 | tf_op jit(solution)/shard_map/ppermute | solution.py:47
  136.3 10.6 %collective-permute-start.23 = (bf16[256,512]{1,0:T(8,128)(2,1)S(1)}, bf16[256,512]{1,0:T(8,128)(2,1)S(1)}, u32[]{:S(2)}, u32[]{:S(2)}) collective-permute-start(bf16[256,512]{1,0:T(8,128)(2,1)S(1)} %shard_map.87), channel_id=1, source_target_pairs={{6,0},{7,1},{4,2},{5,3},{2,4},{3,5},{0,6},{1,7},{14,8},{15,9},{12,... | collective-permute-start | bytes 786440 | tf_op jit(solution)/shard_map/ppermute | solution.py:47
  147.7 26.6 %all-to-all-start.1 = ((bf16[8,32,512]{2,1,0:T(8,128)(2,1)}), bf16[8,32,512]{2,1,0:T(8,128)(2,1)}, u32[]{:S(2)}, u32[]{:S(2)}) async-start(bf16[8,32,512]{2,1,0:T(8,128)(2,1)} %bitcast.26), calls=%async_computation.1 | async-start | bytes 524288 | tf_op jit(solution)/shard_map/all_to_all | solution.py:71
  158.6 10.1 %collective-permute-start.20 = (bf16[256,512]{1,0:T(8,128)(2,1)S(1)}, bf16[256,512]{1,0:T(8,128)(2,1)S(1)}, u32[]{:S(2)}, u32[]{:S(2)}) collective-permute-start(bf16[256,512]{1,0:T(8,128)(2,1)S(1)} %get-tuple-element.61), channel_id=1, source_target_pairs={{64,0},{128,64},{192,128},{256,192},{320,256},{384,320},{448,384},... | collective-permute-start | bytes 786440 | tf_op jit(solution)/shard_map/ppermute | solution.py:78
  160.5 13.0 %collective-permute-start.11 = (bf16[256,512]{1,0:T(8,128)(2,1)S(1)}, bf16[256,512]{1,0:T(8,128)(2,1)S(1)}, u32[]{:S(2)}, u32[]{:S(2)}) collective-permute-start(bf16[256,512]{1,0:T(8,128)(2,1)S(1)} %copy-done.6), channel_id=1, source_target_pairs={{64,0},{128,64},{192,128},{256,192},{320,256},{384,320},{448,384},... | collective-permute-start | bytes 786440 | tf_op jit(solution)/shard_map/ppermute | solution.py:78
  (9 other events, 93.7 us)
where the time goes:
time: 177 us; the launch traced here: 176 us
  starting transfers between devices  73.1 us (41%)
  waiting for transfers between devices  49.8 us (28%)
  blocking collectives  32.8 us (19%)
  Pallas kernels  14.7 us (8%)
  other arithmetic  3.23 us (2%)
    all_to_all x1, blocking collectives, exchanged(): lax.all_to_all(blocks, 'dp', 0, 0, axis_index_groups=alike_groups(), tile...  32.8 us
    ppermute x8, waiting for transfers between devices, passed_back_to_partner(): return lax.ppermute(block, ('section', 'dp'), route)  31.3 us
    ppermute x7, starting transfers between devices, swapped_along_x(): return lax.ppermute(block, 'dp', route)  20.9 us
    ppermute x8, starting transfers between devices, passed_back_to_partner(): return lax.ppermute(block, ('section', 'dp'), route)  20.2 us
    ppermute x7, waiting for transfers between devices, swapped_along_x(): return lax.ppermute(block, 'dp', route)  18.5 us
    ppermute x8, starting transfers between devices, passed_back(): return lax.ppermute(block, 'section', [(i, i - 1) for i in devices if i])  17.9 us
    pallas_call x15, Pallas kernels, call(): pl.pallas_call(kernel, out_shape=tuple((jax.ShapeDtypeStruct(shape, dtype...  14.7 us
    all_to_all x1, starting transfers between devices, exchanged(): lax.all_to_all(blocks, 'dp', 0, 0, axis_index_groups=alike_groups(), tile...  7.91 us
  transfers between devices with their start and end apart: 26, of which 12 were waited for; matrix products, arithmetic and copies ran while one was open for 0% of the time, Pallas kernels for 7%

commit v1 on v0

--- a/solution.py
+++ b/solution.py
@@ -359,11 +359,13 @@
             grads_pair, hidden, addends = lax.optimization_barrier((grads_pair, hidden, addends))
             cotangents.append(cotangent_of(grads_pair))
             outer = functools.partial(outer_rows, hiddens, cotangents, count=quarter)
-            parts = [outer(i * quarter) for i in (3, 1, 2)]
-            from_far = swapped_along_x(parts[0], far_x)
-            from_near = swapped_along_x(parts[1], near_x)
-            from_next = swapped_along_x(parts[2], next_x)
-            slopes, _ = lax.optimization_barrier((slopes, parts))
+            far_rows = outer(3 * quarter)
+            near_rows = outer(quarter)
+            next_rows = outer(2 * quarter)
+            from_far = swapped_along_x(far_rows, far_x)
+            from_near = swapped_along_x(near_rows, near_x)
+            from_next = swapped_along_x(next_rows, next_x)
+            slopes, _ = lax.optimization_barrier((slopes, (far_rows, near_rows, next_rows)))
         cotangent, *addends = backward(
             fresh, last, tokens, acts_pair, grads_pair, gain, slopes, weights
         )
@@ -372,6 +374,7 @@
             blocks = sum(
                 x.astype(jnp.float32) for x in (own, from_near, from_next, from_far)
             ).astype(jnp.bfloat16)
+            blocks, addends = lax.optimization_barrier((blocks, addends))
             parts = exchanged(blocks).reshape(-1, units, half)
         else:
             cotangents.append(cotangent)

time: 177 us -> 174 us (0.983)
  transfers between devices with their start and end apart: 26 -> 26, of which waited for: 12 -> 10; matrix products, arithmetic and copies ran while one was open for 0% -> 0% of each run, Pallas kernels for 7% -> 8%
where the time goes in v1:
time: 174 us; the launch traced here: 173 us
  starting transfers between devices  72.8 us (42%)
  waiting for transfers between devices  48.9 us (28%)
  blocking collectives  32.8 us (19%)
  Pallas kernels  14.7 us (8%)
  other arithmetic  2.27 us (1%)
    all_to_all x1, blocking collectives, exchanged(): lax.all_to_all(blocks, 'dp', 0, 0, axis_index_groups=alike_groups(), tile...  32.8 us
    ppermute x8, waiting for transfers between devices, passed_back_to_partner(): return lax.ppermute(block, ('section', 'dp'), route)  31.7 us
    ppermute x7, starting transfers between devices, swapped_along_x(): return lax.ppermute(block, 'dp', route)  20.9 us
    ppermute x8, starting transfers between devices, passed_back_to_partner(): return lax.ppermute(block, ('section', 'dp'), route)  20 us
    ppermute x8, starting transfers between devices, passed_back(): return lax.ppermute(block, 'section', [(i, i - 1) for i in devices if i])  17.9 us
    ppermute x7, waiting for transfers between devices, swapped_along_x(): return lax.ppermute(block, 'dp', route)  17.1 us
    pallas_call x15, Pallas kernels, call(): pl.pallas_call(kernel, out_shape=tuple((jax.ShapeDtypeStruct(shape, dtype...  14.7 us
    all_to_all x1, starting transfers between devices, exchanged(): lax.all_to_all(blocks, 'dp', 0, 0, axis_index_groups=alike_groups(), tile...  7.85 us
  transfers between devices with their start and end apart: 26, of which 10 were waited for; matrix products, arithmetic and copies ran while one was open for 0% of the time, Pallas kernels for 8%

profile of v1, /device:TPU:48, one launch (start us, length us, event | category | flops | bytes accessed | tf_op | source)
XLA Modules:
  0.0 172.7 jit_solution(1419353581116553514)
XLA Ops:
  1.5 32.8 %all_to_all.17 = bf16[8,32,1024]{2,1,0:T(8,128)(2,1)S(1)} all-to-all(bf16[8,32,1024]{2,1,0:T(8,128)(2,1)S(1)} %tile.2), channel_id=1, replica_groups={{0,1,16,17,32,33,48,49},{2,3,18,19,34,35,50,51},{4,5,20,21,36,37,52,53}..., dimensions={0} | all-to-all | bytes 1048576 | tf_op jit(solution)/shard_map/all_to_all | solution.py:71
  34.3 4.7 %collective-permute-start.2 = (bf16[256,1024]{1,0:T(8,128)(2,1)S(1)}, bf16[256,1024]{1,0:T(8,128)(2,1)S(1)}, u32[]{:S(2)}, u32[]{:S(2)}) collective-permute-start(bf16[256,1024]{1,0:T(8,128)(2,1)S(1)} %bitcast.13), channel_id=1, source_target_pairs={{6,0},{7,1},{4,2},{5,3},{2,4},{3,5},{0,6},{1,7},{14,8},{15,9},{12,... | collective-permute-start | bytes 1572872 | tf_op jit(solution)/shard_map/ppermute | solution.py:47
  41.1 3.2 %collective-permute-start = (f32[128,512]{1,0:T(8,128)S(1)}, f32[128,512]{1,0:T(8,128)S(1)}, u32[]{:S(2)}, u32[]{:S(2)}) collective-permute-start(f32[128,512]{1,0:T(8,128)S(1)} %slice_bitcast_fusion), channel_id=1, source_target_pairs={{8,0},{9,1},{10,2},{11,3},{12,4},{13,5},{14,6},{15,7},{0,8},{1,9},... | collective-permute-start | bytes 786440 | tf_op jit(solution)/shard_map/ppermute | solution.py:55
  44.3 5.1 %collective-permute-done.2.refs_2_ = bf16[256,1024]{1,0:T(8,128)(2,1)S(1)} collective-permute-done((bf16[256,1024]{1,0:T(8,128)(2,1)S(1)}, bf16[256,1024]{1,0:T(8,128)(2,1)S(1)}, u32[]{:S(2)}, u32[]{:S(2)}) %collective-permute-start.2) | collective-permute-done | bytes 524320 | tf_op jit(solution)/shard_map/ppermute | solution.py:47
  51.6 2.3 %collective-permute-done.1.refs_1_ = bf16[256,1024]{1,0:T(8,128)(2,1)S(1)} collective-permute-done((bf16[256,1024]{1,0:T(8,128)(2,1)S(1)}, bf16[256,1024]{1,0:T(8,128)(2,1)S(1)}, u32[]{:S(2)}, u32[]{:S(2)}) %collective-permute-start.1) | collective-permute-done | bytes 524320 | tf_op jit(solution)/shard_map/ppermute | solution.py:47
  56.1 3.0 %collective-permute-start.13 = (bf16[128,512]{1,0:T(8,128)(2,1)S(1)}, bf16[128,512]{1,0:T(8,128)(2,1)S(1)}, u32[]{:S(2)}, u32[]{:S(2)}) collective-permute-start(bf16[128,512]{1,0:T(8,128)(2,1)S(1)} %fusion), channel_id=1, source_target_pairs={{8,0},{9,1},{10,2},{11,3},{12,4},{13,5},{14,6},{15,7},{0,8},{1,9},... | collective-permute-start | bytes 393224 | tf_op jit(solution)/shard_map/ppermute | solution.py:55
  59.1 4.3 %collective-permute-done.4.refs_4_ = bf16[128,1024]{1,0:T(8,128)(2,1)S(1)} collective-permute-done((bf16[128,1024]{1,0:T(8,128)(2,1)S(1)}, bf16[128,1024]{1,0:T(8,128)(2,1)S(1)}, u32[]{:S(2)}, u32[]{:S(2)}) %collective-permute-start.4) | collective-permute-done | bytes 262176 | tf_op jit(solution)/shard_map/ppermute | solution.py:47
  68.0 3.3 %collective-permute-start.14 = (bf16[384,512]{1,0:T(8,128)(2,1)S(1)}, bf16[384,512]{1,0:T(8,128)(2,1)S(1)}, u32[]{:S(2)}, u32[]{:S(2)}) collective-permute-start(bf16[384,512]{1,0:T(8,128)(2,1)S(1)} %get-tuple-element.50), channel_id=1, source_target_pairs={{64,0},{128,64},{192,128},{256,192},{320,256},{384,320},{448,384},... | collective-permute-start | bytes 1179656 | tf_op jit(solution)/shard_map/ppermute | solution.py:78
  71.3 2.3 %collective-permute-start.6 = (bf16[256,512]{1,0:T(8,128)(2,1)S(1)}, bf16[256,512]{1,0:T(8,128)(2,1)S(1)}, u32[]{:S(2)}, u32[]{:S(2)}) collective-permute-start(bf16[256,512]{1,0:T(8,128)(2,1)S(1)} %get-tuple-element.37), channel_id=1, source_target_pairs={{64,8},{65,9},{66,10},{67,11},{68,12},{69,13},{70,14},{71,15},{72,... | collective-permute-start | bytes 786440 | tf_op jit(solution)/shard_map/ppermute | solution.py:88
  73.6 3.8 %collective-permute-start.15 = (bf16[256,512]{1,0:T(8,128)(2,1)S(1)}, bf16[256,512]{1,0:T(8,128)(2,1)S(1)}, u32[]{:S(2)}, u32[]{:S(2)}) collective-permute-start(bf16[256,512]{1,0:T(8,128)(2,1)S(1)} %get-tuple-element.51), channel_id=1, source_target_pairs={{64,8},{65,9},{66,10},{67,11},{68,12},{69,13},{70,14},{71,15},{72,... | collective-permute-start | bytes 786440 | tf_op jit(solution)/shard_map/ppermute | solution.py:88
  77.4 7.2 %collective-permute-done.6.other_ref.acts_other_ref = bf16[256,512]{1,0:T(8,128)(2,1)S(1)} collective-permute-done((bf16[256,512]{1,0:T(8,128)(2,1)S(1)}, bf16[256,512]{1,0:T(8,128)(2,1)S(1)}, u32[]{:S(2)}, u32[]{:S(2)}) %collective-permute-start.6) | collective-permute-done | bytes 262176 | tf_op jit(solution)/shard_map/ppermute | solution.py:88
  89.2 3.1 %collective-permute-start.16 = (bf16[384,512]{1,0:T(8,128)(2,1)S(1)}, bf16[384,512]{1,0:T(8,128)(2,1)S(1)}, u32[]{:S(2)}, u32[]{:S(2)}) collective-permute-start(bf16[384,512]{1,0:T(8,128)(2,1)S(1)} %get-tuple-element.54), channel_id=1, source_target_pairs={{64,0},{128,64},{192,128},{256,192},{320,256},{384,320},{448,384},... | collective-permute-start | bytes 1179656 | tf_op jit(solution)/shard_map/ppermute | solution.py:78
  92.3 2.5 %collective-permute-start.8 = (bf16[256,512]{1,0:T(8,128)(2,1)S(1)}, bf16[256,512]{1,0:T(8,128)(2,1)S(1)}, u32[]{:S(2)}, u32[]{:S(2)}) collective-permute-start(bf16[256,512]{1,0:T(8,128)(2,1)S(1)} %get-tuple-element.39), channel_id=1, source_target_pairs={{64,8},{65,9},{66,10},{67,11},{68,12},{69,13},{70,14},{71,15},{72,... | collective-permute-start | bytes 786440 | tf_op jit(solution)/shard_map/ppermute | solution.py:88
  94.7 2.4 %collective-permute-start.17 = (bf16[256,512]{1,0:T(8,128)(2,1)S(1)}, bf16[256,512]{1,0:T(8,128)(2,1)S(1)}, u32[]{:S(2)}, u32[]{:S(2)}) collective-permute-start(bf16[256,512]{1,0:T(8,128)(2,1)S(1)} %get-tuple-element.55), channel_id=1, source_target_pairs={{64,8},{65,9},{66,10},{67,11},{68,12},{69,13},{70,14},{71,15},{72,... | collective-permute-start | bytes 786440 | tf_op jit(solution)/shard_map/ppermute | solution.py:88
  97.2 8.4 %collective-permute-done.8.other_ref.acts_other_ref = bf16[256,512]{1,0:T(8,128)(2,1)S(1)} collective-permute-done((bf16[256,512]{1,0:T(8,128)(2,1)S(1)}, bf16[256,512]{1,0:T(8,128)(2,1)S(1)}, u32[]{:S(2)}, u32[]{:S(2)}) %collective-permute-start.8) | collective-permute-done | bytes 262176 | tf_op jit(solution)/shard_map/ppermute | solution.py:88
  114.1 2.4 %collective-permute-start.19 = (bf16[256,512]{1,0:T(8,128)(2,1)S(1)}, bf16[256,512]{1,0:T(8,128)(2,1)S(1)}, u32[]{:S(2)}, u32[]{:S(2)}) collective-permute-start(bf16[256,512]{1,0:T(8,128)(2,1)S(1)} %get-tuple-element.59), channel_id=1, source_target_pairs={{64,8},{65,9},{66,10},{67,11},{68,12},{69,13},{70,14},{71,15},{72,... | collective-permute-start | bytes 786440 | tf_op jit(solution)/shard_map/ppermute | solution.py:88
  116.5 4.7 %collective-permute-done.10.other_ref.acts_other_ref = bf16[256,512]{1,0:T(8,128)(2,1)S(1)} collective-permute-done((bf16[256,512]{1,0:T(8,128)(2,1)S(1)}, bf16[256,512]{1,0:T(8,128)(2,1)S(1)}, u32[]{:S(2)}, u32[]{:S(2)}) %collective-permute-start.10) | collective-permute-done | bytes 262176 | tf_op jit(solution)/shard_map/ppermute | solution.py:88
  122.6 5.6 %collective-permute-done.19.other_ref = bf16[256,512]{1,0:T(8,128)(2,1)S(1)} collective-permute-done((bf16[256,512]{1,0:T(8,128)(2,1)S(1)}, bf16[256,512]{1,0:T(8,128)(2,1)S(1)}, u32[]{:S(2)}, u32[]{:S(2)}) %collective-permute-start.19) | collective-permute-done | bytes 262176 | tf_op jit(solution)/shard_map/ppermute | solution.py:88
  131.7 4.2 %collective-permute-start.21 = (bf16[256,512]{1,0:T(8,128)(2,1)S(1)}, bf16[256,512]{1,0:T(8,128)(2,1)S(1)}, u32[]{:S(2)}, u32[]{:S(2)}) collective-permute-start(bf16[256,512]{1,0:T(8,128)(2,1)S(1)} %shard_map.87), channel_id=1, source_target_pairs={{6,0},{7,1},{4,2},{5,3},{2,4},{3,5},{0,6},{1,7},{14,8},{15,9},{12,... | collective-permute-start | bytes 786440 | tf_op jit(solution)/shard_map/ppermute | solution.py:47
  135.9 3.7 %collective-permute-start.22 = (bf16[256,512]{1,0:T(8,128)(2,1)S(1)}, bf16[256,512]{1,0:T(8,128)(2,1)S(1)}, u32[]{:S(2)}, u32[]{:S(2)}) collective-permute-start(bf16[256,512]{1,0:T(8,128)(2,1)S(1)} %shard_map.88), channel_id=1, source_target_pairs={{4,0},{5,1},{6,2},{7,3},{0,4},{1,5},{2,6},{3,7},{12,8},{13,9},{14,... | collective-permute-start | bytes 786440 | tf_op jit(solution)/shard_map/ppermute | solution.py:47
  142.0 5.4 %collective-permute-done.21 = bf16[256,512]{1,0:T(8,128)(2,1)S(1)} collective-permute-done((bf16[256,512]{1,0:T(8,128)(2,1)S(1)}, bf16[256,512]{1,0:T(8,128)(2,1)S(1)}, u32[]{:S(2)}, u32[]{:S(2)}) %collective-permute-start.21) | collective-permute-done | bytes 262176 | tf_op jit(solution)/shard_map/ppermute | solution.py:47
  148.2 7.9 %all-to-all-start.1 = ((bf16[8,32,512]{2,1,0:T(8,128)(2,1)}), bf16[8,32,512]{2,1,0:T(8,128)(2,1)S(1)}, u32[]{:S(2)}, u32[]{:S(2)}) async-start(bf16[8,32,512]{2,1,0:T(8,128)(2,1)} %bitcast.9), calls=%async_computation.1 | async-start | bytes 524288 | tf_op jit(solution)/shard_map/all_to_all | solution.py:71
  159.9 2.6 %collective-permute-start.12 = (bf16[128,512]{1,0:T(8,128)(2,1)S(1)}, bf16[128,512]{1,0:T(8,128)(2,1)S(1)}, u32[]{:S(2)}, u32[]{:S(2)}) collective-permute-start(bf16[128,512]{1,0:T(8,128)(2,1)S(1)} %get-tuple-element.43), channel_id=1, source_target_pairs={{64,8},{65,9},{66,10},{67,11},{68,12},{69,13},{70,14},{71,15},{72,... | collective-permute-start | bytes 393224 | tf_op jit(solution)/shard_map/ppermute | solution.py:88
  167.0 4.2 %collective-permute-done.24.crossed_ref = bf16[128,512]{1,0:T(8,128)(2,1)S(1)} collective-permute-done((bf16[128,512]{1,0:T(8,128)(2,1)S(1)}, bf16[128,512]{1,0:T(8,128)(2,1)S(1)}, u32[]{:S(2)}, u32[]{:S(2)}) %collective-permute-start.24) | collective-permute-done | bytes 131104 | tf_op jit(solution)/shard_map/ppermute | solution.py:88
  (58 shorter events, 42.6 us)
Async XLA Ops:
  34.3 15.1 %collective-permute-start.2 = (bf16[256,1024]{1,0:T(8,128)(2,1)S(1)}, bf16[256,1024]{1,0:T(8,128)(2,1)S(1)}, u32[]{:S(2)}, u32[]{:S(2)}) collective-permute-start(bf16[256,1024]{1,0:T(8,128)(2,1)S(1)} %bitcast.13), channel_id=1, source_target_pairs={{6,0},{7,1},{4,2},{5,3},{2,4},{3,5},{0,6},{1,7},{14,8},{15,9},{12,... | collective-permute-start | bytes 1572872 | tf_op jit(solution)/shard_map/ppermute | solution.py:47
  39.0 15.0 %collective-permute-start.1 = (bf16[256,1024]{1,0:T(8,128)(2,1)S(1)}, bf16[256,1024]{1,0:T(8,128)(2,1)S(1)}, u32[]{:S(2)}, u32[]{:S(2)}) collective-permute-start(bf16[256,1024]{1,0:T(8,128)(2,1)S(1)} %bitcast.14), channel_id=1, source_target_pairs={{2,0},{3,1},{0,2},{1,3},{6,4},{7,5},{4,6},{5,7},{10,8},{11,9},{8,1... | collective-permute-start | bytes 1572872 | tf_op jit(solution)/shard_map/ppermute | solution.py:47
  41.1 17.9 %collective-permute-start = (f32[128,512]{1,0:T(8,128)S(1)}, f32[128,512]{1,0:T(8,128)S(1)}, u32[]{:S(2)}, u32[]{:S(2)}) collective-permute-start(f32[128,512]{1,0:T(8,128)S(1)} %slice_bitcast_fusion), channel_id=1, source_target_pairs={{8,0},{9,1},{10,2},{11,3},{12,4},{13,5},{14,6},{15,7},{0,8},{1,9},... | collective-permute-start | bytes 786440 | tf_op jit(solution)/shard_map/ppermute | solution.py:55
  49.4 9.7 %collective-permute-start.3 = (bf16[128,1024]{1,0:T(8,128)(2,1)S(1)}, bf16[128,1024]{1,0:T(8,128)(2,1)S(1)}, u32[]{:S(2)}, u32[]{:S(2)}) collective-permute-start(bf16[128,1024]{1,0:T(8,128)(2,1)S(1)} %slice.17), channel_id=1, source_target_pairs={{2,0},{3,1},{0,2},{1,3},{6,4},{7,5},{4,6},{5,7},{10,8},{11,9},{8,1... | collective-permute-start | bytes 786440 | tf_op jit(solution)/shard_map/ppermute | solution.py:47
  53.9 9.5 %collective-permute-start.4 = (bf16[128,1024]{1,0:T(8,128)(2,1)S(1)}, bf16[128,1024]{1,0:T(8,128)(2,1)S(1)}, u32[]{:S(2)}, u32[]{:S(2)}) collective-permute-start(bf16[128,1024]{1,0:T(8,128)(2,1)S(1)} %slice.18), channel_id=1, source_target_pairs={{6,0},{7,1},{4,2},{5,3},{2,4},{3,5},{0,6},{1,7},{14,8},{15,9},{12,... | collective-permute-start | bytes 786440 | tf_op jit(solution)/shard_map/ppermute | solution.py:47
  56.1 10.6 %collective-permute-start.13 = (bf16[128,512]{1,0:T(8,128)(2,1)S(1)}, bf16[128,512]{1,0:T(8,128)(2,1)S(1)}, u32[]{:S(2)}, u32[]{:S(2)}) collective-permute-start(bf16[128,512]{1,0:T(8,128)(2,1)S(1)} %fusion), channel_id=1, source_target_pairs={{8,0},{9,1},{10,2},{11,3},{12,4},{13,5},{14,6},{15,7},{0,8},{1,9},... | collective-permute-start | bytes 393224 | tf_op jit(solution)/shard_map/ppermute | solution.py:55
  64.8 19.8 %collective-permute-start.5 = (bf16[384,512]{1,0:T(8,128)(2,1)S(1)}, bf16[384,512]{1,0:T(8,128)(2,1)S(1)}, u32[]{:S(2)}, u32[]{:S(2)}) collective-permute-start(bf16[384,512]{1,0:T(8,128)(2,1)S(1)} %get-tuple-element.36), channel_id=1, source_target_pairs={{64,0},{128,64},{192,128},{256,192},{320,256},{384,320},{448,384},... | collective-permute-start | bytes 1179656 | tf_op jit(solution)/shard_map/ppermute | solution.py:78
  68.0 19.9 %collective-permute-start.14 = (bf16[384,512]{1,0:T(8,128)(2,1)S(1)}, bf16[384,512]{1,0:T(8,128)(2,1)S(1)}, u32[]{:S(2)}, u32[]{:S(2)}) collective-permute-start(bf16[384,512]{1,0:T(8,128)(2,1)S(1)} %get-tuple-element.50), channel_id=1, source_target_pairs={{64,0},{128,64},{192,128},{256,192},{320,256},{384,320},{448,384},... | collective-permute-start | bytes 1179656 | tf_op jit(solution)/shard_map/ppermute | solution.py:78
  71.3 13.3 %collective-permute-start.6 = (bf16[256,512]{1,0:T(8,128)(2,1)S(1)}, bf16[256,512]{1,0:T(8,128)(2,1)S(1)}, u32[]{:S(2)}, u32[]{:S(2)}) collective-permute-start(bf16[256,512]{1,0:T(8,128)(2,1)S(1)} %get-tuple-element.37), channel_id=1, source_target_pairs={{64,8},{65,9},{66,10},{67,11},{68,12},{69,13},{70,14},{71,15},{72,... | collective-permute-start | bytes 786440 | tf_op jit(solution)/shard_map/ppermute | solution.py:88
  73.6 14.3 %collective-permute-start.15 = (bf16[256,512]{1,0:T(8,128)(2,1)S(1)}, bf16[256,512]{1,0:T(8,128)(2,1)S(1)}, u32[]{:S(2)}, u32[]{:S(2)}) collective-permute-start(bf16[256,512]{1,0:T(8,128)(2,1)S(1)} %get-tuple-element.51), channel_id=1, source_target_pairs={{64,8},{65,9},{66,10},{67,11},{68,12},{69,13},{70,14},{71,15},{72,... | collective-permute-start | bytes 786440 | tf_op jit(solution)/shard_map/ppermute | solution.py:88
  85.9 19.6 %collective-permute-start.7 = (bf16[384,512]{1,0:T(8,128)(2,1)S(1)}, bf16[384,512]{1,0:T(8,128)(2,1)S(1)}, u32[]{:S(2)}, u32[]{:S(2)}) collective-permute-start(bf16[384,512]{1,0:T(8,128)(2,1)S(1)} %get-tuple-element.38), channel_id=1, source_target_pairs={{64,0},{128,64},{192,128},{256,192},{320,256},{384,320},{448,384},... | collective-permute-start | bytes 1179656 | tf_op jit(solution)/shard_map/ppermute | solution.py:78
  89.2 19.7 %collective-permute-start.16 = (bf16[384,512]{1,0:T(8,128)(2,1)S(1)}, bf16[384,512]{1,0:T(8,128)(2,1)S(1)}, u32[]{:S(2)}, u32[]{:S(2)}) collective-permute-start(bf16[384,512]{1,0:T(8,128)(2,1)S(1)} %get-tuple-element.54), channel_id=1, source_target_pairs={{64,0},{128,64},{192,128},{256,192},{320,256},{384,320},{448,384},... | collective-permute-start | bytes 1179656 | tf_op jit(solution)/shard_map/ppermute | solution.py:78
  92.3 13.3 %collective-permute-start.8 = (bf16[256,512]{1,0:T(8,128)(2,1)S(1)}, bf16[256,512]{1,0:T(8,128)(2,1)S(1)}, u32[]{:S(2)}, u32[]{:S(2)}) collective-permute-start(bf16[256,512]{1,0:T(8,128)(2,1)S(1)} %get-tuple-element.39), channel_id=1, source_target_pairs={{64,8},{65,9},{66,10},{67,11},{68,12},{69,13},{70,14},{71,15},{72,... | collective-permute-start | bytes 786440 | tf_op jit(solution)/shard_map/ppermute | solution.py:88
  94.7 14.1 %collective-permute-start.17 = (bf16[256,512]{1,0:T(8,128)(2,1)S(1)}, bf16[256,512]{1,0:T(8,128)(2,1)S(1)}, u32[]{:S(2)}, u32[]{:S(2)}) collective-permute-start(bf16[256,512]{1,0:T(8,128)(2,1)S(1)} %get-tuple-element.55), channel_id=1, source_target_pairs={{64,8},{65,9},{66,10},{67,11},{68,12},{69,13},{70,14},{71,15},{72,... | collective-permute-start | bytes 786440 | tf_op jit(solution)/shard_map/ppermute | solution.py:88
  106.9 14.3 %collective-permute-start.9 = (bf16[384,512]{1,0:T(8,128)(2,1)S(1)}, bf16[384,512]{1,0:T(8,128)(2,1)S(1)}, u32[]{:S(2)}, u32[]{:S(2)}) collective-permute-start(bf16[384,512]{1,0:T(8,128)(2,1)S(1)} %get-tuple-element.40), channel_id=1, source_target_pairs={{64,0},{128,64},{192,128},{256,192},{320,256},{384,320},{448,384},... | collective-permute-start | bytes 1179656 | tf_op jit(solution)/shard_map/ppermute | solution.py:78
  110.2 18.0 %collective-permute-start.18 = (bf16[384,512]{1,0:T(8,128)(2,1)S(1)}, bf16[384,512]{1,0:T(8,128)(2,1)S(1)}, u32[]{:S(2)}, u32[]{:S(2)}) collective-permute-start(bf16[384,512]{1,0:T(8,128)(2,1)S(1)} %get-tuple-element.58), channel_id=1, source_target_pairs={{64,0},{128,64},{192,128},{256,192},{320,256},{384,320},{448,384},... | collective-permute-start | bytes 1179656 | tf_op jit(solution)/shard_map/ppermute | solution.py:78
  112.1 9.1 %collective-permute-start.10 = (bf16[256,512]{1,0:T(8,128)(2,1)S(1)}, bf16[256,512]{1,0:T(8,128)(2,1)S(1)}, u32[]{:S(2)}, u32[]{:S(2)}) collective-permute-start(bf16[256,512]{1,0:T(8,128)(2,1)S(1)} %get-tuple-element.41), channel_id=1, source_target_pairs={{64,8},{65,9},{66,10},{67,11},{68,12},{69,13},{70,14},{71,15},{72,... | collective-permute-start | bytes 786440 | tf_op jit(solution)/shard_map/ppermute | solution.py:88
  114.1 14.2 %collective-permute-start.19 = (bf16[256,512]{1,0:T(8,128)(2,1)S(1)}, bf16[256,512]{1,0:T(8,128)(2,1)S(1)}, u32[]{:S(2)}, u32[]{:S(2)}) collective-permute-start(bf16[256,512]{1,0:T(8,128)(2,1)S(1)} %get-tuple-element.59), channel_id=1, source_target_pairs={{64,8},{65,9},{66,10},{67,11},{68,12},{69,13},{70,14},{71,15},{72,... | collective-permute-start | bytes 786440 | tf_op jit(solution)/shard_map/ppermute | solution.py:88
  129.8 12.2 %collective-permute-start.20 = (bf16[256,512]{1,0:T(8,128)(2,1)S(1)}, bf16[256,512]{1,0:T(8,128)(2,1)S(1)}, u32[]{:S(2)}, u32[]{:S(2)}) collective-permute-start(bf16[256,512]{1,0:T(8,128)(2,1)S(1)} %shard_map.86), channel_id=1, source_target_pairs={{2,0},{3,1},{0,2},{1,3},{6,4},{7,5},{4,6},{5,7},{10,8},{11,9},{8,1... | collective-permute-start | bytes 786440 | tf_op jit(solution)/shard_map/ppermute | solution.py:47
  131.7 15.7 %collective-permute-start.21 = (bf16[256,512]{1,0:T(8,128)(2,1)S(1)}, bf16[256,512]{1,0:T(8,128)(2,1)S(1)}, u32[]{:S(2)}, u32[]{:S(2)}) collective-permute-start(bf16[256,512]{1,0:T(8,128)(2,1)S(1)} %shard_map.87), channel_id=1, source_target_pairs={{6,0},{7,1},{4,2},{5,3},{2,4},{3,5},{0,6},{1,7},{14,8},{15,9},{12,... | collective-permute-start | bytes 786440 | tf_op jit(solution)/shard_map/ppermute | solution.py:47
  135.9 11.4 %collective-permute-start.22 = (bf16[256,512]{1,0:T(8,128)(2,1)S(1)}, bf16[256,512]{1,0:T(8,128)(2,1)S(1)}, u32[]{:S(2)}, u32[]{:S(2)}) collective-permute-start(bf16[256,512]{1,0:T(8,128)(2,1)S(1)} %shard_map.88), channel_id=1, source_target_pairs={{4,0},{5,1},{6,2},{7,3},{0,4},{1,5},{2,6},{3,7},{12,8},{13,9},{14,... | collective-permute-start | bytes 786440 | tf_op jit(solution)/shard_map/ppermute | solution.py:47
  148.2 23.9 %all-to-all-start.1 = ((bf16[8,32,512]{2,1,0:T(8,128)(2,1)}), bf16[8,32,512]{2,1,0:T(8,128)(2,1)S(1)}, u32[]{:S(2)}, u32[]{:S(2)}) async-start(bf16[8,32,512]{2,1,0:T(8,128)(2,1)} %bitcast.9), calls=%async_computation.1 | async-start | bytes 524288 | tf_op jit(solution)/shard_map/all_to_all | solution.py:71
  156.1 10.1 %collective-permute-start.11 = (bf16[256,512]{1,0:T(8,128)(2,1)S(1)}, bf16[256,512]{1,0:T(8,128)(2,1)S(1)}, u32[]{:S(2)}, u32[]{:S(2)}) collective-permute-start(bf16[256,512]{1,0:T(8,128)(2,1)S(1)} %get-tuple-element.42), channel_id=1, source_target_pairs={{64,0},{128,64},{192,128},{256,192},{320,256},{384,320},{448,384},... | collective-permute-start | bytes 786440 | tf_op jit(solution)/shard_map/ppermute | solution.py:78
  158.0 13.2 %collective-permute-start.23 = (bf16[256,512]{1,0:T(8,128)(2,1)S(1)}, bf16[256,512]{1,0:T(8,128)(2,1)S(1)}, u32[]{:S(2)}, u32[]{:S(2)}) collective-permute-start(bf16[256,512]{1,0:T(8,128)(2,1)S(1)} %get-tuple-element.66), channel_id=1, source_target_pairs={{64,0},{128,64},{192,128},{256,192},{320,256},{384,320},{448,384},... | collective-permute-start | bytes 786440 | tf_op jit(solution)/shard_map/ppermute | solution.py:78
  (5 other events, 76.9 us)

commit v2 on v0

--- a/solution.py
+++ b/solution.py
@@ -15,6 +15,7 @@
 
 x_size = 4
 pair_size = 2
+chunk = 256
 
 
 def dp_index(z, x, y):
@@ -29,22 +30,12 @@
     return [
         [
             dp_index(z, x, y)
+            for x in range(x_size)
             for z in range(parity, z_size(), 2)
             for y in range(pair_size)
         ]
         for parity in range(2)
-        for x in range(x_size)
     ]
-
-
-def swapped_along_x(block, peer):
-    route = [
-        (dp_index(z, peer(x), y), dp_index(z, x, y))
-        for z in range(z_size())
-        for x in range(x_size)
-        for y in range(pair_size)
-    ]
-    return lax.ppermute(block, "dp", route)
 
 
 def partner(index):
@@ -53,18 +44,6 @@
 
 def swapped_with_partner(block):
     return lax.ppermute(block, "dp", [(partner(i), i) for i in range(lax.axis_size("dp"))])
-
-
-def near_x(x):
-    return x ^ 1
-
-
-def next_x(x):
-    return (x + 1 if x % 2 else x - 1) % x_size
-
-
-def far_x(x):
-    return (x + 2) % x_size
 
 
 def exchanged(blocks):
@@ -86,14 +65,6 @@
         for i in range(size)
     ]
     return lax.ppermute(block, ("section", "dp"), route)
-
-
-def gathered_along_x(block):
-    rows = block.shape[0] // 2
-    near, following = swapped_along_x(block, near_x), swapped_along_x(block, next_x)
-    far_head = swapped_along_x(following[:rows], near_x)
-    far_tail = swapped_along_x(near[rows:], next_x)
-    return block, near, following, far_head, far_tail
 
 
 def inverse_rms(first):
@@ -138,15 +109,15 @@
         crossed_ref[tokens:] = other.astype(dtype)
 
 
-def forward_kernel(fresh, last, own_ref, other_ref, gain_ref, *refs):
-    weight_refs, (hidden_ref, slopes_ref, straight_ref, crossed_ref) = refs[:-4], refs[-4:]
+def forward_kernel(fresh, last, own_ref, other_ref, gain_ref, weight_ref, *refs):
+    hidden_ref, slopes_ref, straight_ref, crossed_ref = refs
     first, second = pair_state(fresh, own_ref, other_ref, 0)
     tokens, half = second.shape
     normed = (first * inverse_rms(first) * gain_ref[...]).astype(jnp.bfloat16)
-    for span, weight_ref in spans(weight_refs):
+    for span, part_ref in spans(weight_ref):
         preact = lax.dot_general(
             normed,
-            weight_ref[:, :half],
+            part_ref[:, :half],
             (((1,), (1,)), ((), ())),
             preferred_element_type=jnp.float32,
         )
@@ -155,8 +126,8 @@
         hidden_ref[:, span] = (preact * normal_cdf).astype(jnp.bfloat16)
         slopes_ref[:, span] = (normal_cdf + preact * density).astype(slopes_ref.dtype)
     branch = sum(
-        jnp.dot(hidden_ref[:, span], weight_ref[:, half:], preferred_element_type=jnp.float32)
-        for span, weight_ref in spans(weight_refs)
+        jnp.dot(hidden_ref[:, span], part_ref[:, half:], preferred_element_type=jnp.float32)
+        for span, part_ref in spans(weight_ref)
     )
     own = (second - branch[:tokens]) / coupling_scale
     other = (0.0 - branch[tokens:]) / coupling_scale
@@ -164,9 +135,9 @@
 
 
 def backward_kernel(
-    fresh, last, acts_ref, acts_other_ref, own_ref, other_ref, gain_ref, slopes_ref, *refs
+    fresh, last, acts_ref, acts_other_ref, own_ref, other_ref, gain_ref, slopes_ref, weight_ref, *refs
 ):
-    weight_refs, (cotangent_ref, straight_ref, crossed_ref, pre_grad) = refs[:-4], refs[-4:]
+    cotangent_ref, straight_ref, crossed_ref, pre_grad = refs
     half = gain_ref.shape[1]
     second_grad, first_grad = pair_state(fresh, own_ref, other_ref, half)
     tokens = first_grad.shape[0]
@@ -174,18 +145,18 @@
         first_grad = coupling_scale * first_grad
     cotangent = second_grad.astype(jnp.bfloat16)
     cotangent_ref[...] = cotangent
-    for span, weight_ref in spans(weight_refs):
+    for span, part_ref in spans(weight_ref):
         hidden_grad = lax.dot_general(
             cotangent,
-            weight_ref[:, half:],
+            part_ref[:, half:],
             (((1,), (1,)), ((), ())),
             preferred_element_type=jnp.float32,
         )
         slopes = slopes_ref[:, span].astype(jnp.float32)
         pre_grad[:, span] = (hidden_grad * slopes).astype(jnp.bfloat16)
     norm_grad = sum(
-        jnp.dot(pre_grad[:, span], weight_ref[:, :half], preferred_element_type=jnp.float32)
-        for span, weight_ref in spans(weight_refs)
+        jnp.dot(pre_grad[:, span], part_ref[:, :half], preferred_element_type=jnp.float32)
+        for span, part_ref in spans(weight_ref)
     )
     first, _ = pair_state(fresh, acts_ref, acts_other_ref, 0)
     inv_rms = inverse_rms(first)
@@ -212,23 +183,21 @@
     out_ref[:, half:] = second
 
 
-def outer_kernel(start, *refs):
+def outer_kernel(*refs):
     ticks = len(refs) // 2
     hidden_refs, cotangent_refs, out_ref = refs[:ticks], refs[ticks:-1], refs[-1]
-    count = out_ref.shape[0]
-    rows = jnp.concatenate([ref[:, start : start + count] for ref in hidden_refs], axis=0)
     cotangents = jnp.concatenate([ref[...] for ref in cotangent_refs], axis=0)
-    total = lax.dot_general(
-        rows, cotangents, (((0,), (0,)), ((), ())), preferred_element_type=jnp.float32
-    )
-    out_ref[...] = total.astype(out_ref.dtype)
-
-
-def spans(weight_refs):
-    offset = 0
-    for ref in weight_refs:
-        yield pl.ds(offset, ref.shape[0]), ref
-        offset += ref.shape[0]
+    for start in range(0, out_ref.shape[0], chunk):
+        rows = jnp.concatenate([ref[:, start : start + chunk] for ref in hidden_refs], axis=0)
+        total = lax.dot_general(
+            rows, cotangents, (((0,), (0,)), ((), ())), preferred_element_type=jnp.float32
+        )
+        out_ref[start : start + chunk] = total.astype(out_ref.dtype)
+
+
+def spans(weight_ref):
+    for start in range(0, weight_ref.shape[0], chunk):
+        yield pl.ds(start, chunk), weight_ref.at[pl.ds(start, chunk)]
 
 
 def in_vmem(count):
@@ -269,7 +238,7 @@
 
 def forward(fresh, last, tokens, acts, gain, weights):
     half = gain.shape[1]
-    units = sum(w.shape[0] for w in weights)
+    units = weights.shape[0]
     return call(
         functools.partial(forward_kernel, fresh, last),
         cost(2 * tokens, units, half),
@@ -278,7 +247,7 @@
             ((2 * tokens, units), jnp.bfloat16),
             *addend_shapes(last, tokens, half),
         ),
-        (*acts, gain, *weights),
+        (*acts, gain, weights),
     )
 
 
@@ -289,7 +258,7 @@
         functools.partial(backward_kernel, fresh, last),
         cost(2 * tokens, units, half),
         (((2 * tokens, half), jnp.bfloat16), *addend_shapes(last, tokens, half)),
-        (*acts, *grads, gain, slopes, *weights),
+        (*acts, *grads, gain, slopes, weights),
         (pltpu.VMEM((2 * tokens, units), jnp.bfloat16),),
     )
 
@@ -317,17 +286,13 @@
     )[0]
 
 
-def outer_rows(hiddens, cotangents, start, count):
+def outer_product(hiddens, cotangents):
     half = cotangents[0].shape[1]
-    tokens = hiddens[0].shape[0] * len(hiddens)
-    return call(
-        functools.partial(outer_kernel, start),
-        pl.CostEstimate(
-            flops=2 * tokens * count * half,
-            bytes_accessed=2 * (tokens * count + tokens * half + count * half),
-            transcendentals=0,
-        ),
-        (((count, half), jnp.bfloat16),),
+    tokens, units = hiddens[0].shape
+    return call(
+        outer_kernel,
+        cost(len(hiddens) * tokens, units, half // 2),
+        (((units, half), jnp.bfloat16),),
         (*hiddens, *cotangents),
     )[0]
 
@@ -344,8 +309,7 @@
     tick_count = min(4, lax.axis_size("section") // 2)
     shard = jnp.concatenate([in_proj[0], out_proj[0]], axis=1)
     group_size = len(alike_groups()[0])
-    weights = gathered_along_x(exchanged(jnp.tile(shard, (group_size, 1))))
-    quarter = group_size * units
+    weights = exchanged(jnp.tile(shard, (group_size, 1)))
 
     acts_pair = (acts[0], swapped_with_partner(acts[0, :, :half]))
     grads_pair = (grads[0], swapped_with_partner(grads[0, :, half:].astype(jnp.bfloat16)))
@@ -358,22 +322,12 @@
         if last:
             grads_pair, hidden, addends = lax.optimization_barrier((grads_pair, hidden, addends))
             cotangents.append(cotangent_of(grads_pair))
-            outer = functools.partial(outer_rows, hiddens, cotangents, count=quarter)
-            parts = [outer(i * quarter) for i in (3, 1, 2)]
-            from_far = swapped_along_x(parts[0], far_x)
-            from_near = swapped_along_x(parts[1], near_x)
-            from_next = swapped_along_x(parts[2], next_x)
-            slopes, _ = lax.optimization_barrier((slopes, parts))
+            blocks = outer_product(hiddens, cotangents)
+            parts = exchanged(blocks).reshape(-1, units, half)
         cotangent, *addends = backward(
             fresh, last, tokens, acts_pair, grads_pair, gain, slopes, weights
         )
-        if last:
-            own = outer(0)
-            blocks = sum(
-                x.astype(jnp.float32) for x in (own, from_near, from_next, from_far)
-            ).astype(jnp.bfloat16)
-            parts = exchanged(blocks).reshape(-1, units, half)
-        else:
+        if not last:
             cotangents.append(cotangent)
         next_grads = sent_back(*addends)
         acts_pair, grads_pair = next_acts, next_grads

time: 177 us -> 208 us (1.18)
  the two profiles are of different devices: /device:TPU:48 before, /device:TPU:16 now
where the time goes in v2:
time: 208 us; the launch traced here: 207 us
  waiting for transfers between devices  122 us (59%)
  starting transfers between devices  64.4 us (31%)
  Pallas kernels  11.9 us (6%)
  local copies, waits for them, and re-layouts  4.85 us (2%)
  other arithmetic  2.79 us (1%)
    all_to_all x2, waiting for transfers between devices, exchanged(): lax.all_to_all(blocks, 'dp', 0, 0, axis_index_groups=alike_groups(), tile...  44 us
    ppermute x8, waiting for transfers between devices, passed_back_to_partner(): return lax.ppermute(block, ('section', 'dp'), route)  42.6 us
    ppermute x2, waiting for transfers between devices, swapped_with_partner(): lax.ppermute(block, 'dp', [(partner(i), i) for i in range(lax.axis_size('...  35.1 us
    all_to_all x2, starting transfers between devices, exchanged(): lax.all_to_all(blocks, 'dp', 0, 0, axis_index_groups=alike_groups(), tile...  23.7 us
    ppermute x8, starting transfers between devices, passed_back_to_partner(): return lax.ppermute(block, ('section', 'dp'), route)  19.5 us
    ppermute x8, starting transfers between devices, passed_back(): return lax.ppermute(block, 'section', [(i, i - 1) for i in devices if i])  15.4 us
    pallas_call x12, Pallas kernels, call(): pl.pallas_call(kernel, out_shape=tuple((jax.ShapeDtypeStruct(shape, dtype...  11.9 us
    ppermute x2, starting transfers between devices, swapped_with_partner(): lax.ppermute(block, 'dp', [(partner(i), i) for i in range(lax.axis_size('...  5.83 us
  transfers between devices with their start and end apart: 20, of which 10 were waited for; matrix products, arithmetic and copies ran while one was open for 0% of the time, Pallas kernels for 5%

profile of v2, /device:TPU:16, one launch (start us, length us, event | category | flops | bytes accessed | tf_op | source)
XLA Modules:
  0.0 206.7 jit_solution(9501583275381037083)
XLA Ops:
  3.0 16.8 %all-to-all-start = ((bf16[32,32,1024]{2,1,0:T(8,128)(2,1)}), bf16[32,32,1024]{2,1,0:T(8,128)(2,1)S(1)}, u32[]{:S(2)}, u32[]{:S(2)}) async-start(bf16[32,32,1024]{2,1,0:T(8,128)(2,1)} %tile.2), calls=%async_computation | async-start | bytes 4194304 | tf_op jit(solution)/shard_map/all_to_all | solution.py:50
  19.8 3.4 %collective-permute-start = (f32[128,512]{1,0:T(8,128)S(1)}, f32[128,512]{1,0:T(8,128)S(1)}, u32[]{:S(2)}, u32[]{:S(2)}) collective-permute-start(f32[128,512]{1,0:T(8,128)S(1)} %slice_bitcast_fusion), channel_id=1, source_target_pairs={{8,0},{9,1},{10,2},{11,3},{12,4},{13,5},{14,6},{15,7},{0,8},{1,9},... | collective-permute-start | bytes 786440 | tf_op jit(solution)/shard_map/ppermute | solution.py:46
  23.9 2.4 %collective-permute-start.9 = (bf16[128,512]{1,0:T(8,128)(2,1)}, bf16[128,512]{1,0:T(8,128)(2,1)S(1)}, u32[]{:S(2)}, u32[]{:S(2)}) collective-permute-start(bf16[128,512]{1,0:T(8,128)(2,1)} %fusion), channel_id=1, source_target_pairs={{8,0},{9,1},{10,2},{11,3},{12,4},{13,5},{14,6},{15,7},{0,8},{1,9},... | collective-permute-start | bytes 393224 | tf_op jit(solution)/shard_map/ppermute | solution.py:46
  26.4 35.1 %collective-permute-done.other_ref.acts_other_ref = f32[128,512]{1,0:T(8,128)S(1)} collective-permute-done((f32[128,512]{1,0:T(8,128)S(1)}, f32[128,512]{1,0:T(8,128)S(1)}, u32[]{:S(2)}, u32[]{:S(2)}) %collective-permute-start) | collective-permute-done | bytes 262176 | tf_op jit(solution)/shard_map/ppermute | solution.py:46
  61.5 33.3 %all-to-all-done = bf16[32,32,1024]{2,1,0:T(8,128)(2,1)S(1)} async-done(((bf16[32,32,1024]{2,1,0:T(8,128)(2,1)}), bf16[32,32,1024]{2,1,0:T(8,128)(2,1)S(1)}, u32[]{:S(2)}, u32[]{:S(2)}) %all-to-all-start) | async-done | bytes 2097184 | tf_op jit(solution)/shard_map/all_to_all | solution.py:50
  95.9 1.9 collective-permute-start.1
  98.7 1.9 collective-permute-start.10
  100.6 1.9 collective-permute-start.2
  102.6 1.9 collective-permute-start.11
  104.5 5.6 %collective-permute-done.2.other_ref.acts_other_ref = bf16[256,512]{1,0:T(8,128)(2,1)S(1)} collective-permute-done((bf16[256,512]{1,0:T(8,128)(2,1)S(1)}, bf16[256,512]{1,0:T(8,128)(2,1)S(1)}, u32[]{:S(2)}, u32[]{:S(2)}) %collective-permute-start.2) | collective-permute-done | bytes 262176 | tf_op jit(solution)/shard_map/ppermute | solution.py:67
  111.3 1.9 collective-permute-start.3
  116.0 4.7 %collective-permute-start.4 = (bf16[256,512]{1,0:T(8,128)(2,1)S(1)}, bf16[256,512]{1,0:T(8,128)(2,1)S(1)}, u32[]{:S(2)}, u32[]{:S(2)}) collective-permute-start(bf16[256,512]{1,0:T(8,128)(2,1)S(1)} %get-tuple-element.35), channel_id=1, source_target_pairs={{64,8},{65,9},{66,10},{67,11},{68,12},{69,13},{70,14},{71,15},{72,... | collective-permute-start | bytes 786440 | tf_op jit(solution)/shard_map/ppermute | solution.py:67
  120.7 2.2 %collective-permute-start.13 = (bf16[256,512]{1,0:T(8,128)(2,1)S(1)}, bf16[256,512]{1,0:T(8,128)(2,1)S(1)}, u32[]{:S(2)}, u32[]{:S(2)}) collective-permute-start(bf16[256,512]{1,0:T(8,128)(2,1)S(1)} %get-tuple-element.45), channel_id=1, source_target_pairs={{64,8},{65,9},{66,10},{67,11},{68,12},{69,13},{70,14},{71,15},{72,... | collective-permute-start | bytes 786440 | tf_op jit(solution)/shard_map/ppermute | solution.py:67
  123.0 8.3 %collective-permute-done.4.other_ref.acts_other_ref = bf16[256,512]{1,0:T(8,128)(2,1)S(1)} collective-permute-done((bf16[256,512]{1,0:T(8,128)(2,1)S(1)}, bf16[256,512]{1,0:T(8,128)(2,1)S(1)}, u32[]{:S(2)}, u32[]{:S(2)}) %collective-permute-start.4) | collective-permute-done | bytes 262176 | tf_op jit(solution)/shard_map/ppermute | solution.py:67
  132.4 1.9 collective-permute-start.5
  134.3 5.4 %collective-permute-done.13.other_ref = bf16[256,512]{1,0:T(8,128)(2,1)S(1)} collective-permute-done((bf16[256,512]{1,0:T(8,128)(2,1)S(1)}, bf16[256,512]{1,0:T(8,128)(2,1)S(1)}, u32[]{:S(2)}, u32[]{:S(2)}) %collective-permute-start.13) | collective-permute-done | bytes 262176 | tf_op jit(solution)/shard_map/ppermute | solution.py:67
  146.4 9.5 %collective-permute-done.6.other_ref.acts_other_ref = bf16[256,512]{1,0:T(8,128)(2,1)S(1)} collective-permute-done((bf16[256,512]{1,0:T(8,128)(2,1)S(1)}, bf16[256,512]{1,0:T(8,128)(2,1)S(1)}, u32[]{:S(2)}, u32[]{:S(2)}) %collective-permute-start.6) | collective-permute-done | bytes 262176 | tf_op jit(solution)/shard_map/ppermute | solution.py:67
  158.7 2.3 %shard_map.87 = bf16[1024,512]{1,0:T(8,128)(2,1)} custom-call(bf16[256,1024]{1,0:T(8,128)(2,1)S(1)} %get-tuple-element.55.refs_0_, bf16[256,1024]{1,0:T(8,128)(2,1)S(1)} %get-tuple-element.56.refs_1_, bf16[256,1024]{1,0:T(8,128)(2,1)S(1)} %get-tuple-element.57.refs_2_, bf16[256,1024]{1,0:T(8,128)(2,1)S(1)} %get-tuple-element.49.refs_3_, ...), custom_call_target="tpu_custom_call" | custom-call | flops 1073741824 | bytes 5242880 | tf_op jit(solution)/shard_map/pallas_call | solution.py:220
  161.0 7.0 %all-to-all-start.1 = ((bf16[32,32,512]{2,1,0:T(8,128)(2,1)}), bf16[32,32,512]{2,1,0:T(8,128)(2,1)}, u32[]{:S(2)}, u32[]{:S(2)}) async-start(bf16[32,32,512]{2,1,0:T(8,128)(2,1)} %bitcast.9), calls=%async_computation.1 | async-start | bytes 2097152 | tf_op jit(solution)/shard_map/all_to_all | solution.py:50
  169.8 1.9 collective-permute-start.16
  175.6 3.0 %collective-permute-start.8 = (bf16[128,512]{1,0:T(8,128)(2,1)S(1)}, bf16[128,512]{1,0:T(8,128)(2,1)S(1)}, u32[]{:S(2)}, u32[]{:S(2)}) collective-permute-start(bf16[128,512]{1,0:T(8,128)(2,1)S(1)} %get-tuple-element.39), channel_id=1, source_target_pairs={{64,8},{65,9},{66,10},{67,11},{68,12},{69,13},{70,14},{71,15},{72,... | collective-permute-start | bytes 393224 | tf_op jit(solution)/shard_map/ppermute | solution.py:67
  178.6 12.4 %collective-permute-done.17.crossed_ref = bf16[128,512]{1,0:T(8,128)(2,1)S(1)} collective-permute-done((bf16[128,512]{1,0:T(8,128)(2,1)S(1)}, bf16[128,512]{1,0:T(8,128)(2,1)S(1)}, u32[]{:S(2)}, u32[]{:S(2)}) %collective-permute-start.17) | collective-permute-done | bytes 131104 | tf_op jit(solution)/shard_map/ppermute | solution.py:67
  194.0 10.7 %all-to-all-done.1 = bf16[32,32,512]{2,1,0:T(8,128)(2,1)} async-done(((bf16[32,32,512]{2,1,0:T(8,128)(2,1)}), bf16[32,32,512]{2,1,0:T(8,128)(2,1)}, u32[]{:S(2)}, u32[]{:S(2)}) %all-to-all-start.1) | async-done | bytes 1048608 | tf_op jit(solution)/shard_map/all_to_all | solution.py:50
  204.7 2.0 convert_reduce_fusion
  (47 shorter events, 28.3 us)
Async XLA Ops:
  3.0 16.8 %copy-start = (f32[1,128,1024]{2,1,0:T(8,128)S(1)}, f32[1,128,1024]{2,1,0:T(8,128)}, u32[]{:S(2)}) copy-start(f32[1,128,1024]{2,1,0:T(8,128)} %param.5) | copy-start | bytes 1572868
  3.0 20.2 %copy-start.1 = (f32[1,128,1024]{2,1,0:T(8,128)S(1)}, f32[1,128,1024]{2,1,0:T(8,128)}, u32[]{:S(2)}) copy-start(f32[1,128,1024]{2,1,0:T(8,128)} %param.6) | copy-start | bytes 1572868
  3.0 91.8 %copy-start.4 = (f32[1,512]{1,0:T(1,128)S(1)}, f32[1,512]{1,0:T(1,128)}, u32[]{:S(2)}) copy-start(f32[1,512]{1,0:T(1,128)} %gain_ref.15) | copy-start | bytes 6148
  3.0 91.8 %all-to-all-start = ((bf16[32,32,1024]{2,1,0:T(8,128)(2,1)}), bf16[32,32,1024]{2,1,0:T(8,128)(2,1)S(1)}, u32[]{:S(2)}, u32[]{:S(2)}) async-start(bf16[32,32,1024]{2,1,0:T(8,128)(2,1)} %tile.2), calls=%async_computation | async-start | bytes 4194304 | tf_op jit(solution)/shard_map/all_to_all | solution.py:50
  19.8 41.7 %collective-permute-start = (f32[128,512]{1,0:T(8,128)S(1)}, f32[128,512]{1,0:T(8,128)S(1)}, u32[]{:S(2)}, u32[]{:S(2)}) collective-permute-start(f32[128,512]{1,0:T(8,128)S(1)} %slice_bitcast_fusion), channel_id=1, source_target_pairs={{8,0},{9,1},{10,2},{11,3},{12,4},{13,5},{14,6},{15,7},{0,8},{1,9},... | collective-permute-start | bytes 786440 | tf_op jit(solution)/shard_map/ppermute | solution.py:46
  23.9 73.9 %collective-permute-start.9 = (bf16[128,512]{1,0:T(8,128)(2,1)}, bf16[128,512]{1,0:T(8,128)(2,1)S(1)}, u32[]{:S(2)}, u32[]{:S(2)}) collective-permute-start(bf16[128,512]{1,0:T(8,128)(2,1)} %fusion), channel_id=1, source_target_pairs={{8,0},{9,1},{10,2},{11,3},{12,4},{13,5},{14,6},{15,7},{0,8},{1,9},... | collective-permute-start | bytes 393224 | tf_op jit(solution)/shard_map/ppermute | solution.py:46
  95.9 14.2 %collective-permute-start.1 = (bf16[384,512]{1,0:T(8,128)(2,1)S(1)}, bf16[384,512]{1,0:T(8,128)(2,1)S(1)}, u32[]{:S(2)}, u32[]{:S(2)}) collective-permute-start(bf16[384,512]{1,0:T(8,128)(2,1)S(1)} %get-tuple-element.32), channel_id=1, source_target_pairs={{64,0},{128,64},{192,128},{256,192},{320,256},{384,320},{448,384},... | collective-permute-start | bytes 1179656 | tf_op jit(solution)/shard_map/ppermute | solution.py:57
  98.7 14.5 %collective-permute-start.10 = (bf16[384,512]{1,0:T(8,128)(2,1)S(1)}, bf16[384,512]{1,0:T(8,128)(2,1)S(1)}, u32[]{:S(2)}, u32[]{:S(2)}) collective-permute-start(bf16[384,512]{1,0:T(8,128)(2,1)S(1)} %get-tuple-element.41), channel_id=1, source_target_pairs={{64,0},{128,64},{192,128},{256,192},{320,256},{384,320},{448,384},... | collective-permute-start | bytes 1179656 | tf_op jit(solution)/shard_map/ppermute | solution.py:57
  100.6 9.5 %collective-permute-start.2 = (bf16[256,512]{1,0:T(8,128)(2,1)S(1)}, bf16[256,512]{1,0:T(8,128)(2,1)S(1)}, u32[]{:S(2)}, u32[]{:S(2)}) collective-permute-start(bf16[256,512]{1,0:T(8,128)(2,1)S(1)} %get-tuple-element.33), channel_id=1, source_target_pairs={{64,8},{65,9},{66,10},{67,11},{68,12},{69,13},{70,14},{71,15},{72,... | collective-permute-start | bytes 786440 | tf_op jit(solution)/shard_map/ppermute | solution.py:67
  102.6 10.6 %collective-permute-start.11 = (bf16[256,512]{1,0:T(8,128)(2,1)S(1)}, bf16[256,512]{1,0:T(8,128)(2,1)S(1)}, u32[]{:S(2)}, u32[]{:S(2)}) collective-permute-start(bf16[256,512]{1,0:T(8,128)(2,1)S(1)} %get-tuple-element.42), channel_id=1, source_target_pairs={{64,8},{65,9},{66,10},{67,11},{68,12},{69,13},{70,14},{71,15},{72,... | collective-permute-start | bytes 786440 | tf_op jit(solution)/shard_map/ppermute | solution.py:67
  111.3 20.0 %collective-permute-start.3 = (bf16[384,512]{1,0:T(8,128)(2,1)S(1)}, bf16[384,512]{1,0:T(8,128)(2,1)S(1)}, u32[]{:S(2)}, u32[]{:S(2)}) collective-permute-start(bf16[384,512]{1,0:T(8,128)(2,1)S(1)} %get-tuple-element.34), channel_id=1, source_target_pairs={{64,0},{128,64},{192,128},{256,192},{320,256},{384,320},{448,384},... | collective-permute-start | bytes 1179656 | tf_op jit(solution)/shard_map/ppermute | solution.py:57
  114.1 25.6 %collective-permute-start.12 = (bf16[384,512]{1,0:T(8,128)(2,1)S(1)}, bf16[384,512]{1,0:T(8,128)(2,1)S(1)}, u32[]{:S(2)}, u32[]{:S(2)}) collective-permute-start(bf16[384,512]{1,0:T(8,128)(2,1)S(1)} %get-tuple-element.44), channel_id=1, source_target_pairs={{64,0},{128,64},{192,128},{256,192},{320,256},{384,320},{448,384},... | collective-permute-start | bytes 1179656 | tf_op jit(solution)/shard_map/ppermute | solution.py:57
  116.0 15.3 %collective-permute-start.4 = (bf16[256,512]{1,0:T(8,128)(2,1)S(1)}, bf16[256,512]{1,0:T(8,128)(2,1)S(1)}, u32[]{:S(2)}, u32[]{:S(2)}) collective-permute-start(bf16[256,512]{1,0:T(8,128)(2,1)S(1)} %get-tuple-element.35), channel_id=1, source_target_pairs={{64,8},{65,9},{66,10},{67,11},{68,12},{69,13},{70,14},{71,15},{72,... | collective-permute-start | bytes 786440 | tf_op jit(solution)/shard_map/ppermute | solution.py:67
  120.7 19.0 %collective-permute-start.13 = (bf16[256,512]{1,0:T(8,128)(2,1)S(1)}, bf16[256,512]{1,0:T(8,128)(2,1)S(1)}, u32[]{:S(2)}, u32[]{:S(2)}) collective-permute-start(bf16[256,512]{1,0:T(8,128)(2,1)S(1)} %get-tuple-element.45), channel_id=1, source_target_pairs={{64,8},{65,9},{66,10},{67,11},{68,12},{69,13},{70,14},{71,15},{72,... | collective-permute-start | bytes 786440 | tf_op jit(solution)/shard_map/ppermute | solution.py:67
  132.4 23.4 %collective-permute-start.5 = (bf16[384,512]{1,0:T(8,128)(2,1)S(1)}, bf16[384,512]{1,0:T(8,128)(2,1)S(1)}, u32[]{:S(2)}, u32[]{:S(2)}) collective-permute-start(bf16[384,512]{1,0:T(8,128)(2,1)S(1)} %get-tuple-element.36), channel_id=1, source_target_pairs={{64,0},{128,64},{192,128},{256,192},{320,256},{384,320},{448,384},... | collective-permute-start | bytes 1179656 | tf_op jit(solution)/shard_map/ppermute | solution.py:57
  140.6 18.0 %collective-permute-start.14 = (bf16[384,512]{1,0:T(8,128)(2,1)S(1)}, bf16[384,512]{1,0:T(8,128)(2,1)S(1)}, u32[]{:S(2)}, u32[]{:S(2)}) collective-permute-start(bf16[384,512]{1,0:T(8,128)(2,1)S(1)} %get-tuple-element.47), channel_id=1, source_target_pairs={{64,0},{128,64},{192,128},{256,192},{320,256},{384,320},{448,384},... | collective-permute-start | bytes 1179656 | tf_op jit(solution)/shard_map/ppermute | solution.py:57
  142.5 13.3 %collective-permute-start.6 = (bf16[256,512]{1,0:T(8,128)(2,1)S(1)}, bf16[256,512]{1,0:T(8,128)(2,1)S(1)}, u32[]{:S(2)}, u32[]{:S(2)}) collective-permute-start(bf16[256,512]{1,0:T(8,128)(2,1)S(1)} %get-tuple-element.37), channel_id=1, source_target_pairs={{64,8},{65,9},{66,10},{67,11},{68,12},{69,13},{70,14},{71,15},{72,... | collective-permute-start | bytes 786440 | tf_op jit(solution)/shard_map/ppermute | solution.py:67
  144.4 14.2 %collective-permute-start.15 = (bf16[256,512]{1,0:T(8,128)(2,1)S(1)}, bf16[256,512]{1,0:T(8,128)(2,1)S(1)}, u32[]{:S(2)}, u32[]{:S(2)}) collective-permute-start(bf16[256,512]{1,0:T(8,128)(2,1)S(1)} %get-tuple-element.48), channel_id=1, source_target_pairs={{64,8},{65,9},{66,10},{67,11},{68,12},{69,13},{70,14},{71,15},{72,... | collective-permute-start | bytes 786440 | tf_op jit(solution)/shard_map/ppermute | solution.py:67
  161.0 43.7 %all-to-all-start.1 = ((bf16[32,32,512]{2,1,0:T(8,128)(2,1)}), bf16[32,32,512]{2,1,0:T(8,128)(2,1)}, u32[]{:S(2)}, u32[]{:S(2)}) async-start(bf16[32,32,512]{2,1,0:T(8,128)(2,1)} %bitcast.9), calls=%async_computation.1 | async-start | bytes 2097152 | tf_op jit(solution)/shard_map/all_to_all | solution.py:50
  169.0 2.8 %copy-start.6 = (bf16[256,512]{1,0:T(8,128)(2,1)S(1)}, bf16[256,512]{1,0:T(8,128)(2,1)}, u32[]{:S(2)}) copy-start(bf16[256,512]{1,0:T(8,128)(2,1)} %copy-done.5) | copy-start | bytes 786436
  169.8 21.2 %collective-permute-start.16 = (bf16[256,512]{1,0:T(8,128)(2,1)S(1)}, bf16[256,512]{1,0:T(8,128)(2,1)S(1)}, u32[]{:S(2)}, u32[]{:S(2)}) collective-permute-start(bf16[256,512]{1,0:T(8,128)(2,1)S(1)} %get-tuple-element.53), channel_id=1, source_target_pairs={{64,0},{128,64},{192,128},{256,192},{320,256},{384,320},{448,384},... | collective-permute-start | bytes 786440 | tf_op jit(solution)/shard_map/ppermute | solution.py:57
  171.8 21.4 %collective-permute-start.7 = (bf16[256,512]{1,0:T(8,128)(2,1)S(1)}, bf16[256,512]{1,0:T(8,128)(2,1)S(1)}, u32[]{:S(2)}, u32[]{:S(2)}) collective-permute-start(bf16[256,512]{1,0:T(8,128)(2,1)S(1)} %copy-done.6), channel_id=1, source_target_pairs={{64,0},{128,64},{192,128},{256,192},{320,256},{384,320},{448,384},... | collective-permute-start | bytes 786440 | tf_op jit(solution)/shard_map/ppermute | solution.py:57
  173.7 17.4 %collective-permute-start.17 = (bf16[128,512]{1,0:T(8,128)(2,1)S(1)}, bf16[128,512]{1,0:T(8,128)(2,1)S(1)}, u32[]{:S(2)}, u32[]{:S(2)}) collective-permute-start(bf16[128,512]{1,0:T(8,128)(2,1)S(1)} %get-tuple-element.54), channel_id=1, source_target_pairs={{64,8},{65,9},{66,10},{67,11},{68,12},{69,13},{70,14},{71,15},{72,... | collective-permute-start | bytes 393224 | tf_op jit(solution)/shard_map/ppermute | solution.py:67
  175.6 17.5 %collective-permute-start.8 = (bf16[128,512]{1,0:T(8,128)(2,1)S(1)}, bf16[128,512]{1,0:T(8,128)(2,1)S(1)}, u32[]{:S(2)}, u32[]{:S(2)}) collective-permute-start(bf16[128,512]{1,0:T(8,128)(2,1)S(1)} %get-tuple-element.39), channel_id=1, source_target_pairs={{64,8},{65,9},{66,10},{67,11},{68,12},{69,13},{70,14},{71,15},{72,... | collective-permute-start | bytes 393224 | tf_op jit(solution)/shard_map/ppermute | solution.py:67
  (3 other events, 2.5 us)

commit v3 on v1

--- a/solution.py
+++ b/solution.py
@@ -100,6 +100,14 @@
     return lax.rsqrt(jnp.mean(first * first, axis=-1, keepdims=True) + rms_epsilon)
 
 
+def split(counts, refs):
+    parts, start = [], 0
+    for count in counts:
+        parts.append(refs[start : start + count])
+        start += count
+    return *parts, refs[start:]
+
+
 def pair_sums(straight, crossed):
     tokens = crossed.shape[0] // 2
     straight, crossed = straight.astype(jnp.float32), crossed.astype(jnp.float32)
@@ -108,9 +116,10 @@
     )
 
 
-def pair_state(fresh, own_ref, other_ref, current):
+def pair_state(fresh, current, waiting_at, state_refs):
+    own_ref, other_ref = state_refs[:2]
     if fresh:
-        half = other_ref.shape[1]
+        _, half = other_ref.shape
         waiting = half - current
         both = jnp.concatenate(
             [
@@ -121,26 +130,35 @@
         )
         return both, own_ref[:, waiting : waiting + half]
     rows = other_ref.shape[0]
-    return pair_sums(own_ref[:rows], other_ref[...]), own_ref[rows:].astype(jnp.float32)
-
-
-def put_addends(last, straight_ref, crossed_ref, own, other, kept):
+    both = pair_sums(own_ref[:rows], other_ref[...])
+    if waiting_at is None:
+        return both, None
+    if len(state_refs) == 3:
+        start = waiting_at * (rows // 2)
+        waiting = state_refs[2][start : start + rows // 2]
+    else:
+        waiting = own_ref[rows:]
+    return both, waiting.astype(jnp.float32)
+
+
+def put_addends(last, refs, own, other, kept):
     tokens = own.shape[0]
-    dtype = straight_ref.dtype
+    straight_ref, dtype = refs[0], refs[0].dtype
     straight_ref[:tokens] = own.astype(dtype)
     if last:
-        crossed_ref[...] = other.astype(dtype)
+        refs[1][...] = other.astype(dtype)
         straight_ref[tokens:] = kept.astype(dtype)
-    else:
-        straight_ref[tokens : 2 * tokens] = other.astype(dtype)
+        return
+    straight_ref[tokens : 2 * tokens] = other.astype(dtype)
+    if len(refs) == 2:
         straight_ref[2 * tokens :] = kept.astype(dtype)
-        crossed_ref[:tokens] = own.astype(dtype)
-        crossed_ref[tokens:] = other.astype(dtype)
-
-
-def forward_kernel(fresh, last, own_ref, other_ref, gain_ref, *refs):
-    weight_refs, (hidden_ref, slopes_ref, straight_ref, crossed_ref) = refs[:-4], refs[-4:]
-    first, second = pair_state(fresh, own_ref, other_ref, 0)
+        refs[1][:tokens] = own.astype(dtype)
+        refs[1][tokens:] = other.astype(dtype)
+
+
+def forward_kernel(fresh, last, counts, *refs):
+    state_refs, (gain_ref,), weight_refs, (hidden_ref, slopes_ref, *addend_refs) = split(counts, refs)
+    first, second = pair_state(fresh, 0, 0, state_refs)
     tokens, half = second.shape
     normed = (first * inverse_rms(first) * gain_ref[...]).astype(jnp.bfloat16)
     for span, weight_ref in spans(weight_refs):
@@ -160,15 +178,14 @@
     )
     own = (second - branch[:tokens]) / coupling_scale
     other = (0.0 - branch[tokens:]) / coupling_scale
-    put_addends(last, straight_ref, crossed_ref, own, other, first[:tokens])
-
-
-def backward_kernel(
-    fresh, last, acts_ref, acts_other_ref, own_ref, other_ref, gain_ref, slopes_ref, *refs
-):
-    weight_refs, (cotangent_ref, straight_ref, crossed_ref, pre_grad) = refs[:-4], refs[-4:]
+    put_addends(last, addend_refs, own, other, first[:tokens])
+
+
+def backward_kernel(fresh, last, counts, *refs):
+    acts_refs, state_refs, (gain_ref, slopes_ref), weight_refs, outs = split(counts, refs)
+    cotangent_ref, *addend_refs, pre_grad = outs
     half = gain_ref.shape[1]
-    second_grad, first_grad = pair_state(fresh, own_ref, other_ref, half)
+    second_grad, first_grad = pair_state(fresh, half, 1, state_refs)
     tokens = first_grad.shape[0]
     if not fresh:
         first_grad = coupling_scale * first_grad
@@ -187,13 +204,13 @@
         jnp.dot(pre_grad[:, span], weight_ref[:, :half], preferred_element_type=jnp.float32)
         for span, weight_ref in spans(weight_refs)
     )
-    first, _ = pair_state(fresh, acts_ref, acts_other_ref, 0)
+    first = pair_state(fresh, 0, None, acts_refs)[0]
     inv_rms = inverse_rms(first)
     scaled = norm_grad * gain_ref[...]
     inner = jnp.mean(first * scaled, axis=-1, keepdims=True)
     input_grad = inv_rms * scaled - first * (inv_rms * inv_rms * inv_rms) * inner
     own = first_grad + input_grad[:tokens]
-    put_addends(last, straight_ref, crossed_ref, own, input_grad[tokens:], cotangent[:tokens])
+    put_addends(last, addend_refs, own, input_grad[tokens:], cotangent[:tokens])
 
 
 def cotangent_kernel(own_ref, other_ref, out_ref):
@@ -259,7 +276,9 @@
     )(*operands)
 
 
-def addend_shapes(last, tokens, half):
+def addend_shapes(fresh, last, tokens, half):
+    if fresh:
+        return (((2 * tokens, half), jnp.bfloat16),)
     straight, crossed = (2, 1) if last else (3, 2)
     return (
         ((straight * tokens, half), jnp.bfloat16),
@@ -271,12 +290,12 @@
     half = gain.shape[1]
     units = sum(w.shape[0] for w in weights)
     return call(
-        functools.partial(forward_kernel, fresh, last),
+        functools.partial(forward_kernel, fresh, last, (len(acts), 1, len(weights))),
         cost(2 * tokens, units, half),
         (
             ((2 * tokens, units), jnp.bfloat16),
             ((2 * tokens, units), jnp.bfloat16),
-            *addend_shapes(last, tokens, half),
+            *addend_shapes(fresh, last, tokens, half),
         ),
         (*acts, gain, *weights),
     )
@@ -285,10 +304,11 @@
 def backward(fresh, last, tokens, acts, grads, gain, slopes, weights):
     half = gain.shape[1]
     units = slopes.shape[1]
+    counts = (len(acts), len(grads), 2, len(weights))
     return call(
-        functools.partial(backward_kernel, fresh, last),
+        functools.partial(backward_kernel, fresh, last, counts),
         cost(2 * tokens, units, half),
-        (((2 * tokens, half), jnp.bfloat16), *addend_shapes(last, tokens, half)),
+        (((2 * tokens, half), jnp.bfloat16), *addend_shapes(fresh, last, tokens, half)),
         (*acts, *grads, gain, slopes, *weights),
         (pltpu.VMEM((2 * tokens, units), jnp.bfloat16),),
     )
@@ -332,7 +352,8 @@
     )[0]
 
 
-def sent_back(straight, crossed):
+def sent_back(straight, crossed=None):
+    crossed = straight if crossed is None else crossed
     crossed = passed_back_to_partner(crossed)
     straight = passed_back(straight)
     return straight, crossed
@@ -349,6 +370,9 @@
 
     acts_pair = (acts[0], swapped_with_partner(acts[0, :, :half]))
     grads_pair = (grads[0], swapped_with_partner(grads[0, :, half:].astype(jnp.bfloat16)))
+    sent_ahead = passed_back(
+        jnp.concatenate([acts[0, :, :half], grads[0, :, half:]], axis=0).astype(jnp.bfloat16)
+    )
     hiddens, cotangents = [], []
     for tick_index in range(tick_count):
         fresh, last = tick_index == 0, tick_index == tick_count - 1
@@ -367,7 +391,7 @@
             from_next = swapped_along_x(next_rows, next_x)
             slopes, _ = lax.optimization_barrier((slopes, (far_rows, near_rows, next_rows)))
         cotangent, *addends = backward(
-            fresh, last, tokens, acts_pair, grads_pair, gain, slopes, weights
+            fresh, last, tokens, acts_pair[:2], grads_pair, gain, slopes, weights
         )
         if last:
             own = outer(0)
@@ -380,6 +404,8 @@
             cotangents.append(cotangent)
         next_grads = sent_back(*addends)
         acts_pair, grads_pair = next_acts, next_grads
+        if fresh:
+            acts_pair, grads_pair = (*acts_pair, sent_ahead), (*grads_pair, sent_ahead)
 
     share = jnp.sum(parts.astype(jnp.float32), axis=0)
     acts_out = output_of(1.0, False, *acts_pair)

time: 174 us -> 169 us (0.971)
  waiting for transfers between devices: 48.9 us -> 40.4 us
  starting transfers between devices: 72.8 us -> 76.2 us
    ppermute x8, waiting for transfers between devices: 31.7 us -> 24.6 us  [passed_back_to_partner(): return lax.ppermute(block, ('section', 'dp'), route)]
    ppermute x8 -> x9, starting transfers between devices: 17.9 us -> 21.5 us  [passed_back(): return lax.ppermute(block, 'section', [(i, i - 1) for i in devices if i])]
  transfers between devices with their start and end apart: 26 -> 27, of which waited for: 10 -> 11; matrix products, arithmetic and copies ran while one was open for 0% -> 0% of each run, Pallas kernels for 8% -> 8%
where the time goes in v3:
time: 169 us; the launch traced here: 168 us
  starting transfers between devices  76.2 us (45%)
  waiting for transfers between devices  40.4 us (24%)
  blocking collectives  32.8 us (19%)
  Pallas kernels  14.7 us (9%)
  other arithmetic  2.3 us (1%)
    all_to_all x1, blocking collectives, exchanged(): lax.all_to_all(blocks, 'dp', 0, 0, axis_index_groups=alike_groups(), tile...  32.8 us
    ppermute x8, waiting for transfers between devices, passed_back_to_partner(): return lax.ppermute(block, ('section', 'dp'), route)  24.6 us
    ppermute x9, starting transfers between devices, passed_back(): return lax.ppermute(block, 'section', [(i, i - 1) for i in devices if i])  21.5 us
    ppermute x7, starting transfers between devices, swapped_along_x(): return lax.ppermute(block, 'dp', route)  20.9 us
    ppermute x8, starting transfers between devices, passed_back_to_partner(): return lax.ppermute(block, ('section', 'dp'), route)  20.1 us
    ppermute x7, waiting for transfers between devices, swapped_along_x(): return lax.ppermute(block, 'dp', route)  15.8 us
    pallas_call x15, Pallas kernels, call(): pl.pallas_call(kernel, out_shape=tuple((jax.ShapeDtypeStruct(shape, dtype...  14.7 us
    all_to_all x1, starting transfers between devices, exchanged(): lax.all_to_all(blocks, 'dp', 0, 0, axis_index_groups=alike_groups(), tile...  7.84 us
  transfers between devices with their start and end apart: 27, of which 11 were waited for; matrix products, arithmetic and copies ran while one was open for 0% of the time, Pallas kernels for 8%

profile of v3, /device:TPU:48, one launch (start us, length us, event | category | flops | bytes accessed | tf_op | source)
XLA Modules:
  0.0 167.7 jit_solution(15709891250777092293)
XLA Ops:
  1.5 32.8 %all_to_all.17 = bf16[8,32,1024]{2,1,0:T(8,128)(2,1)S(1)} all-to-all(bf16[8,32,1024]{2,1,0:T(8,128)(2,1)S(1)} %tile.2), channel_id=1, replica_groups={{0,1,16,17,32,33,48,49},{2,3,18,19,34,35,50,51},{4,5,20,21,36,37,52,53}..., dimensions={0} | all-to-all | bytes 1048576 | tf_op jit(solution)/shard_map/all_to_all | solution.py:71
  34.3 4.7 %collective-permute-start.2 = (bf16[256,1024]{1,0:T(8,128)(2,1)S(1)}, bf16[256,1024]{1,0:T(8,128)(2,1)S(1)}, u32[]{:S(2)}, u32[]{:S(2)}) collective-permute-start(bf16[256,1024]{1,0:T(8,128)(2,1)S(1)} %bitcast.15), channel_id=1, source_target_pairs={{6,0},{7,1},{4,2},{5,3},{2,4},{3,5},{0,6},{1,7},{14,8},{15,9},{12,... | collective-permute-start | bytes 1572872 | tf_op jit(solution)/shard_map/ppermute | solution.py:47
  41.1 3.0 %collective-permute-start.14 = (bf16[128,512]{1,0:T(8,128)(2,1)S(1)}, bf16[128,512]{1,0:T(8,128)(2,1)S(1)}, u32[]{:S(2)}, u32[]{:S(2)}) collective-permute-start(bf16[128,512]{1,0:T(8,128)(2,1)S(1)} %fusion), channel_id=1, source_target_pairs={{8,0},{9,1},{10,2},{11,3},{12,4},{13,5},{14,6},{15,7},{0,8},{1,9},... | collective-permute-start | bytes 393224 | tf_op jit(solution)/shard_map/ppermute | solution.py:55
  44.2 2.8 %collective-permute-start = (f32[128,512]{1,0:T(8,128)S(1)}, f32[128,512]{1,0:T(8,128)S(1)}, u32[]{:S(2)}, u32[]{:S(2)}) collective-permute-start(f32[128,512]{1,0:T(8,128)S(1)} %slice_bitcast_fusion), channel_id=1, source_target_pairs={{8,0},{9,1},{10,2},{11,3},{12,4},{13,5},{14,6},{15,7},{0,8},{1,9},... | collective-permute-start | bytes 786440 | tf_op jit(solution)/shard_map/ppermute | solution.py:55
  47.0 2.3 %collective-permute-done.2.refs_5_.refs_6_.refs_8_.refs_9_ = bf16[256,1024]{1,0:T(8,128)(2,1)S(1)} collective-permute-done((bf16[256,1024]{1,0:T(8,128)(2,1)S(1)}, bf16[256,1024]{1,0:T(8,128)(2,1)S(1)}, u32[]{:S(2)}, u32[]{:S(2)}) %collective-permute-start.2) | collective-permute-done | bytes 524320 | tf_op jit(solution)/shard_map/ppermute | solution.py:47
  51.6 2.3 %collective-permute-done.1.refs_4_.refs_5_.refs_7_.refs_8_ = bf16[256,1024]{1,0:T(8,128)(2,1)S(1)} collective-permute-done((bf16[256,1024]{1,0:T(8,128)(2,1)S(1)}, bf16[256,1024]{1,0:T(8,128)(2,1)S(1)}, u32[]{:S(2)}, u32[]{:S(2)}) %collective-permute-start.1) | collective-permute-done | bytes 524320 | tf_op jit(solution)/shard_map/ppermute | solution.py:47
  58.2 5.3 %collective-permute-done.4.refs_7_.refs_8_.refs_10_.refs_11_ = bf16[128,1024]{1,0:T(8,128)(2,1)S(1)} collective-permute-done((bf16[128,1024]{1,0:T(8,128)(2,1)S(1)}, bf16[128,1024]{1,0:T(8,128)(2,1)S(1)}, u32[]{:S(2)}, u32[]{:S(2)}) %collective-permute-start.4) | collective-permute-done | bytes 262176 | tf_op jit(solution)/shard_map/ppermute | solution.py:47
  66.7 3.9 %collective-permute-start.5 = (bf16[256,512]{1,0:T(8,128)(2,1)S(1)}, bf16[256,512]{1,0:T(8,128)(2,1)S(1)}, u32[]{:S(2)}, u32[]{:S(2)}) collective-permute-start(bf16[256,512]{1,0:T(8,128)(2,1)S(1)} %get-tuple-element.34), channel_id=1, source_target_pairs={{64,0},{128,64},{192,128},{256,192},{320,256},{384,320},{448,384},... | collective-permute-start | bytes 786440 | tf_op jit(solution)/shard_map/ppermute | solution.py:78
  71.9 2.4 %collective-permute-start.16 = (bf16[256,512]{1,0:T(8,128)(2,1)S(1)}, bf16[256,512]{1,0:T(8,128)(2,1)S(1)}, u32[]{:S(2)}, u32[]{:S(2)}) collective-permute-start(bf16[256,512]{1,0:T(8,128)(2,1)S(1)} %get-tuple-element.47), channel_id=1, source_target_pairs={{64,8},{65,9},{66,10},{67,11},{68,12},{69,13},{70,14},{71,15},{72,... | collective-permute-start | bytes 786440 | tf_op jit(solution)/shard_map/ppermute | solution.py:88
  74.3 3.3 %collective-permute-start.15 = (bf16[256,512]{1,0:T(8,128)(2,1)S(1)}, bf16[256,512]{1,0:T(8,128)(2,1)S(1)}, u32[]{:S(2)}, u32[]{:S(2)}) collective-permute-start(bf16[256,512]{1,0:T(8,128)(2,1)S(1)} %get-tuple-element.47), channel_id=1, source_target_pairs={{64,0},{128,64},{192,128},{256,192},{320,256},{384,320},{448,384},... | collective-permute-start | bytes 786440 | tf_op jit(solution)/shard_map/ppermute | solution.py:78
  83.6 2.9 %collective-permute-start.17 = (bf16[384,512]{1,0:T(8,128)(2,1)S(1)}, bf16[384,512]{1,0:T(8,128)(2,1)S(1)}, u32[]{:S(2)}, u32[]{:S(2)}) collective-permute-start(bf16[384,512]{1,0:T(8,128)(2,1)S(1)} %get-tuple-element.50), channel_id=1, source_target_pairs={{64,0},{128,64},{192,128},{256,192},{320,256},{384,320},{448,384},... | collective-permute-start | bytes 1179656 | tf_op jit(solution)/shard_map/ppermute | solution.py:78
  86.5 2.6 %collective-permute-start.9 = (bf16[256,512]{1,0:T(8,128)(2,1)S(1)}, bf16[256,512]{1,0:T(8,128)(2,1)S(1)}, u32[]{:S(2)}, u32[]{:S(2)}) collective-permute-start(bf16[256,512]{1,0:T(8,128)(2,1)S(1)} %get-tuple-element.36), channel_id=1, source_target_pairs={{64,8},{65,9},{66,10},{67,11},{68,12},{69,13},{70,14},{71,15},{72,... | collective-permute-start | bytes 786440 | tf_op jit(solution)/shard_map/ppermute | solution.py:88
  89.2 3.0 %collective-permute-start.18 = (bf16[256,512]{1,0:T(8,128)(2,1)S(1)}, bf16[256,512]{1,0:T(8,128)(2,1)S(1)}, u32[]{:S(2)}, u32[]{:S(2)}) collective-permute-start(bf16[256,512]{1,0:T(8,128)(2,1)S(1)} %get-tuple-element.51), channel_id=1, source_target_pairs={{64,8},{65,9},{66,10},{67,11},{68,12},{69,13},{70,14},{71,15},{72,... | collective-permute-start | bytes 786440 | tf_op jit(solution)/shard_map/ppermute | solution.py:88
  92.2 7.6 %collective-permute-done.9.refs_1_ = bf16[256,512]{1,0:T(8,128)(2,1)S(1)} collective-permute-done((bf16[256,512]{1,0:T(8,128)(2,1)S(1)}, bf16[256,512]{1,0:T(8,128)(2,1)S(1)}, u32[]{:S(2)}, u32[]{:S(2)}) %collective-permute-start.9) | collective-permute-done | bytes 262176 | tf_op jit(solution)/shard_map/ppermute | solution.py:88
  106.3 3.2 %collective-permute-start.11 = (bf16[256,512]{1,0:T(8,128)(2,1)S(1)}, bf16[256,512]{1,0:T(8,128)(2,1)S(1)}, u32[]{:S(2)}, u32[]{:S(2)}) collective-permute-start(bf16[256,512]{1,0:T(8,128)(2,1)S(1)} %get-tuple-element.38), channel_id=1, source_target_pairs={{64,8},{65,9},{66,10},{67,11},{68,12},{69,13},{70,14},{71,15},{72,... | collective-permute-start | bytes 786440 | tf_op jit(solution)/shard_map/ppermute | solution.py:88
  111.5 4.0 %collective-permute-done.11.refs_1_ = bf16[256,512]{1,0:T(8,128)(2,1)S(1)} collective-permute-done((bf16[256,512]{1,0:T(8,128)(2,1)S(1)}, bf16[256,512]{1,0:T(8,128)(2,1)S(1)}, u32[]{:S(2)}, u32[]{:S(2)}) %collective-permute-start.11) | collective-permute-done | bytes 262176 | tf_op jit(solution)/shard_map/ppermute | solution.py:88
  116.8 6.1 %collective-permute-done.20.other_ref.refs_3_ = bf16[256,512]{1,0:T(8,128)(2,1)S(1)} collective-permute-done((bf16[256,512]{1,0:T(8,128)(2,1)S(1)}, bf16[256,512]{1,0:T(8,128)(2,1)S(1)}, u32[]{:S(2)}, u32[]{:S(2)}) %collective-permute-start.20) | collective-permute-done | bytes 262176 | tf_op jit(solution)/shard_map/ppermute | solution.py:88
  126.4 4.2 %collective-permute-start.22 = (bf16[256,512]{1,0:T(8,128)(2,1)S(1)}, bf16[256,512]{1,0:T(8,128)(2,1)S(1)}, u32[]{:S(2)}, u32[]{:S(2)}) collective-permute-start(bf16[256,512]{1,0:T(8,128)(2,1)S(1)} %shard_map.87), channel_id=1, source_target_pairs={{6,0},{7,1},{4,2},{5,3},{2,4},{3,5},{0,6},{1,7},{14,8},{15,9},{12,... | collective-permute-start | bytes 786440 | tf_op jit(solution)/shard_map/ppermute | solution.py:47
  130.6 3.7 %collective-permute-start.23 = (bf16[256,512]{1,0:T(8,128)(2,1)S(1)}, bf16[256,512]{1,0:T(8,128)(2,1)S(1)}, u32[]{:S(2)}, u32[]{:S(2)}) collective-permute-start(bf16[256,512]{1,0:T(8,128)(2,1)S(1)} %shard_map.88), channel_id=1, source_target_pairs={{4,0},{5,1},{6,2},{7,3},{0,4},{1,5},{2,6},{3,7},{12,8},{13,9},{14,... | collective-permute-start | bytes 786440 | tf_op jit(solution)/shard_map/ppermute | solution.py:47
  136.7 5.7 %collective-permute-done.22 = bf16[256,512]{1,0:T(8,128)(2,1)S(1)} collective-permute-done((bf16[256,512]{1,0:T(8,128)(2,1)S(1)}, bf16[256,512]{1,0:T(8,128)(2,1)S(1)}, u32[]{:S(2)}, u32[]{:S(2)}) %collective-permute-start.22) | collective-permute-done | bytes 262176 | tf_op jit(solution)/shard_map/ppermute | solution.py:47
  143.2 7.8 %all-to-all-start.1 = ((bf16[8,32,512]{2,1,0:T(8,128)(2,1)}), bf16[8,32,512]{2,1,0:T(8,128)(2,1)S(1)}, u32[]{:S(2)}, u32[]{:S(2)}) async-start(bf16[8,32,512]{2,1,0:T(8,128)(2,1)} %bitcast.9), calls=%async_computation.1 | async-start | bytes 524288 | tf_op jit(solution)/shard_map/all_to_all | solution.py:71
  154.9 2.6 %collective-permute-start.13 = (bf16[128,512]{1,0:T(8,128)(2,1)S(1)}, bf16[128,512]{1,0:T(8,128)(2,1)S(1)}, u32[]{:S(2)}, u32[]{:S(2)}) collective-permute-start(bf16[128,512]{1,0:T(8,128)(2,1)S(1)} %get-tuple-element.40), channel_id=1, source_target_pairs={{64,8},{65,9},{66,10},{67,11},{68,12},{69,13},{70,14},{71,15},{72,... | collective-permute-start | bytes 393224 | tf_op jit(solution)/shard_map/ppermute | solution.py:88
  157.5 2.4 %collective-permute-start.25 = (bf16[128,512]{1,0:T(8,128)(2,1)S(1)}, bf16[128,512]{1,0:T(8,128)(2,1)S(1)}, u32[]{:S(2)}, u32[]{:S(2)}) collective-permute-start(bf16[128,512]{1,0:T(8,128)(2,1)S(1)} %get-tuple-element.63), channel_id=1, source_target_pairs={{64,8},{65,9},{66,10},{67,11},{68,12},{69,13},{70,14},{71,15},{72,... | collective-permute-start | bytes 393224 | tf_op jit(solution)/shard_map/ppermute | solution.py:88
  162.0 4.2 %collective-permute-done.25.crossed_ref = bf16[128,512]{1,0:T(8,128)(2,1)S(1)} collective-permute-done((bf16[128,512]{1,0:T(8,128)(2,1)S(1)}, bf16[128,512]{1,0:T(8,128)(2,1)S(1)}, u32[]{:S(2)}, u32[]{:S(2)}) %collective-permute-start.25) | collective-permute-done | bytes 131104 | tf_op jit(solution)/shard_map/ppermute | solution.py:88
  (62 shorter events, 43.9 us)
Async XLA Ops:
  34.3 15.1 %collective-permute-start.2 = (bf16[256,1024]{1,0:T(8,128)(2,1)S(1)}, bf16[256,1024]{1,0:T(8,128)(2,1)S(1)}, u32[]{:S(2)}, u32[]{:S(2)}) collective-permute-start(bf16[256,1024]{1,0:T(8,128)(2,1)S(1)} %bitcast.15), channel_id=1, source_target_pairs={{6,0},{7,1},{4,2},{5,3},{2,4},{3,5},{0,6},{1,7},{14,8},{15,9},{12,... | collective-permute-start | bytes 1572872 | tf_op jit(solution)/shard_map/ppermute | solution.py:47
  39.0 15.0 %collective-permute-start.1 = (bf16[256,1024]{1,0:T(8,128)(2,1)S(1)}, bf16[256,1024]{1,0:T(8,128)(2,1)S(1)}, u32[]{:S(2)}, u32[]{:S(2)}) collective-permute-start(bf16[256,1024]{1,0:T(8,128)(2,1)S(1)} %bitcast.16), channel_id=1, source_target_pairs={{2,0},{3,1},{0,2},{1,3},{6,4},{7,5},{4,6},{5,7},{10,8},{11,9},{8,1... | collective-permute-start | bytes 1572872 | tf_op jit(solution)/shard_map/ppermute | solution.py:47
  41.1 29.4 %collective-permute-start.14 = (bf16[128,512]{1,0:T(8,128)(2,1)S(1)}, bf16[128,512]{1,0:T(8,128)(2,1)S(1)}, u32[]{:S(2)}, u32[]{:S(2)}) collective-permute-start(bf16[128,512]{1,0:T(8,128)(2,1)S(1)} %fusion), channel_id=1, source_target_pairs={{8,0},{9,1},{10,2},{11,3},{12,4},{13,5},{14,6},{15,7},{0,8},{1,9},... | collective-permute-start | bytes 393224 | tf_op jit(solution)/shard_map/ppermute | solution.py:55
  44.2 13.8 %collective-permute-start = (f32[128,512]{1,0:T(8,128)S(1)}, f32[128,512]{1,0:T(8,128)S(1)}, u32[]{:S(2)}, u32[]{:S(2)}) collective-permute-start(f32[128,512]{1,0:T(8,128)S(1)} %slice_bitcast_fusion), channel_id=1, source_target_pairs={{8,0},{9,1},{10,2},{11,3},{12,4},{13,5},{14,6},{15,7},{0,8},{1,9},... | collective-permute-start | bytes 786440 | tf_op jit(solution)/shard_map/ppermute | solution.py:55
  49.4 8.8 %collective-permute-start.3 = (bf16[128,1024]{1,0:T(8,128)(2,1)S(1)}, bf16[128,1024]{1,0:T(8,128)(2,1)S(1)}, u32[]{:S(2)}, u32[]{:S(2)}) collective-permute-start(bf16[128,1024]{1,0:T(8,128)(2,1)S(1)} %slice.18), channel_id=1, source_target_pairs={{2,0},{3,1},{0,2},{1,3},{6,4},{7,5},{4,6},{5,7},{10,8},{11,9},{8,1... | collective-permute-start | bytes 786440 | tf_op jit(solution)/shard_map/ppermute | solution.py:47
  54.0 9.5 %collective-permute-start.4 = (bf16[128,1024]{1,0:T(8,128)(2,1)S(1)}, bf16[128,1024]{1,0:T(8,128)(2,1)S(1)}, u32[]{:S(2)}, u32[]{:S(2)}) collective-permute-start(bf16[128,1024]{1,0:T(8,128)(2,1)S(1)} %slice.19), channel_id=1, source_target_pairs={{6,0},{7,1},{4,2},{5,3},{2,4},{3,5},{0,6},{1,7},{14,8},{15,9},{12,... | collective-permute-start | bytes 786440 | tf_op jit(solution)/shard_map/ppermute | solution.py:47
  56.1 21.5 %collective-permute-start.7 = (bf16[256,512]{1,0:T(8,128)(2,1)S(1)}, bf16[256,512]{1,0:T(8,128)(2,1)S(1)}, u32[]{:S(2)}, u32[]{:S(2)}) collective-permute-start(bf16[256,512]{1,0:T(8,128)(2,1)S(1)} %pad_maximum_fusion), channel_id=1, source_target_pairs={{64,0},{128,64},{192,128},{256,192},{320,256},{384,320},{448,384},... | collective-permute-start | bytes 786440 | tf_op jit(solution)/shard_map/ppermute | solution.py:78
  64.8 12.8 %collective-permute-start.6 = (bf16[256,512]{1,0:T(8,128)(2,1)S(1)}, bf16[256,512]{1,0:T(8,128)(2,1)S(1)}, u32[]{:S(2)}, u32[]{:S(2)}) collective-permute-start(bf16[256,512]{1,0:T(8,128)(2,1)S(1)} %get-tuple-element.34), channel_id=1, source_target_pairs={{64,8},{65,9},{66,10},{67,11},{68,12},{69,13},{70,14},{71,15},{72,... | collective-permute-start | bytes 786440 | tf_op jit(solution)/shard_map/ppermute | solution.py:88
  66.7 10.9 %collective-permute-start.5 = (bf16[256,512]{1,0:T(8,128)(2,1)S(1)}, bf16[256,512]{1,0:T(8,128)(2,1)S(1)}, u32[]{:S(2)}, u32[]{:S(2)}) collective-permute-start(bf16[256,512]{1,0:T(8,128)(2,1)S(1)} %get-tuple-element.34), channel_id=1, source_target_pairs={{64,0},{128,64},{192,128},{256,192},{320,256},{384,320},{448,384},... | collective-permute-start | bytes 786440 | tf_op jit(solution)/shard_map/ppermute | solution.py:78
  71.9 10.5 %collective-permute-start.16 = (bf16[256,512]{1,0:T(8,128)(2,1)S(1)}, bf16[256,512]{1,0:T(8,128)(2,1)S(1)}, u32[]{:S(2)}, u32[]{:S(2)}) collective-permute-start(bf16[256,512]{1,0:T(8,128)(2,1)S(1)} %get-tuple-element.47), channel_id=1, source_target_pairs={{64,8},{65,9},{66,10},{67,11},{68,12},{69,13},{70,14},{71,15},{72,... | collective-permute-start | bytes 786440 | tf_op jit(solution)/shard_map/ppermute | solution.py:88
  79.0 20.9 %collective-permute-start.8 = (bf16[384,512]{1,0:T(8,128)(2,1)S(1)}, bf16[384,512]{1,0:T(8,128)(2,1)S(1)}, u32[]{:S(2)}, u32[]{:S(2)}) collective-permute-start(bf16[384,512]{1,0:T(8,128)(2,1)S(1)} %get-tuple-element.35), channel_id=1, source_target_pairs={{64,0},{128,64},{192,128},{256,192},{320,256},{384,320},{448,384},... | collective-permute-start | bytes 1179656 | tf_op jit(solution)/shard_map/ppermute | solution.py:78
  83.6 19.5 %collective-permute-start.17 = (bf16[384,512]{1,0:T(8,128)(2,1)S(1)}, bf16[384,512]{1,0:T(8,128)(2,1)S(1)}, u32[]{:S(2)}, u32[]{:S(2)}) collective-permute-start(bf16[384,512]{1,0:T(8,128)(2,1)S(1)} %get-tuple-element.50), channel_id=1, source_target_pairs={{64,0},{128,64},{192,128},{256,192},{320,256},{384,320},{448,384},... | collective-permute-start | bytes 1179656 | tf_op jit(solution)/shard_map/ppermute | solution.py:78
  86.5 13.3 %collective-permute-start.9 = (bf16[256,512]{1,0:T(8,128)(2,1)S(1)}, bf16[256,512]{1,0:T(8,128)(2,1)S(1)}, u32[]{:S(2)}, u32[]{:S(2)}) collective-permute-start(bf16[256,512]{1,0:T(8,128)(2,1)S(1)} %get-tuple-element.36), channel_id=1, source_target_pairs={{64,8},{65,9},{66,10},{67,11},{68,12},{69,13},{70,14},{71,15},{72,... | collective-permute-start | bytes 786440 | tf_op jit(solution)/shard_map/ppermute | solution.py:88
  89.2 14.0 %collective-permute-start.18 = (bf16[256,512]{1,0:T(8,128)(2,1)S(1)}, bf16[256,512]{1,0:T(8,128)(2,1)S(1)}, u32[]{:S(2)}, u32[]{:S(2)}) collective-permute-start(bf16[256,512]{1,0:T(8,128)(2,1)S(1)} %get-tuple-element.51), channel_id=1, source_target_pairs={{64,8},{65,9},{66,10},{67,11},{68,12},{69,13},{70,14},{71,15},{72,... | collective-permute-start | bytes 786440 | tf_op jit(solution)/shard_map/ppermute | solution.py:88
  101.2 14.3 %collective-permute-start.10 = (bf16[384,512]{1,0:T(8,128)(2,1)S(1)}, bf16[384,512]{1,0:T(8,128)(2,1)S(1)}, u32[]{:S(2)}, u32[]{:S(2)}) collective-permute-start(bf16[384,512]{1,0:T(8,128)(2,1)S(1)} %get-tuple-element.37), channel_id=1, source_target_pairs={{64,0},{128,64},{192,128},{256,192},{320,256},{384,320},{448,384},... | collective-permute-start | bytes 1179656 | tf_op jit(solution)/shard_map/ppermute | solution.py:78
  104.4 18.5 %collective-permute-start.19 = (bf16[384,512]{1,0:T(8,128)(2,1)S(1)}, bf16[384,512]{1,0:T(8,128)(2,1)S(1)}, u32[]{:S(2)}, u32[]{:S(2)}) collective-permute-start(bf16[384,512]{1,0:T(8,128)(2,1)S(1)} %get-tuple-element.54), channel_id=1, source_target_pairs={{64,0},{128,64},{192,128},{256,192},{320,256},{384,320},{448,384},... | collective-permute-start | bytes 1179656 | tf_op jit(solution)/shard_map/ppermute | solution.py:78
  106.3 9.1 %collective-permute-start.11 = (bf16[256,512]{1,0:T(8,128)(2,1)S(1)}, bf16[256,512]{1,0:T(8,128)(2,1)S(1)}, u32[]{:S(2)}, u32[]{:S(2)}) collective-permute-start(bf16[256,512]{1,0:T(8,128)(2,1)S(1)} %get-tuple-element.38), channel_id=1, source_target_pairs={{64,8},{65,9},{66,10},{67,11},{68,12},{69,13},{70,14},{71,15},{72,... | collective-permute-start | bytes 786440 | tf_op jit(solution)/shard_map/ppermute | solution.py:88
  109.6 13.3 %collective-permute-start.20 = (bf16[256,512]{1,0:T(8,128)(2,1)S(1)}, bf16[256,512]{1,0:T(8,128)(2,1)S(1)}, u32[]{:S(2)}, u32[]{:S(2)}) collective-permute-start(bf16[256,512]{1,0:T(8,128)(2,1)S(1)} %get-tuple-element.55), channel_id=1, source_target_pairs={{64,8},{65,9},{66,10},{67,11},{68,12},{69,13},{70,14},{71,15},{72,... | collective-permute-start | bytes 786440 | tf_op jit(solution)/shard_map/ppermute | solution.py:88
  124.4 12.2 %collective-permute-start.21 = (bf16[256,512]{1,0:T(8,128)(2,1)S(1)}, bf16[256,512]{1,0:T(8,128)(2,1)S(1)}, u32[]{:S(2)}, u32[]{:S(2)}) collective-permute-start(bf16[256,512]{1,0:T(8,128)(2,1)S(1)} %shard_map.86), channel_id=1, source_target_pairs={{2,0},{3,1},{0,2},{1,3},{6,4},{7,5},{4,6},{5,7},{10,8},{11,9},{8,1... | collective-permute-start | bytes 786440 | tf_op jit(solution)/shard_map/ppermute | solution.py:47
  126.4 16.0 %collective-permute-start.22 = (bf16[256,512]{1,0:T(8,128)(2,1)S(1)}, bf16[256,512]{1,0:T(8,128)(2,1)S(1)}, u32[]{:S(2)}, u32[]{:S(2)}) collective-permute-start(bf16[256,512]{1,0:T(8,128)(2,1)S(1)} %shard_map.87), channel_id=1, source_target_pairs={{6,0},{7,1},{4,2},{5,3},{2,4},{3,5},{0,6},{1,7},{14,8},{15,9},{12,... | collective-permute-start | bytes 786440 | tf_op jit(solution)/shard_map/ppermute | solution.py:47
  130.6 11.8 %collective-permute-start.23 = (bf16[256,512]{1,0:T(8,128)(2,1)S(1)}, bf16[256,512]{1,0:T(8,128)(2,1)S(1)}, u32[]{:S(2)}, u32[]{:S(2)}) collective-permute-start(bf16[256,512]{1,0:T(8,128)(2,1)S(1)} %shard_map.88), channel_id=1, source_target_pairs={{4,0},{5,1},{6,2},{7,3},{0,4},{1,5},{2,6},{3,7},{12,8},{13,9},{14,... | collective-permute-start | bytes 786440 | tf_op jit(solution)/shard_map/ppermute | solution.py:47
  143.2 23.8 %all-to-all-start.1 = ((bf16[8,32,512]{2,1,0:T(8,128)(2,1)}), bf16[8,32,512]{2,1,0:T(8,128)(2,1)S(1)}, u32[]{:S(2)}, u32[]{:S(2)}) async-start(bf16[8,32,512]{2,1,0:T(8,128)(2,1)} %bitcast.9), calls=%async_computation.1 | async-start | bytes 524288 | tf_op jit(solution)/shard_map/all_to_all | solution.py:71
  151.1 10.1 %collective-permute-start.12 = (bf16[256,512]{1,0:T(8,128)(2,1)S(1)}, bf16[256,512]{1,0:T(8,128)(2,1)S(1)}, u32[]{:S(2)}, u32[]{:S(2)}) collective-permute-start(bf16[256,512]{1,0:T(8,128)(2,1)S(1)} %get-tuple-element.39), channel_id=1, source_target_pairs={{64,0},{128,64},{192,128},{256,192},{320,256},{384,320},{448,384},... | collective-permute-start | bytes 786440 | tf_op jit(solution)/shard_map/ppermute | solution.py:78
  153.0 13.2 %collective-permute-start.24 = (bf16[256,512]{1,0:T(8,128)(2,1)S(1)}, bf16[256,512]{1,0:T(8,128)(2,1)S(1)}, u32[]{:S(2)}, u32[]{:S(2)}) collective-permute-start(bf16[256,512]{1,0:T(8,128)(2,1)S(1)} %get-tuple-element.62), channel_id=1, source_target_pairs={{64,0},{128,64},{192,128},{256,192},{320,256},{384,320},{448,384},... | collective-permute-start | bytes 786440 | tf_op jit(solution)/shard_map/ppermute | solution.py:78
  (6 other events, 112.8 us)

commit v4 on v3

--- a/solution.py
+++ b/solution.py
@@ -158,8 +158,8 @@
 
 def forward_kernel(fresh, last, counts, *refs):
     state_refs, (gain_ref,), weight_refs, (hidden_ref, slopes_ref, *addend_refs) = split(counts, refs)
-    first, second = pair_state(fresh, 0, 0, state_refs)
-    tokens, half = second.shape
+    first, second = pair_state(fresh, 0, None if last else 0, state_refs)
+    tokens, half = first.shape[0] // 2, first.shape[1]
     normed = (first * inverse_rms(first) * gain_ref[...]).astype(jnp.bfloat16)
     for span, weight_ref in spans(weight_refs):
         preact = lax.dot_general(
@@ -176,14 +176,28 @@
         jnp.dot(hidden_ref[:, span], weight_ref[:, half:], preferred_element_type=jnp.float32)
         for span, weight_ref in spans(weight_refs)
     )
+    other = (0.0 - branch[tokens:]) / coupling_scale
+    if last:
+        crossed_ref, branch_ref, first_ref = addend_refs
+        crossed_ref[...] = other.astype(crossed_ref.dtype)
+        branch_ref[...] = branch[:tokens]
+        first_ref[...] = first[:tokens].astype(first_ref.dtype)
+        return
     own = (second - branch[:tokens]) / coupling_scale
-    other = (0.0 - branch[tokens:]) / coupling_scale
     put_addends(last, addend_refs, own, other, first[:tokens])
 
 
-def backward_kernel(fresh, last, counts, *refs):
+def acts_end_kernel(waiting_ref, branch_ref, first_ref, out_ref):
+    tokens = branch_ref.shape[0]
+    second = waiting_ref[:tokens].astype(jnp.float32)
+    out_ref[:tokens] = ((second - branch_ref[...]) / coupling_scale).astype(out_ref.dtype)
+    out_ref[tokens:] = first_ref[...]
+
+
+def backward_kernel(fresh, alone, last, counts, *refs):
     acts_refs, state_refs, (gain_ref, slopes_ref), weight_refs, outs = split(counts, refs)
     cotangent_ref, *addend_refs, pre_grad = outs
+    ahead_ref = addend_refs.pop() if alone and not fresh else None
     half = gain_ref.shape[1]
     second_grad, first_grad = pair_state(fresh, half, 1, state_refs)
     tokens = first_grad.shape[0]
@@ -205,6 +219,9 @@
         for span, weight_ref in spans(weight_refs)
     )
     first = pair_state(fresh, 0, None, acts_refs)[0]
+    if ahead_ref is not None:
+        ahead_ref[:tokens] = first[:tokens].astype(ahead_ref.dtype)
+        ahead_ref[tokens:] = cotangent[:tokens]
     inv_rms = inverse_rms(first)
     scaled = norm_grad * gain_ref[...]
     inner = jnp.mean(first * scaled, axis=-1, keepdims=True)
@@ -276,8 +293,8 @@
     )(*operands)
 
 
-def addend_shapes(fresh, last, tokens, half):
-    if fresh:
+def addend_shapes(alone, last, tokens, half):
+    if alone:
         return (((2 * tokens, half), jnp.bfloat16),)
     straight, crossed = (2, 1) if last else (3, 2)
     return (
@@ -286,8 +303,12 @@
     )
 
 
-def forward(fresh, last, tokens, acts, gain, weights):
+def forward(fresh, alone, last, tokens, acts, gain, weights):
     half = gain.shape[1]
+    addends = addend_shapes(alone, last, tokens, half)
+    if last:
+        block = (tokens, half)
+        addends = ((block, jnp.bfloat16), (block, jnp.float32), (block, jnp.bfloat16))
     units = sum(w.shape[0] for w in weights)
     return call(
         functools.partial(forward_kernel, fresh, last, (len(acts), 1, len(weights))),
@@ -295,20 +316,31 @@
         (
             ((2 * tokens, units), jnp.bfloat16),
             ((2 * tokens, units), jnp.bfloat16),
-            *addend_shapes(fresh, last, tokens, half),
+            *addends,
         ),
         (*acts, gain, *weights),
     )
 
 
-def backward(fresh, last, tokens, acts, grads, gain, slopes, weights):
+def acts_end(waiting, branch, first):
+    tokens, half = branch.shape
+    return call(
+        acts_end_kernel,
+        small_cost(tokens, half),
+        (((2 * tokens, half), jnp.bfloat16),),
+        (waiting, branch, first),
+    )[0]
+
+
+def backward(fresh, alone, last, tokens, acts, grads, gain, slopes, weights):
     half = gain.shape[1]
+    ahead = (((2 * tokens, half), jnp.bfloat16),) if alone and not fresh else ()
     units = slopes.shape[1]
     counts = (len(acts), len(grads), 2, len(weights))
     return call(
-        functools.partial(backward_kernel, fresh, last, counts),
+        functools.partial(backward_kernel, fresh, alone, last, counts),
         cost(2 * tokens, units, half),
-        (((2 * tokens, half), jnp.bfloat16), *addend_shapes(fresh, last, tokens, half)),
+        (((2 * tokens, half), jnp.bfloat16), *addend_shapes(alone, last, tokens, half), *ahead),
         (*acts, *grads, gain, slopes, *weights),
         (pltpu.VMEM((2 * tokens, units), jnp.bfloat16),),
     )
@@ -376,12 +408,21 @@
     hiddens, cotangents = [], []
     for tick_index in range(tick_count):
         fresh, last = tick_index == 0, tick_index == tick_count - 1
-        hidden, slopes, *addends = forward(fresh, last, tokens, acts_pair, gain, weights)
+        alone = tick_index in (0, tick_count - 2)
+        state = acts_pair[:2] if last else acts_pair
+        hidden, slopes, *addends = forward(fresh, alone, last, tokens, state, gain, weights)
         hiddens.append(hidden)
-        next_acts = sent_back(*addends)
         if last:
-            grads_pair, hidden, addends = lax.optimization_barrier((grads_pair, hidden, addends))
-            cotangents.append(cotangent_of(grads_pair))
+            crossed, branch, first = addends
+            crossed = passed_back_to_partner(crossed)
+            straight = passed_back(acts_end(acts_pair[2], branch, first))
+            next_acts = straight, crossed
+        else:
+            next_acts = sent_back(*addends)
+        if last:
+            straight, crossed, hidden = lax.optimization_barrier((*grads_pair[:2], hidden))
+            grads_pair = (straight, crossed, grads_pair[2])
+            cotangents.append(cotangent_of(grads_pair[:2]))
             outer = functools.partial(outer_rows, hiddens, cotangents, count=quarter)
             far_rows = outer(3 * quarter)
             near_rows = outer(quarter)
@@ -391,7 +432,7 @@
             from_next = swapped_along_x(next_rows, next_x)
             slopes, _ = lax.optimization_barrier((slopes, (far_rows, near_rows, next_rows)))
         cotangent, *addends = backward(
-            fresh, last, tokens, acts_pair[:2], grads_pair, gain, slopes, weights
+            fresh, alone, last, tokens, acts_pair[:2], grads_pair, gain, slopes, weights
         )
         if last:
             own = outer(0)
@@ -402,9 +443,12 @@
             parts = exchanged(blocks).reshape(-1, units, half)
         else:
             cotangents.append(cotangent)
+        ahead = addends.pop() if alone and not fresh else None
         next_grads = sent_back(*addends)
+        if ahead is not None:
+            sent_ahead = passed_back(ahead)
         acts_pair, grads_pair = next_acts, next_grads
-        if fresh:
+        if alone:
             acts_pair, grads_pair = (*acts_pair, sent_ahead), (*grads_pair, sent_ahead)
 
     share = jnp.sum(parts.astype(jnp.float32), axis=0)

time: 169 us -> 166 us (0.982)
  waiting for transfers between devices: 40.4 us -> 35.4 us
  starting transfers between devices: 76.2 us -> 78.1 us
    ppermute x8, waiting for transfers between devices: 24.6 us -> 18.5 us  [passed_back_to_partner(): return lax.ppermute(block, ('section', 'dp'), route)]
    ppermute x9 -> x10, starting transfers between devices: 21.5 us -> 25 us  [passed_back(): return lax.ppermute(block, 'section', [(i, i - 1) for i in devices if i])]
    pallas_call x15 -> x16, Pallas kernels: 14.7 us -> 14.7 us  [call(): pl.pallas_call(kernel, out_shape=tuple((jax.ShapeDtypeStruct(shape, dtype...]
  transfers between devices with their start and end apart: 27 -> 28, of which waited for: 11 -> 10; matrix products, arithmetic and copies ran while one was open for 0% -> 0% of each run, Pallas kernels for 8% -> 9%
where the time goes in v4:
time: 166 us; the launch traced here: 165 us
  starting transfers between devices  78.1 us (47%)
  waiting for transfers between devices  35.4 us (21%)
  blocking collectives  32.8 us (20%)
  Pallas kernels  14.7 us (9%)
  other arithmetic  2.29 us (1%)
    all_to_all x1, blocking collectives, exchanged(): lax.all_to_all(blocks, 'dp', 0, 0, axis_index_groups=alike_groups(), tile...  32.8 us
    ppermute x10, starting transfers between devices, passed_back(): return lax.ppermute(block, 'section', [(i, i - 1) for i in devices if i])  25 us
    ppermute x7, starting transfers between devices, swapped_along_x(): return lax.ppermute(block, 'dp', route)  20.9 us
    ppermute x8, starting transfers between devices, passed_back_to_partner(): return lax.ppermute(block, ('section', 'dp'), route)  18.7 us
    ppermute x8, waiting for transfers between devices, passed_back_to_partner(): return lax.ppermute(block, ('section', 'dp'), route)  18.5 us
    ppermute x7, waiting for transfers between devices, swapped_along_x(): return lax.ppermute(block, 'dp', route)  16.9 us
    pallas_call x16, Pallas kernels, call(): pl.pallas_call(kernel, out_shape=tuple((jax.ShapeDtypeStruct(shape, dtype...  14.7 us
    all_to_all x1, starting transfers between devices, exchanged(): lax.all_to_all(blocks, 'dp', 0, 0, axis_index_groups=alike_groups(), tile...  7.78 us
  transfers between devices with their start and end apart: 28, of which 10 were waited for; matrix products, arithmetic and copies ran while one was open for 0% of the time, Pallas kernels for 9%

profile of v4, /device:TPU:48, one launch (start us, length us, event | category | flops | bytes accessed | tf_op | source)
XLA Modules:
  0.0 164.6 jit_solution(10802405126671301092)
XLA Ops:
  1.5 32.8 %all_to_all.17 = bf16[8,32,1024]{2,1,0:T(8,128)(2,1)S(1)} all-to-all(bf16[8,32,1024]{2,1,0:T(8,128)(2,1)S(1)} %tile.2), channel_id=1, replica_groups={{0,1,16,17,32,33,48,49},{2,3,18,19,34,35,50,51},{4,5,20,21,36,37,52,53}..., dimensions={0} | all-to-all | bytes 1048576 | tf_op jit(solution)/shard_map/all_to_all | solution.py:71
  34.3 4.7 %collective-permute-start.2 = (bf16[256,1024]{1,0:T(8,128)(2,1)S(1)}, bf16[256,1024]{1,0:T(8,128)(2,1)S(1)}, u32[]{:S(2)}, u32[]{:S(2)}) collective-permute-start(bf16[256,1024]{1,0:T(8,128)(2,1)S(1)} %bitcast.15), channel_id=1, source_target_pairs={{6,0},{7,1},{4,2},{5,3},{2,4},{3,5},{0,6},{1,7},{14,8},{15,9},{12,... | collective-permute-start | bytes 1572872 | tf_op jit(solution)/shard_map/ppermute | solution.py:47
  41.1 3.0 %collective-permute-start.10 = (bf16[128,512]{1,0:T(8,128)(2,1)S(1)}, bf16[128,512]{1,0:T(8,128)(2,1)S(1)}, u32[]{:S(2)}, u32[]{:S(2)}) collective-permute-start(bf16[128,512]{1,0:T(8,128)(2,1)S(1)} %fusion), channel_id=1, source_target_pairs={{8,0},{9,1},{10,2},{11,3},{12,4},{13,5},{14,6},{15,7},{0,8},{1,9},... | collective-permute-start | bytes 393224 | tf_op jit(solution)/shard_map/ppermute | solution.py:55
  44.2 2.8 %collective-permute-start = (f32[128,512]{1,0:T(8,128)S(1)}, f32[128,512]{1,0:T(8,128)S(1)}, u32[]{:S(2)}, u32[]{:S(2)}) collective-permute-start(f32[128,512]{1,0:T(8,128)S(1)} %slice_bitcast_fusion), channel_id=1, source_target_pairs={{8,0},{9,1},{10,2},{11,3},{12,4},{13,5},{14,6},{15,7},{0,8},{1,9},... | collective-permute-start | bytes 786440 | tf_op jit(solution)/shard_map/ppermute | solution.py:55
  47.0 2.3 %collective-permute-done.2.refs_5_.refs_6_.refs_8_.refs_9_ = bf16[256,1024]{1,0:T(8,128)(2,1)S(1)} collective-permute-done((bf16[256,1024]{1,0:T(8,128)(2,1)S(1)}, bf16[256,1024]{1,0:T(8,128)(2,1)S(1)}, u32[]{:S(2)}, u32[]{:S(2)}) %collective-permute-start.2) | collective-permute-done | bytes 524320 | tf_op jit(solution)/shard_map/ppermute | solution.py:47
  49.4 2.2 %collective-permute-start.3 = (bf16[128,1024]{1,0:T(8,128)(2,1)S(1)}, bf16[128,1024]{1,0:T(8,128)(2,1)S(1)}, u32[]{:S(2)}, u32[]{:S(2)}) collective-permute-start(bf16[128,1024]{1,0:T(8,128)(2,1)S(1)} %slice.18), channel_id=1, source_target_pairs={{2,0},{3,1},{0,2},{1,3},{6,4},{7,5},{4,6},{5,7},{10,8},{11,9},{8,1... | collective-permute-start | bytes 786440 | tf_op jit(solution)/shard_map/ppermute | solution.py:47
  51.6 2.3 %collective-permute-done.1.refs_4_.refs_5_.refs_7_.refs_8_ = bf16[256,1024]{1,0:T(8,128)(2,1)S(1)} collective-permute-done((bf16[256,1024]{1,0:T(8,128)(2,1)S(1)}, bf16[256,1024]{1,0:T(8,128)(2,1)S(1)}, u32[]{:S(2)}, u32[]{:S(2)}) %collective-permute-start.1) | collective-permute-done | bytes 524320 | tf_op jit(solution)/shard_map/ppermute | solution.py:47
  58.2 5.3 %collective-permute-done.4.refs_7_.refs_8_.refs_10_.refs_11_ = bf16[128,1024]{1,0:T(8,128)(2,1)S(1)} collective-permute-done((bf16[128,1024]{1,0:T(8,128)(2,1)S(1)}, bf16[128,1024]{1,0:T(8,128)(2,1)S(1)}, u32[]{:S(2)}, u32[]{:S(2)}) %collective-permute-start.4) | collective-permute-done | bytes 262176 | tf_op jit(solution)/shard_map/ppermute | solution.py:47
  66.7 3.9 %collective-permute-start.5 = (bf16[256,512]{1,0:T(8,128)(2,1)S(1)}, bf16[256,512]{1,0:T(8,128)(2,1)S(1)}, u32[]{:S(2)}, u32[]{:S(2)}) collective-permute-start(bf16[256,512]{1,0:T(8,128)(2,1)S(1)} %get-tuple-element.34), channel_id=1, source_target_pairs={{64,0},{128,64},{192,128},{256,192},{320,256},{384,320},{448,384},... | collective-permute-start | bytes 786440 | tf_op jit(solution)/shard_map/ppermute | solution.py:78
  71.9 2.4 %collective-permute-start.12 = (bf16[256,512]{1,0:T(8,128)(2,1)S(1)}, bf16[256,512]{1,0:T(8,128)(2,1)S(1)}, u32[]{:S(2)}, u32[]{:S(2)}) collective-permute-start(bf16[256,512]{1,0:T(8,128)(2,1)S(1)} %get-tuple-element.38), channel_id=1, source_target_pairs={{64,8},{65,9},{66,10},{67,11},{68,12},{69,13},{70,14},{71,15},{72,... | collective-permute-start | bytes 786440 | tf_op jit(solution)/shard_map/ppermute | solution.py:88
  74.3 3.3 %collective-permute-start.11 = (bf16[256,512]{1,0:T(8,128)(2,1)S(1)}, bf16[256,512]{1,0:T(8,128)(2,1)S(1)}, u32[]{:S(2)}, u32[]{:S(2)}) collective-permute-start(bf16[256,512]{1,0:T(8,128)(2,1)S(1)} %get-tuple-element.38), channel_id=1, source_target_pairs={{64,0},{128,64},{192,128},{256,192},{320,256},{384,320},{448,384},... | collective-permute-start | bytes 786440 | tf_op jit(solution)/shard_map/ppermute | solution.py:78
  83.6 2.9 %collective-permute-start.13 = (bf16[384,512]{1,0:T(8,128)(2,1)S(1)}, bf16[384,512]{1,0:T(8,128)(2,1)S(1)}, u32[]{:S(2)}, u32[]{:S(2)}) collective-permute-start(bf16[384,512]{1,0:T(8,128)(2,1)S(1)} %get-tuple-element.40), channel_id=1, source_target_pairs={{64,0},{128,64},{192,128},{256,192},{320,256},{384,320},{448,384},... | collective-permute-start | bytes 1179656 | tf_op jit(solution)/shard_map/ppermute | solution.py:78
  86.5 2.6 %collective-permute-start.9 = (bf16[256,512]{1,0:T(8,128)(2,1)S(1)}, bf16[256,512]{1,0:T(8,128)(2,1)S(1)}, u32[]{:S(2)}, u32[]{:S(2)}) collective-permute-start(bf16[256,512]{1,0:T(8,128)(2,1)S(1)} %get-tuple-element.36), channel_id=1, source_target_pairs={{64,8},{65,9},{66,10},{67,11},{68,12},{69,13},{70,14},{71,15},{72,... | collective-permute-start | bytes 786440 | tf_op jit(solution)/shard_map/ppermute | solution.py:88
  89.2 3.0 %collective-permute-start.14 = (bf16[256,512]{1,0:T(8,128)(2,1)S(1)}, bf16[256,512]{1,0:T(8,128)(2,1)S(1)}, u32[]{:S(2)}, u32[]{:S(2)}) collective-permute-start(bf16[256,512]{1,0:T(8,128)(2,1)S(1)} %get-tuple-element.41), channel_id=1, source_target_pairs={{64,8},{65,9},{66,10},{67,11},{68,12},{69,13},{70,14},{71,15},{72,... | collective-permute-start | bytes 786440 | tf_op jit(solution)/shard_map/ppermute | solution.py:88
  92.2 7.6 %collective-permute-done.9.refs_1_ = bf16[256,512]{1,0:T(8,128)(2,1)S(1)} collective-permute-done((bf16[256,512]{1,0:T(8,128)(2,1)S(1)}, bf16[256,512]{1,0:T(8,128)(2,1)S(1)}, u32[]{:S(2)}, u32[]{:S(2)}) %collective-permute-start.9) | collective-permute-done | bytes 262176 | tf_op jit(solution)/shard_map/ppermute | solution.py:88
  103.1 3.4 %collective-permute-start.16 = (bf16[256,512]{1,0:T(8,128)(2,1)S(1)}, bf16[256,512]{1,0:T(8,128)(2,1)S(1)}, u32[]{:S(2)}, u32[]{:S(2)}) collective-permute-start(bf16[256,512]{1,0:T(8,128)(2,1)S(1)} %get-tuple-element.44), channel_id=1, source_target_pairs={{64,0},{128,64},{192,128},{256,192},{320,256},{384,320},{448,384},... | collective-permute-start | bytes 786440 | tf_op jit(solution)/shard_map/ppermute | solution.py:78
  115.0 3.3 %collective-permute-done.21.other_ref.refs_3_ = bf16[256,512]{1,0:T(8,128)(2,1)S(1)} collective-permute-done((bf16[256,512]{1,0:T(8,128)(2,1)S(1)}, bf16[256,512]{1,0:T(8,128)(2,1)S(1)}, u32[]{:S(2)}, u32[]{:S(2)}) %collective-permute-start.21) | collective-permute-done | bytes 262176 | tf_op jit(solution)/shard_map/ppermute | solution.py:88
  121.7 4.2 %collective-permute-start.23 = (bf16[256,512]{1,0:T(8,128)(2,1)S(1)}, bf16[256,512]{1,0:T(8,128)(2,1)S(1)}, u32[]{:S(2)}, u32[]{:S(2)}) collective-permute-start(bf16[256,512]{1,0:T(8,128)(2,1)S(1)} %shard_map.88), channel_id=1, source_target_pairs={{6,0},{7,1},{4,2},{5,3},{2,4},{3,5},{0,6},{1,7},{14,8},{15,9},{12,... | collective-permute-start | bytes 786440 | tf_op jit(solution)/shard_map/ppermute | solution.py:47
  126.0 3.7 %collective-permute-start.24 = (bf16[256,512]{1,0:T(8,128)(2,1)S(1)}, bf16[256,512]{1,0:T(8,128)(2,1)S(1)}, u32[]{:S(2)}, u32[]{:S(2)}) collective-permute-start(bf16[256,512]{1,0:T(8,128)(2,1)S(1)} %shard_map.89), channel_id=1, source_target_pairs={{4,0},{5,1},{6,2},{7,3},{0,4},{1,5},{2,6},{3,7},{12,8},{13,9},{14,... | collective-permute-start | bytes 786440 | tf_op jit(solution)/shard_map/ppermute | solution.py:47
  132.0 6.8 %collective-permute-done.23 = bf16[256,512]{1,0:T(8,128)(2,1)S(1)} collective-permute-done((bf16[256,512]{1,0:T(8,128)(2,1)S(1)}, bf16[256,512]{1,0:T(8,128)(2,1)S(1)}, u32[]{:S(2)}, u32[]{:S(2)}) %collective-permute-start.23) | collective-permute-done | bytes 262176 | tf_op jit(solution)/shard_map/ppermute | solution.py:47
  139.6 7.8 %all-to-all-start.1 = ((bf16[8,32,512]{2,1,0:T(8,128)(2,1)}), bf16[8,32,512]{2,1,0:T(8,128)(2,1)S(1)}, u32[]{:S(2)}, u32[]{:S(2)}) async-start(bf16[8,32,512]{2,1,0:T(8,128)(2,1)} %bitcast.9), calls=%async_computation.1 | async-start | bytes 524288 | tf_op jit(solution)/shard_map/all_to_all | solution.py:71
  151.3 2.7 %collective-permute-start.19 = (bf16[128,512]{1,0:T(8,128)(2,1)S(1)}, bf16[128,512]{1,0:T(8,128)(2,1)S(1)}, u32[]{:S(2)}, u32[]{:S(2)}) collective-permute-start(bf16[128,512]{1,0:T(8,128)(2,1)S(1)} %get-tuple-element.47), channel_id=1, source_target_pairs={{64,8},{65,9},{66,10},{67,11},{68,12},{69,13},{70,14},{71,15},{72,... | collective-permute-start | bytes 393224 | tf_op jit(solution)/shard_map/ppermute | solution.py:88
  156.2 2.7 %collective-permute-done.19.crossed_ref = bf16[128,512]{1,0:T(8,128)(2,1)S(1)} collective-permute-done((bf16[128,512]{1,0:T(8,128)(2,1)S(1)}, bf16[128,512]{1,0:T(8,128)(2,1)S(1)}, u32[]{:S(2)}, u32[]{:S(2)}) %collective-permute-start.19) | collective-permute-done | bytes 131104 | tf_op jit(solution)/shard_map/ppermute | solution.py:88
  159.8 3.3 %collective-permute-done.26.crossed_ref = bf16[128,512]{1,0:T(8,128)(2,1)S(1)} collective-permute-done((bf16[128,512]{1,0:T(8,128)(2,1)S(1)}, bf16[128,512]{1,0:T(8,128)(2,1)S(1)}, u32[]{:S(2)}, u32[]{:S(2)}) %collective-permute-start.26) | collective-permute-done | bytes 131104 | tf_op jit(solution)/shard_map/ppermute | solution.py:88
  (65 shorter events, 44.3 us)
Async XLA Ops:
  34.3 15.1 %collective-permute-start.2 = (bf16[256,1024]{1,0:T(8,128)(2,1)S(1)}, bf16[256,1024]{1,0:T(8,128)(2,1)S(1)}, u32[]{:S(2)}, u32[]{:S(2)}) collective-permute-start(bf16[256,1024]{1,0:T(8,128)(2,1)S(1)} %bitcast.15), channel_id=1, source_target_pairs={{6,0},{7,1},{4,2},{5,3},{2,4},{3,5},{0,6},{1,7},{14,8},{15,9},{12,... | collective-permute-start | bytes 1572872 | tf_op jit(solution)/shard_map/ppermute | solution.py:47
  39.0 15.0 %collective-permute-start.1 = (bf16[256,1024]{1,0:T(8,128)(2,1)S(1)}, bf16[256,1024]{1,0:T(8,128)(2,1)S(1)}, u32[]{:S(2)}, u32[]{:S(2)}) collective-permute-start(bf16[256,1024]{1,0:T(8,128)(2,1)S(1)} %bitcast.16), channel_id=1, source_target_pairs={{2,0},{3,1},{0,2},{1,3},{6,4},{7,5},{4,6},{5,7},{10,8},{11,9},{8,1... | collective-permute-start | bytes 1572872 | tf_op jit(solution)/shard_map/ppermute | solution.py:47
  41.1 29.4 %collective-permute-start.10 = (bf16[128,512]{1,0:T(8,128)(2,1)S(1)}, bf16[128,512]{1,0:T(8,128)(2,1)S(1)}, u32[]{:S(2)}, u32[]{:S(2)}) collective-permute-start(bf16[128,512]{1,0:T(8,128)(2,1)S(1)} %fusion), channel_id=1, source_target_pairs={{8,0},{9,1},{10,2},{11,3},{12,4},{13,5},{14,6},{15,7},{0,8},{1,9},... | collective-permute-start | bytes 393224 | tf_op jit(solution)/shard_map/ppermute | solution.py:55
  44.2 13.8 %collective-permute-start = (f32[128,512]{1,0:T(8,128)S(1)}, f32[128,512]{1,0:T(8,128)S(1)}, u32[]{:S(2)}, u32[]{:S(2)}) collective-permute-start(f32[128,512]{1,0:T(8,128)S(1)} %slice_bitcast_fusion), channel_id=1, source_target_pairs={{8,0},{9,1},{10,2},{11,3},{12,4},{13,5},{14,6},{15,7},{0,8},{1,9},... | collective-permute-start | bytes 786440 | tf_op jit(solution)/shard_map/ppermute | solution.py:55
  54.0 9.5 %collective-permute-start.4 = (bf16[128,1024]{1,0:T(8,128)(2,1)S(1)}, bf16[128,1024]{1,0:T(8,128)(2,1)S(1)}, u32[]{:S(2)}, u32[]{:S(2)}) collective-permute-start(bf16[128,1024]{1,0:T(8,128)(2,1)S(1)} %slice.19), channel_id=1, source_target_pairs={{6,0},{7,1},{4,2},{5,3},{2,4},{3,5},{0,6},{1,7},{14,8},{15,9},{12,... | collective-permute-start | bytes 786440 | tf_op jit(solution)/shard_map/ppermute | solution.py:47
  56.1 21.5 %collective-permute-start.7 = (bf16[256,512]{1,0:T(8,128)(2,1)S(1)}, bf16[256,512]{1,0:T(8,128)(2,1)S(1)}, u32[]{:S(2)}, u32[]{:S(2)}) collective-permute-start(bf16[256,512]{1,0:T(8,128)(2,1)S(1)} %pad_maximum_fusion), channel_id=1, source_target_pairs={{64,0},{128,64},{192,128},{256,192},{320,256},{384,320},{448,384},... | collective-permute-start | bytes 786440 | tf_op jit(solution)/shard_map/ppermute | solution.py:78
  64.8 12.8 %collective-permute-start.6 = (bf16[256,512]{1,0:T(8,128)(2,1)S(1)}, bf16[256,512]{1,0:T(8,128)(2,1)S(1)}, u32[]{:S(2)}, u32[]{:S(2)}) collective-permute-start(bf16[256,512]{1,0:T(8,128)(2,1)S(1)} %get-tuple-element.34), channel_id=1, source_target_pairs={{64,8},{65,9},{66,10},{67,11},{68,12},{69,13},{70,14},{71,15},{72,... | collective-permute-start | bytes 786440 | tf_op jit(solution)/shard_map/ppermute | solution.py:88
  66.7 10.9 %collective-permute-start.5 = (bf16[256,512]{1,0:T(8,128)(2,1)S(1)}, bf16[256,512]{1,0:T(8,128)(2,1)S(1)}, u32[]{:S(2)}, u32[]{:S(2)}) collective-permute-start(bf16[256,512]{1,0:T(8,128)(2,1)S(1)} %get-tuple-element.34), channel_id=1, source_target_pairs={{64,0},{128,64},{192,128},{256,192},{320,256},{384,320},{448,384},... | collective-permute-start | bytes 786440 | tf_op jit(solution)/shard_map/ppermute | solution.py:78
  71.9 10.5 %collective-permute-start.12 = (bf16[256,512]{1,0:T(8,128)(2,1)S(1)}, bf16[256,512]{1,0:T(8,128)(2,1)S(1)}, u32[]{:S(2)}, u32[]{:S(2)}) collective-permute-start(bf16[256,512]{1,0:T(8,128)(2,1)S(1)} %get-tuple-element.38), channel_id=1, source_target_pairs={{64,8},{65,9},{66,10},{67,11},{68,12},{69,13},{70,14},{71,15},{72,... | collective-permute-start | bytes 786440 | tf_op jit(solution)/shard_map/ppermute | solution.py:88
  79.0 20.9 %collective-permute-start.8 = (bf16[384,512]{1,0:T(8,128)(2,1)S(1)}, bf16[384,512]{1,0:T(8,128)(2,1)S(1)}, u32[]{:S(2)}, u32[]{:S(2)}) collective-permute-start(bf16[384,512]{1,0:T(8,128)(2,1)S(1)} %get-tuple-element.35), channel_id=1, source_target_pairs={{64,0},{128,64},{192,128},{256,192},{320,256},{384,320},{448,384},... | collective-permute-start | bytes 1179656 | tf_op jit(solution)/shard_map/ppermute | solution.py:78
  83.6 22.9 %collective-permute-start.13 = (bf16[384,512]{1,0:T(8,128)(2,1)S(1)}, bf16[384,512]{1,0:T(8,128)(2,1)S(1)}, u32[]{:S(2)}, u32[]{:S(2)}) collective-permute-start(bf16[384,512]{1,0:T(8,128)(2,1)S(1)} %get-tuple-element.40), channel_id=1, source_target_pairs={{64,0},{128,64},{192,128},{256,192},{320,256},{384,320},{448,384},... | collective-permute-start | bytes 1179656 | tf_op jit(solution)/shard_map/ppermute | solution.py:78
  86.5 13.3 %collective-permute-start.9 = (bf16[256,512]{1,0:T(8,128)(2,1)S(1)}, bf16[256,512]{1,0:T(8,128)(2,1)S(1)}, u32[]{:S(2)}, u32[]{:S(2)}) collective-permute-start(bf16[256,512]{1,0:T(8,128)(2,1)S(1)} %get-tuple-element.36), channel_id=1, source_target_pairs={{64,8},{65,9},{66,10},{67,11},{68,12},{69,13},{70,14},{71,15},{72,... | collective-permute-start | bytes 786440 | tf_op jit(solution)/shard_map/ppermute | solution.py:88
  89.2 17.4 %collective-permute-start.14 = (bf16[256,512]{1,0:T(8,128)(2,1)S(1)}, bf16[256,512]{1,0:T(8,128)(2,1)S(1)}, u32[]{:S(2)}, u32[]{:S(2)}) collective-permute-start(bf16[256,512]{1,0:T(8,128)(2,1)S(1)} %get-tuple-element.41), channel_id=1, source_target_pairs={{64,8},{65,9},{66,10},{67,11},{68,12},{69,13},{70,14},{71,15},{72,... | collective-permute-start | bytes 786440 | tf_op jit(solution)/shard_map/ppermute | solution.py:88
  101.2 12.4 %collective-permute-start.17 = (bf16[256,512]{1,0:T(8,128)(2,1)S(1)}, bf16[256,512]{1,0:T(8,128)(2,1)S(1)}, u32[]{:S(2)}, u32[]{:S(2)}) collective-permute-start(bf16[256,512]{1,0:T(8,128)(2,1)S(1)} %get-tuple-element.44), channel_id=1, source_target_pairs={{64,8},{65,9},{66,10},{67,11},{68,12},{69,13},{70,14},{71,15},{72,... | collective-permute-start | bytes 786440 | tf_op jit(solution)/shard_map/ppermute | solution.py:88
  103.1 10.5 %collective-permute-start.16 = (bf16[256,512]{1,0:T(8,128)(2,1)S(1)}, bf16[256,512]{1,0:T(8,128)(2,1)S(1)}, u32[]{:S(2)}, u32[]{:S(2)}) collective-permute-start(bf16[256,512]{1,0:T(8,128)(2,1)S(1)} %get-tuple-element.44), channel_id=1, source_target_pairs={{64,0},{128,64},{192,128},{256,192},{320,256},{384,320},{448,384},... | collective-permute-start | bytes 786440 | tf_op jit(solution)/shard_map/ppermute | solution.py:78
  107.8 10.5 %collective-permute-start.21 = (bf16[256,512]{1,0:T(8,128)(2,1)S(1)}, bf16[256,512]{1,0:T(8,128)(2,1)S(1)}, u32[]{:S(2)}, u32[]{:S(2)}) collective-permute-start(bf16[256,512]{1,0:T(8,128)(2,1)S(1)} %get-tuple-element.55), channel_id=1, source_target_pairs={{64,8},{65,9},{66,10},{67,11},{68,12},{69,13},{70,14},{71,15},{72,... | collective-permute-start | bytes 786440 | tf_op jit(solution)/shard_map/ppermute | solution.py:88
  111.6 18.5 %collective-permute-start.15 = (bf16[256,512]{1,0:T(8,128)(2,1)S(1)}, bf16[256,512]{1,0:T(8,128)(2,1)S(1)}, u32[]{:S(2)}, u32[]{:S(2)}) collective-permute-start(bf16[256,512]{1,0:T(8,128)(2,1)S(1)} %get-tuple-element.43), channel_id=1, source_target_pairs={{64,0},{128,64},{192,128},{256,192},{320,256},{384,320},{448,384},... | collective-permute-start | bytes 786440 | tf_op jit(solution)/shard_map/ppermute | solution.py:78
  119.8 12.2 %collective-permute-start.22 = (bf16[256,512]{1,0:T(8,128)(2,1)S(1)}, bf16[256,512]{1,0:T(8,128)(2,1)S(1)}, u32[]{:S(2)}, u32[]{:S(2)}) collective-permute-start(bf16[256,512]{1,0:T(8,128)(2,1)S(1)} %shard_map.87), channel_id=1, source_target_pairs={{2,0},{3,1},{0,2},{1,3},{6,4},{7,5},{4,6},{5,7},{10,8},{11,9},{8,1... | collective-permute-start | bytes 786440 | tf_op jit(solution)/shard_map/ppermute | solution.py:47
  121.7 17.1 %collective-permute-start.23 = (bf16[256,512]{1,0:T(8,128)(2,1)S(1)}, bf16[256,512]{1,0:T(8,128)(2,1)S(1)}, u32[]{:S(2)}, u32[]{:S(2)}) collective-permute-start(bf16[256,512]{1,0:T(8,128)(2,1)S(1)} %shard_map.88), channel_id=1, source_target_pairs={{6,0},{7,1},{4,2},{5,3},{2,4},{3,5},{0,6},{1,7},{14,8},{15,9},{12,... | collective-permute-start | bytes 786440 | tf_op jit(solution)/shard_map/ppermute | solution.py:47
  126.0 12.8 %collective-permute-start.24 = (bf16[256,512]{1,0:T(8,128)(2,1)S(1)}, bf16[256,512]{1,0:T(8,128)(2,1)S(1)}, u32[]{:S(2)}, u32[]{:S(2)}) collective-permute-start(bf16[256,512]{1,0:T(8,128)(2,1)S(1)} %shard_map.89), channel_id=1, source_target_pairs={{4,0},{5,1},{6,2},{7,3},{0,4},{1,5},{2,6},{3,7},{12,8},{13,9},{14,... | collective-permute-start | bytes 786440 | tf_op jit(solution)/shard_map/ppermute | solution.py:47
  139.6 24.3 %all-to-all-start.1 = ((bf16[8,32,512]{2,1,0:T(8,128)(2,1)}), bf16[8,32,512]{2,1,0:T(8,128)(2,1)S(1)}, u32[]{:S(2)}, u32[]{:S(2)}) async-start(bf16[8,32,512]{2,1,0:T(8,128)(2,1)} %bitcast.9), calls=%async_computation.1 | async-start | bytes 524288 | tf_op jit(solution)/shard_map/all_to_all | solution.py:71
  147.5 11.5 %collective-permute-start.18 = (bf16[256,512]{1,0:T(8,128)(2,1)S(1)}, bf16[256,512]{1,0:T(8,128)(2,1)S(1)}, u32[]{:S(2)}, u32[]{:S(2)}) collective-permute-start(bf16[256,512]{1,0:T(8,128)(2,1)S(1)} %shard_map.83), channel_id=1, source_target_pairs={{64,0},{128,64},{192,128},{256,192},{320,256},{384,320},{448,384},... | collective-permute-start | bytes 786440 | tf_op jit(solution)/shard_map/ppermute | solution.py:78
  149.4 13.7 %collective-permute-start.25 = (bf16[256,512]{1,0:T(8,128)(2,1)S(1)}, bf16[256,512]{1,0:T(8,128)(2,1)S(1)}, u32[]{:S(2)}, u32[]{:S(2)}) collective-permute-start(bf16[256,512]{1,0:T(8,128)(2,1)S(1)} %get-tuple-element.62), channel_id=1, source_target_pairs={{64,0},{128,64},{192,128},{256,192},{320,256},{384,320},{448,384},... | collective-permute-start | bytes 786440 | tf_op jit(solution)/shard_map/ppermute | solution.py:78
  154.1 9.0 %collective-permute-start.26 = (bf16[128,512]{1,0:T(8,128)(2,1)S(1)}, bf16[128,512]{1,0:T(8,128)(2,1)S(1)}, u32[]{:S(2)}, u32[]{:S(2)}) collective-permute-start(bf16[128,512]{1,0:T(8,128)(2,1)S(1)} %get-tuple-element.63), channel_id=1, source_target_pairs={{64,8},{65,9},{66,10},{67,11},{68,12},{69,13},{70,14},{71,15},{72,... | collective-permute-start | bytes 393224 | tf_op jit(solution)/shard_map/ppermute | solution.py:88
  (7 other events, 122.7 us)

commit v5 on v3

--- a/solution.py
+++ b/solution.py
@@ -352,6 +352,16 @@
     )[0]
 
 
+def sum_kernel(*refs):
+    total = sum(ref[...].astype(jnp.float32) for ref in refs[:-1])
+    refs[-1][...] = total.astype(refs[-1].dtype)
+
+
+def sum_of(*parts):
+    shape = parts[0].shape
+    return call(sum_kernel, small_cost(*shape), ((shape, jnp.bfloat16),), parts)[0]
+
+
 def sent_back(straight, crossed=None):
     crossed = straight if crossed is None else crossed
     crossed = passed_back_to_partner(crossed)
@@ -395,9 +405,7 @@
         )
         if last:
             own = outer(0)
-            blocks = sum(
-                x.astype(jnp.float32) for x in (own, from_near, from_next, from_far)
-            ).astype(jnp.bfloat16)
+            blocks = sum_of(own, from_near, from_next, from_far)
             blocks, addends = lax.optimization_barrier((blocks, addends))
             parts = exchanged(blocks).reshape(-1, units, half)
         else:

time: 169 us -> 169 us (level)
    pallas_call x15 -> x16, Pallas kernels: 14.7 us -> 15.6 us  [call(): pl.pallas_call(kernel, out_shape=tuple((jax.ShapeDtypeStruct(shape, dtype...]
where the time goes in v5:
time: 169 us; the launch traced here: 168 us
  starting transfers between devices  76.2 us (45%)
  waiting for transfers between devices  40.5 us (24%)
  blocking collectives  32.8 us (19%)
  Pallas kernels  15.6 us (9%)
    all_to_all x1, blocking collectives, exchanged(): lax.all_to_all(blocks, 'dp', 0, 0, axis_index_groups=alike_groups(), tile...  32.8 us
    ppermute x8, waiting for transfers between devices, passed_back_to_partner(): return lax.ppermute(block, ('section', 'dp'), route)  24.6 us
    ppermute x9, starting transfers between devices, passed_back(): return lax.ppermute(block, 'section', [(i, i - 1) for i in devices if i])  21.5 us
    ppermute x7, starting transfers between devices, swapped_along_x(): return lax.ppermute(block, 'dp', route)  20.9 us
    ppermute x8, starting transfers between devices, passed_back_to_partner(): return lax.ppermute(block, ('section', 'dp'), route)  20.1 us
    ppermute x7, waiting for transfers between devices, swapped_along_x(): return lax.ppermute(block, 'dp', route)  15.8 us
    pallas_call x16, Pallas kernels, call(): pl.pallas_call(kernel, out_shape=tuple((jax.ShapeDtypeStruct(shape, dtype...  15.6 us
    all_to_all x1, starting transfers between devices, exchanged(): lax.all_to_all(blocks, 'dp', 0, 0, axis_index_groups=alike_groups(), tile...  7.84 us
  transfers between devices with their start and end apart: 27, of which 11 were waited for; matrix products, arithmetic and copies ran while one was open for 0% of the time, Pallas kernels for 8%

profile of v5, /device:TPU:48, one launch (start us, length us, event | category | flops | bytes accessed | tf_op | source)
XLA Modules:
  0.0 167.7 jit_solution(12661234380021832677)
XLA Ops:
  1.5 32.8 %all_to_all.17 = bf16[8,32,1024]{2,1,0:T(8,128)(2,1)S(1)} all-to-all(bf16[8,32,1024]{2,1,0:T(8,128)(2,1)S(1)} %tile.2), channel_id=1, replica_groups={{0,1,16,17,32,33,48,49},{2,3,18,19,34,35,50,51},{4,5,20,21,36,37,52,53}..., dimensions={0} | all-to-all | bytes 1048576 | tf_op jit(solution)/shard_map/all_to_all | solution.py:71
  34.3 4.7 %collective-permute-start.2 = (bf16[256,1024]{1,0:T(8,128)(2,1)S(1)}, bf16[256,1024]{1,0:T(8,128)(2,1)S(1)}, u32[]{:S(2)}, u32[]{:S(2)}) collective-permute-start(bf16[256,1024]{1,0:T(8,128)(2,1)S(1)} %bitcast.15), channel_id=1, source_target_pairs={{6,0},{7,1},{4,2},{5,3},{2,4},{3,5},{0,6},{1,7},{14,8},{15,9},{12,... | collective-permute-start | bytes 1572872 | tf_op jit(solution)/shard_map/ppermute | solution.py:47
  41.1 3.0 %collective-permute-start.14 = (bf16[128,512]{1,0:T(8,128)(2,1)S(1)}, bf16[128,512]{1,0:T(8,128)(2,1)S(1)}, u32[]{:S(2)}, u32[]{:S(2)}) collective-permute-start(bf16[128,512]{1,0:T(8,128)(2,1)S(1)} %fusion), channel_id=1, source_target_pairs={{8,0},{9,1},{10,2},{11,3},{12,4},{13,5},{14,6},{15,7},{0,8},{1,9},... | collective-permute-start | bytes 393224 | tf_op jit(solution)/shard_map/ppermute | solution.py:55
  44.2 2.8 %collective-permute-start = (f32[128,512]{1,0:T(8,128)S(1)}, f32[128,512]{1,0:T(8,128)S(1)}, u32[]{:S(2)}, u32[]{:S(2)}) collective-permute-start(f32[128,512]{1,0:T(8,128)S(1)} %slice_bitcast_fusion), channel_id=1, source_target_pairs={{8,0},{9,1},{10,2},{11,3},{12,4},{13,5},{14,6},{15,7},{0,8},{1,9},... | collective-permute-start | bytes 786440 | tf_op jit(solution)/shard_map/ppermute | solution.py:55
  47.0 2.3 %collective-permute-done.2.refs_5_.refs_6_.refs_8_.refs_9_ = bf16[256,1024]{1,0:T(8,128)(2,1)S(1)} collective-permute-done((bf16[256,1024]{1,0:T(8,128)(2,1)S(1)}, bf16[256,1024]{1,0:T(8,128)(2,1)S(1)}, u32[]{:S(2)}, u32[]{:S(2)}) %collective-permute-start.2) | collective-permute-done | bytes 524320 | tf_op jit(solution)/shard_map/ppermute | solution.py:47
  51.6 2.3 %collective-permute-done.1.refs_4_.refs_5_.refs_7_.refs_8_ = bf16[256,1024]{1,0:T(8,128)(2,1)S(1)} collective-permute-done((bf16[256,1024]{1,0:T(8,128)(2,1)S(1)}, bf16[256,1024]{1,0:T(8,128)(2,1)S(1)}, u32[]{:S(2)}, u32[]{:S(2)}) %collective-permute-start.1) | collective-permute-done | bytes 524320 | tf_op jit(solution)/shard_map/ppermute | solution.py:47
  58.2 5.3 %collective-permute-done.4.refs_7_.refs_8_.refs_10_.refs_11_ = bf16[128,1024]{1,0:T(8,128)(2,1)S(1)} collective-permute-done((bf16[128,1024]{1,0:T(8,128)(2,1)S(1)}, bf16[128,1024]{1,0:T(8,128)(2,1)S(1)}, u32[]{:S(2)}, u32[]{:S(2)}) %collective-permute-start.4) | collective-permute-done | bytes 262176 | tf_op jit(solution)/shard_map/ppermute | solution.py:47
  66.7 3.9 %collective-permute-start.5 = (bf16[256,512]{1,0:T(8,128)(2,1)S(1)}, bf16[256,512]{1,0:T(8,128)(2,1)S(1)}, u32[]{:S(2)}, u32[]{:S(2)}) collective-permute-start(bf16[256,512]{1,0:T(8,128)(2,1)S(1)} %get-tuple-element.34), channel_id=1, source_target_pairs={{64,0},{128,64},{192,128},{256,192},{320,256},{384,320},{448,384},... | collective-permute-start | bytes 786440 | tf_op jit(solution)/shard_map/ppermute | solution.py:78
  71.9 2.4 %collective-permute-start.16 = (bf16[256,512]{1,0:T(8,128)(2,1)S(1)}, bf16[256,512]{1,0:T(8,128)(2,1)S(1)}, u32[]{:S(2)}, u32[]{:S(2)}) collective-permute-start(bf16[256,512]{1,0:T(8,128)(2,1)S(1)} %get-tuple-element.47), channel_id=1, source_target_pairs={{64,8},{65,9},{66,10},{67,11},{68,12},{69,13},{70,14},{71,15},{72,... | collective-permute-start | bytes 786440 | tf_op jit(solution)/shard_map/ppermute | solution.py:88
  74.3 3.3 %collective-permute-start.15 = (bf16[256,512]{1,0:T(8,128)(2,1)S(1)}, bf16[256,512]{1,0:T(8,128)(2,1)S(1)}, u32[]{:S(2)}, u32[]{:S(2)}) collective-permute-start(bf16[256,512]{1,0:T(8,128)(2,1)S(1)} %get-tuple-element.47), channel_id=1, source_target_pairs={{64,0},{128,64},{192,128},{256,192},{320,256},{384,320},{448,384},... | collective-permute-start | bytes 786440 | tf_op jit(solution)/shard_map/ppermute | solution.py:78
  83.6 2.9 %collective-permute-start.17 = (bf16[384,512]{1,0:T(8,128)(2,1)S(1)}, bf16[384,512]{1,0:T(8,128)(2,1)S(1)}, u32[]{:S(2)}, u32[]{:S(2)}) collective-permute-start(bf16[384,512]{1,0:T(8,128)(2,1)S(1)} %get-tuple-element.50), channel_id=1, source_target_pairs={{64,0},{128,64},{192,128},{256,192},{320,256},{384,320},{448,384},... | collective-permute-start | bytes 1179656 | tf_op jit(solution)/shard_map/ppermute | solution.py:78
  86.5 2.6 %collective-permute-start.9 = (bf16[256,512]{1,0:T(8,128)(2,1)S(1)}, bf16[256,512]{1,0:T(8,128)(2,1)S(1)}, u32[]{:S(2)}, u32[]{:S(2)}) collective-permute-start(bf16[256,512]{1,0:T(8,128)(2,1)S(1)} %get-tuple-element.36), channel_id=1, source_target_pairs={{64,8},{65,9},{66,10},{67,11},{68,12},{69,13},{70,14},{71,15},{72,... | collective-permute-start | bytes 786440 | tf_op jit(solution)/shard_map/ppermute | solution.py:88
  89.2 3.0 %collective-permute-start.18 = (bf16[256,512]{1,0:T(8,128)(2,1)S(1)}, bf16[256,512]{1,0:T(8,128)(2,1)S(1)}, u32[]{:S(2)}, u32[]{:S(2)}) collective-permute-start(bf16[256,512]{1,0:T(8,128)(2,1)S(1)} %get-tuple-element.51), channel_id=1, source_target_pairs={{64,8},{65,9},{66,10},{67,11},{68,12},{69,13},{70,14},{71,15},{72,... | collective-permute-start | bytes 786440 | tf_op jit(solution)/shard_map/ppermute | solution.py:88
  92.2 7.6 %collective-permute-done.9.refs_1_ = bf16[256,512]{1,0:T(8,128)(2,1)S(1)} collective-permute-done((bf16[256,512]{1,0:T(8,128)(2,1)S(1)}, bf16[256,512]{1,0:T(8,128)(2,1)S(1)}, u32[]{:S(2)}, u32[]{:S(2)}) %collective-permute-start.9) | collective-permute-done | bytes 262176 | tf_op jit(solution)/shard_map/ppermute | solution.py:88
  106.3 3.2 %collective-permute-start.11 = (bf16[256,512]{1,0:T(8,128)(2,1)S(1)}, bf16[256,512]{1,0:T(8,128)(2,1)S(1)}, u32[]{:S(2)}, u32[]{:S(2)}) collective-permute-start(bf16[256,512]{1,0:T(8,128)(2,1)S(1)} %get-tuple-element.38), channel_id=1, source_target_pairs={{64,8},{65,9},{66,10},{67,11},{68,12},{69,13},{70,14},{71,15},{72,... | collective-permute-start | bytes 786440 | tf_op jit(solution)/shard_map/ppermute | solution.py:88
  111.5 4.0 %collective-permute-done.11.refs_1_ = bf16[256,512]{1,0:T(8,128)(2,1)S(1)} collective-permute-done((bf16[256,512]{1,0:T(8,128)(2,1)S(1)}, bf16[256,512]{1,0:T(8,128)(2,1)S(1)}, u32[]{:S(2)}, u32[]{:S(2)}) %collective-permute-start.11) | collective-permute-done | bytes 262176 | tf_op jit(solution)/shard_map/ppermute | solution.py:88
  116.8 6.1 %collective-permute-done.20.other_ref.refs_3_ = bf16[256,512]{1,0:T(8,128)(2,1)S(1)} collective-permute-done((bf16[256,512]{1,0:T(8,128)(2,1)S(1)}, bf16[256,512]{1,0:T(8,128)(2,1)S(1)}, u32[]{:S(2)}, u32[]{:S(2)}) %collective-permute-start.20) | collective-permute-done | bytes 262176 | tf_op jit(solution)/shard_map/ppermute | solution.py:88
  126.4 4.2 %collective-permute-start.22 = (bf16[256,512]{1,0:T(8,128)(2,1)S(1)}, bf16[256,512]{1,0:T(8,128)(2,1)S(1)}, u32[]{:S(2)}, u32[]{:S(2)}) collective-permute-start(bf16[256,512]{1,0:T(8,128)(2,1)S(1)} %shard_map.87), channel_id=1, source_target_pairs={{6,0},{7,1},{4,2},{5,3},{2,4},{3,5},{0,6},{1,7},{14,8},{15,9},{12,... | collective-permute-start | bytes 786440 | tf_op jit(solution)/shard_map/ppermute | solution.py:47
  130.6 3.7 %collective-permute-start.23 = (bf16[256,512]{1,0:T(8,128)(2,1)S(1)}, bf16[256,512]{1,0:T(8,128)(2,1)S(1)}, u32[]{:S(2)}, u32[]{:S(2)}) collective-permute-start(bf16[256,512]{1,0:T(8,128)(2,1)S(1)} %shard_map.88), channel_id=1, source_target_pairs={{4,0},{5,1},{6,2},{7,3},{0,4},{1,5},{2,6},{3,7},{12,8},{13,9},{14,... | collective-permute-start | bytes 786440 | tf_op jit(solution)/shard_map/ppermute | solution.py:47
  136.7 5.7 %collective-permute-done.22.refs_2_ = bf16[256,512]{1,0:T(8,128)(2,1)S(1)} collective-permute-done((bf16[256,512]{1,0:T(8,128)(2,1)S(1)}, bf16[256,512]{1,0:T(8,128)(2,1)S(1)}, u32[]{:S(2)}, u32[]{:S(2)}) %collective-permute-start.22) | collective-permute-done | bytes 262176 | tf_op jit(solution)/shard_map/ppermute | solution.py:47
  143.2 7.8 %all-to-all-start.1 = ((bf16[8,32,512]{2,1,0:T(8,128)(2,1)}), bf16[8,32,512]{2,1,0:T(8,128)(2,1)S(1)}, u32[]{:S(2)}, u32[]{:S(2)}) async-start(bf16[8,32,512]{2,1,0:T(8,128)(2,1)} %bitcast.9), calls=%async_computation.1 | async-start | bytes 524288 | tf_op jit(solution)/shard_map/all_to_all | solution.py:71
  154.9 2.6 %collective-permute-start.13 = (bf16[128,512]{1,0:T(8,128)(2,1)S(1)}, bf16[128,512]{1,0:T(8,128)(2,1)S(1)}, u32[]{:S(2)}, u32[]{:S(2)}) collective-permute-start(bf16[128,512]{1,0:T(8,128)(2,1)S(1)} %get-tuple-element.40), channel_id=1, source_target_pairs={{64,8},{65,9},{66,10},{67,11},{68,12},{69,13},{70,14},{71,15},{72,... | collective-permute-start | bytes 393224 | tf_op jit(solution)/shard_map/ppermute | solution.py:88
  157.5 2.3 %collective-permute-start.25 = (bf16[128,512]{1,0:T(8,128)(2,1)S(1)}, bf16[128,512]{1,0:T(8,128)(2,1)S(1)}, u32[]{:S(2)}, u32[]{:S(2)}) collective-permute-start(bf16[128,512]{1,0:T(8,128)(2,1)S(1)} %get-tuple-element.63), channel_id=1, source_target_pairs={{64,8},{65,9},{66,10},{67,11},{68,12},{69,13},{70,14},{71,15},{72,... | collective-permute-start | bytes 393224 | tf_op jit(solution)/shard_map/ppermute | solution.py:88
  162.0 4.2 %collective-permute-done.25.crossed_ref = bf16[128,512]{1,0:T(8,128)(2,1)S(1)} collective-permute-done((bf16[128,512]{1,0:T(8,128)(2,1)S(1)}, bf16[128,512]{1,0:T(8,128)(2,1)S(1)}, u32[]{:S(2)}, u32[]{:S(2)}) %collective-permute-start.25) | collective-permute-done | bytes 131104 | tf_op jit(solution)/shard_map/ppermute | solution.py:88
  (62 shorter events, 43.9 us)
Async XLA Ops:
  34.3 15.1 %collective-permute-start.2 = (bf16[256,1024]{1,0:T(8,128)(2,1)S(1)}, bf16[256,1024]{1,0:T(8,128)(2,1)S(1)}, u32[]{:S(2)}, u32[]{:S(2)}) collective-permute-start(bf16[256,1024]{1,0:T(8,128)(2,1)S(1)} %bitcast.15), channel_id=1, source_target_pairs={{6,0},{7,1},{4,2},{5,3},{2,4},{3,5},{0,6},{1,7},{14,8},{15,9},{12,... | collective-permute-start | bytes 1572872 | tf_op jit(solution)/shard_map/ppermute | solution.py:47
  39.0 15.0 %collective-permute-start.1 = (bf16[256,1024]{1,0:T(8,128)(2,1)S(1)}, bf16[256,1024]{1,0:T(8,128)(2,1)S(1)}, u32[]{:S(2)}, u32[]{:S(2)}) collective-permute-start(bf16[256,1024]{1,0:T(8,128)(2,1)S(1)} %bitcast.16), channel_id=1, source_target_pairs={{2,0},{3,1},{0,2},{1,3},{6,4},{7,5},{4,6},{5,7},{10,8},{11,9},{8,1... | collective-permute-start | bytes 1572872 | tf_op jit(solution)/shard_map/ppermute | solution.py:47
  41.1 29.4 %collective-permute-start.14 = (bf16[128,512]{1,0:T(8,128)(2,1)S(1)}, bf16[128,512]{1,0:T(8,128)(2,1)S(1)}, u32[]{:S(2)}, u32[]{:S(2)}) collective-permute-start(bf16[128,512]{1,0:T(8,128)(2,1)S(1)} %fusion), channel_id=1, source_target_pairs={{8,0},{9,1},{10,2},{11,3},{12,4},{13,5},{14,6},{15,7},{0,8},{1,9},... | collective-permute-start | bytes 393224 | tf_op jit(solution)/shard_map/ppermute | solution.py:55
  44.2 13.8 %collective-permute-start = (f32[128,512]{1,0:T(8,128)S(1)}, f32[128,512]{1,0:T(8,128)S(1)}, u32[]{:S(2)}, u32[]{:S(2)}) collective-permute-start(f32[128,512]{1,0:T(8,128)S(1)} %slice_bitcast_fusion), channel_id=1, source_target_pairs={{8,0},{9,1},{10,2},{11,3},{12,4},{13,5},{14,6},{15,7},{0,8},{1,9},... | collective-permute-start | bytes 786440 | tf_op jit(solution)/shard_map/ppermute | solution.py:55
  49.4 8.8 %collective-permute-start.3 = (bf16[128,1024]{1,0:T(8,128)(2,1)S(1)}, bf16[128,1024]{1,0:T(8,128)(2,1)S(1)}, u32[]{:S(2)}, u32[]{:S(2)}) collective-permute-start(bf16[128,1024]{1,0:T(8,128)(2,1)S(1)} %slice.18), channel_id=1, source_target_pairs={{2,0},{3,1},{0,2},{1,3},{6,4},{7,5},{4,6},{5,7},{10,8},{11,9},{8,1... | collective-permute-start | bytes 786440 | tf_op jit(solution)/shard_map/ppermute | solution.py:47
  54.0 9.5 %collective-permute-start.4 = (bf16[128,1024]{1,0:T(8,128)(2,1)S(1)}, bf16[128,1024]{1,0:T(8,128)(2,1)S(1)}, u32[]{:S(2)}, u32[]{:S(2)}) collective-permute-start(bf16[128,1024]{1,0:T(8,128)(2,1)S(1)} %slice.19), channel_id=1, source_target_pairs={{6,0},{7,1},{4,2},{5,3},{2,4},{3,5},{0,6},{1,7},{14,8},{15,9},{12,... | collective-permute-start | bytes 786440 | tf_op jit(solution)/shard_map/ppermute | solution.py:47
  56.1 21.5 %collective-permute-start.7 = (bf16[256,512]{1,0:T(8,128)(2,1)S(1)}, bf16[256,512]{1,0:T(8,128)(2,1)S(1)}, u32[]{:S(2)}, u32[]{:S(2)}) collective-permute-start(bf16[256,512]{1,0:T(8,128)(2,1)S(1)} %pad_maximum_fusion), channel_id=1, source_target_pairs={{64,0},{128,64},{192,128},{256,192},{320,256},{384,320},{448,384},... | collective-permute-start | bytes 786440 | tf_op jit(solution)/shard_map/ppermute | solution.py:78
  64.8 12.8 %collective-permute-start.6 = (bf16[256,512]{1,0:T(8,128)(2,1)S(1)}, bf16[256,512]{1,0:T(8,128)(2,1)S(1)}, u32[]{:S(2)}, u32[]{:S(2)}) collective-permute-start(bf16[256,512]{1,0:T(8,128)(2,1)S(1)} %get-tuple-element.34), channel_id=1, source_target_pairs={{64,8},{65,9},{66,10},{67,11},{68,12},{69,13},{70,14},{71,15},{72,... | collective-permute-start | bytes 786440 | tf_op jit(solution)/shard_map/ppermute | solution.py:88
  66.7 10.9 %collective-permute-start.5 = (bf16[256,512]{1,0:T(8,128)(2,1)S(1)}, bf16[256,512]{1,0:T(8,128)(2,1)S(1)}, u32[]{:S(2)}, u32[]{:S(2)}) collective-permute-start(bf16[256,512]{1,0:T(8,128)(2,1)S(1)} %get-tuple-element.34), channel_id=1, source_target_pairs={{64,0},{128,64},{192,128},{256,192},{320,256},{384,320},{448,384},... | collective-permute-start | bytes 786440 | tf_op jit(solution)/shard_map/ppermute | solution.py:78
  71.9 10.5 %collective-permute-start.16 = (bf16[256,512]{1,0:T(8,128)(2,1)S(1)}, bf16[256,512]{1,0:T(8,128)(2,1)S(1)}, u32[]{:S(2)}, u32[]{:S(2)}) collective-permute-start(bf16[256,512]{1,0:T(8,128)(2,1)S(1)} %get-tuple-element.47), channel_id=1, source_target_pairs={{64,8},{65,9},{66,10},{67,11},{68,12},{69,13},{70,14},{71,15},{72,... | collective-permute-start | bytes 786440 | tf_op jit(solution)/shard_map/ppermute | solution.py:88
  79.0 20.9 %collective-permute-start.8 = (bf16[384,512]{1,0:T(8,128)(2,1)S(1)}, bf16[384,512]{1,0:T(8,128)(2,1)S(1)}, u32[]{:S(2)}, u32[]{:S(2)}) collective-permute-start(bf16[384,512]{1,0:T(8,128)(2,1)S(1)} %get-tuple-element.35), channel_id=1, source_target_pairs={{64,0},{128,64},{192,128},{256,192},{320,256},{384,320},{448,384},... | collective-permute-start | bytes 1179656 | tf_op jit(solution)/shard_map/ppermute | solution.py:78
  83.6 19.5 %collective-permute-start.17 = (bf16[384,512]{1,0:T(8,128)(2,1)S(1)}, bf16[384,512]{1,0:T(8,128)(2,1)S(1)}, u32[]{:S(2)}, u32[]{:S(2)}) collective-permute-start(bf16[384,512]{1,0:T(8,128)(2,1)S(1)} %get-tuple-element.50), channel_id=1, source_target_pairs={{64,0},{128,64},{192,128},{256,192},{320,256},{384,320},{448,384},... | collective-permute-start | bytes 1179656 | tf_op jit(solution)/shard_map/ppermute | solution.py:78
  86.5 13.3 %collective-permute-start.9 = (bf16[256,512]{1,0:T(8,128)(2,1)S(1)}, bf16[256,512]{1,0:T(8,128)(2,1)S(1)}, u32[]{:S(2)}, u32[]{:S(2)}) collective-permute-start(bf16[256,512]{1,0:T(8,128)(2,1)S(1)} %get-tuple-element.36), channel_id=1, source_target_pairs={{64,8},{65,9},{66,10},{67,11},{68,12},{69,13},{70,14},{71,15},{72,... | collective-permute-start | bytes 786440 | tf_op jit(solution)/shard_map/ppermute | solution.py:88
  89.2 14.0 %collective-permute-start.18 = (bf16[256,512]{1,0:T(8,128)(2,1)S(1)}, bf16[256,512]{1,0:T(8,128)(2,1)S(1)}, u32[]{:S(2)}, u32[]{:S(2)}) collective-permute-start(bf16[256,512]{1,0:T(8,128)(2,1)S(1)} %get-tuple-element.51), channel_id=1, source_target_pairs={{64,8},{65,9},{66,10},{67,11},{68,12},{69,13},{70,14},{71,15},{72,... | collective-permute-start | bytes 786440 | tf_op jit(solution)/shard_map/ppermute | solution.py:88
  101.2 14.3 %collective-permute-start.10 = (bf16[384,512]{1,0:T(8,128)(2,1)S(1)}, bf16[384,512]{1,0:T(8,128)(2,1)S(1)}, u32[]{:S(2)}, u32[]{:S(2)}) collective-permute-start(bf16[384,512]{1,0:T(8,128)(2,1)S(1)} %get-tuple-element.37), channel_id=1, source_target_pairs={{64,0},{128,64},{192,128},{256,192},{320,256},{384,320},{448,384},... | collective-permute-start | bytes 1179656 | tf_op jit(solution)/shard_map/ppermute | solution.py:78
  104.4 18.5 %collective-permute-start.19 = (bf16[384,512]{1,0:T(8,128)(2,1)S(1)}, bf16[384,512]{1,0:T(8,128)(2,1)S(1)}, u32[]{:S(2)}, u32[]{:S(2)}) collective-permute-start(bf16[384,512]{1,0:T(8,128)(2,1)S(1)} %get-tuple-element.54), channel_id=1, source_target_pairs={{64,0},{128,64},{192,128},{256,192},{320,256},{384,320},{448,384},... | collective-permute-start | bytes 1179656 | tf_op jit(solution)/shard_map/ppermute | solution.py:78
  106.3 9.1 %collective-permute-start.11 = (bf16[256,512]{1,0:T(8,128)(2,1)S(1)}, bf16[256,512]{1,0:T(8,128)(2,1)S(1)}, u32[]{:S(2)}, u32[]{:S(2)}) collective-permute-start(bf16[256,512]{1,0:T(8,128)(2,1)S(1)} %get-tuple-element.38), channel_id=1, source_target_pairs={{64,8},{65,9},{66,10},{67,11},{68,12},{69,13},{70,14},{71,15},{72,... | collective-permute-start | bytes 786440 | tf_op jit(solution)/shard_map/ppermute | solution.py:88
  109.6 13.3 %collective-permute-start.20 = (bf16[256,512]{1,0:T(8,128)(2,1)S(1)}, bf16[256,512]{1,0:T(8,128)(2,1)S(1)}, u32[]{:S(2)}, u32[]{:S(2)}) collective-permute-start(bf16[256,512]{1,0:T(8,128)(2,1)S(1)} %get-tuple-element.55), channel_id=1, source_target_pairs={{64,8},{65,9},{66,10},{67,11},{68,12},{69,13},{70,14},{71,15},{72,... | collective-permute-start | bytes 786440 | tf_op jit(solution)/shard_map/ppermute | solution.py:88
  124.4 12.2 %collective-permute-start.21 = (bf16[256,512]{1,0:T(8,128)(2,1)S(1)}, bf16[256,512]{1,0:T(8,128)(2,1)S(1)}, u32[]{:S(2)}, u32[]{:S(2)}) collective-permute-start(bf16[256,512]{1,0:T(8,128)(2,1)S(1)} %shard_map.86), channel_id=1, source_target_pairs={{2,0},{3,1},{0,2},{1,3},{6,4},{7,5},{4,6},{5,7},{10,8},{11,9},{8,1... | collective-permute-start | bytes 786440 | tf_op jit(solution)/shard_map/ppermute | solution.py:47
  126.4 16.0 %collective-permute-start.22 = (bf16[256,512]{1,0:T(8,128)(2,1)S(1)}, bf16[256,512]{1,0:T(8,128)(2,1)S(1)}, u32[]{:S(2)}, u32[]{:S(2)}) collective-permute-start(bf16[256,512]{1,0:T(8,128)(2,1)S(1)} %shard_map.87), channel_id=1, source_target_pairs={{6,0},{7,1},{4,2},{5,3},{2,4},{3,5},{0,6},{1,7},{14,8},{15,9},{12,... | collective-permute-start | bytes 786440 | tf_op jit(solution)/shard_map/ppermute | solution.py:47
  130.6 11.8 %collective-permute-start.23 = (bf16[256,512]{1,0:T(8,128)(2,1)S(1)}, bf16[256,512]{1,0:T(8,128)(2,1)S(1)}, u32[]{:S(2)}, u32[]{:S(2)}) collective-permute-start(bf16[256,512]{1,0:T(8,128)(2,1)S(1)} %shard_map.88), channel_id=1, source_target_pairs={{4,0},{5,1},{6,2},{7,3},{0,4},{1,5},{2,6},{3,7},{12,8},{13,9},{14,... | collective-permute-start | bytes 786440 | tf_op jit(solution)/shard_map/ppermute | solution.py:47
  143.2 23.8 %all-to-all-start.1 = ((bf16[8,32,512]{2,1,0:T(8,128)(2,1)}), bf16[8,32,512]{2,1,0:T(8,128)(2,1)S(1)}, u32[]{:S(2)}, u32[]{:S(2)}) async-start(bf16[8,32,512]{2,1,0:T(8,128)(2,1)} %bitcast.9), calls=%async_computation.1 | async-start | bytes 524288 | tf_op jit(solution)/shard_map/all_to_all | solution.py:71
  151.1 10.1 %collective-permute-start.12 = (bf16[256,512]{1,0:T(8,128)(2,1)S(1)}, bf16[256,512]{1,0:T(8,128)(2,1)S(1)}, u32[]{:S(2)}, u32[]{:S(2)}) collective-permute-start(bf16[256,512]{1,0:T(8,128)(2,1)S(1)} %get-tuple-element.39), channel_id=1, source_target_pairs={{64,0},{128,64},{192,128},{256,192},{320,256},{384,320},{448,384},... | collective-permute-start | bytes 786440 | tf_op jit(solution)/shard_map/ppermute | solution.py:78
  153.0 13.2 %collective-permute-start.24 = (bf16[256,512]{1,0:T(8,128)(2,1)S(1)}, bf16[256,512]{1,0:T(8,128)(2,1)S(1)}, u32[]{:S(2)}, u32[]{:S(2)}) collective-permute-start(bf16[256,512]{1,0:T(8,128)(2,1)S(1)} %get-tuple-element.62), channel_id=1, source_target_pairs={{64,0},{128,64},{192,128},{256,192},{320,256},{384,320},{448,384},... | collective-permute-start | bytes 786440 | tf_op jit(solution)/shard_map/ppermute | solution.py:78
  (6 other events, 112.8 us)
